TPU v7x, 256 devices: a whole 4x4x8 slice. The times are simulated.
256 devices in a mesh: ctx: 128 (over y, x_lo, z, core), head: 2 (over x_hi).
Axes of the slice: x: 4 (x_hi: 2, x_lo: 2; x = x_hi * 2 + x_lo), y: 4, z: 8, core: 2. Of those that a mesh axis runs over, the one named last changes fastest.
Arguments:
- queries: bfloat16 [8192, 2048], P('ctx', 'head'), may hold values from -6 to 6
- keys_first: bfloat16 [8192, 512], P('ctx', 'head'), may hold values from -6 to 6
- primary_value_array: bfloat16 [8192, 512], P('ctx', 'head'), may hold values from -6 to 6
- keys_second: bfloat16 [8192, 512], P('ctx', 'head'), may hold values from -6 to 6
- secondary_value_array: bfloat16 [8192, 512], P('ctx', 'head'), may hold values from -6 to 6
- out_weight: bfloat16 [2048, 4096], P('head'), may hold values from -6 to 6
Outputs:
- projected: bfloat16 [8192, 4096], P('ctx', 'head')
All inputs are finite; a program needn't handle non-finite values.
Results may differ from a plain program's by a relative error of at most 0.01.
Values may be sent and summed in bfloat16 or wider, within the bound.
No kernel may reach another device: no remote copies, remote signals or barrier semaphores. Data moves between devices by JAX's collectives and lax.ppermute only.
A program may use at most 128 MiB of HBM per device.

v0:
```python
import math

import jax
import jax.numpy as jnp
from jax import lax
from jax.sharding import PartitionSpec as P

HEAD_SIZE = 128
FIRST_WINDOW = 512
SECOND_WINDOW = 16


NEGATIVE = -1e30


def shifted(value, axis, steps):
    count = lax.axis_size(axis)
    initial, last = (max(0, -steps), min(count, count - steps))
    return lax.ppermute(value, axis, [(source, source + steps) for source in range(initial, last)])


def split_up(array, dim, count):
    before, after = (array.shape[:dim], array.shape[dim + 1 :])
    return jnp.moveaxis(array.reshape(*before, count, -1, *after), dim, 0)


def summed_on_arrival(array, axis, dim):
    parts = split_up(array, dim, lax.axis_size(axis))
    arrived = lax.all_to_all(parts, axis, split_axis=0, concat_axis=0, tiled=True)
    return arrived.astype(jnp.float32).sum(axis=0)


def body(queries, keys_first, primary_value_array, keys_second, secondary_value_array, out_weight):
    shard_rows = queries.shape[0]
    kv_heads = keys_first.shape[1] // HEAD_SIZE
    q_heads = queries.shape[1] // HEAD_SIZE
    group_count = q_heads // kv_heads
    score_scale = 1.0 / math.sqrt(HEAD_SIZE)
    shard_start = lax.axis_index("ctx") * shard_rows
    block_reach = FIRST_WINDOW // shard_rows
    tail_keys = keys_second[shard_rows - SECOND_WINDOW :]
    tail_values = secondary_value_array[shard_rows - SECOND_WINDOW :]
    near_keys, near_values, edge_keys, edge_values = shifted(
        (keys_first, primary_value_array, tail_keys, tail_values), "ctx", 1
    )
    joined_keys = jnp.concatenate([edge_keys, keys_second], axis=0)
    joined_values = jnp.concatenate([edge_values, secondary_value_array], axis=0)
    window_keys = jnp.stack(
        [joined_keys[offset + 1 : offset + 1 + shard_rows] for offset in range(SECOND_WINDOW)],
        axis=1,
    )
    window_values = jnp.stack(
        [joined_values[offset + 1 : offset + 1 + shard_rows] for offset in range(SECOND_WINDOW)],
        axis=1,
    )
    secondary_heads = window_keys.reshape(shard_rows, SECOND_WINDOW, kv_heads, HEAD_SIZE).transpose(
        2, 0, 1, 3
    )[:, None]
    secondary_values = (
        window_values.reshape(shard_rows, SECOND_WINDOW, kv_heads, HEAD_SIZE)
        .transpose(2, 0, 1, 3)[:, None]
        .astype(jnp.float32)
    )
    head_queries = queries.reshape(shard_rows, kv_heads, group_count, HEAD_SIZE).transpose(
        1, 2, 0, 3
    )[:, :, :, None, :]
    products = (
        head_queries.astype(jnp.float32) * secondary_heads.astype(jnp.float32) * score_scale
    ).astype(jnp.bfloat16)
    products = products.reshape(kv_heads, group_count, shard_rows * SECOND_WINDOW, HEAD_SIZE)
    query_pos = shard_start + jnp.arange(shard_rows, dtype=jnp.int32)
    second_ok = (
        query_pos[:, None] - SECOND_WINDOW + 1 + jnp.arange(SECOND_WINDOW, dtype=jnp.int32)[None, :]
        >= 0
    )

    def absorb(running, block_keys, block_values, block_start):
        row_top, row_total, accumulated = running
        block_width = block_keys.shape[0]
        head_keys = block_keys.reshape(block_width, kv_heads, HEAD_SIZE)
        scores = jnp.einsum(
            "gmxd,jgd->gmjx", products, head_keys, preferred_element_type=jnp.float32
        )
        scores = scores.reshape(kv_heads, group_count, block_width, shard_rows, SECOND_WINDOW)
        key_pos = block_start + jnp.arange(block_width, dtype=jnp.int32)
        allowed_pairs = (
            (key_pos[:, None] <= query_pos[None, :])
            & (key_pos[:, None] > query_pos[None, :] - FIRST_WINDOW)
            & (key_pos[:, None] >= 0)
        )
        allowed_pairs = allowed_pairs[:, :, None] & second_ok[None]
        masked = jnp.where(allowed_pairs, scores, NEGATIVE)
        new_top = jnp.maximum(row_top, jnp.max(masked, axis=(2, 4)))
        expo = jnp.where(allowed_pairs, jnp.exp(scores - new_top[:, :, None, :, None]), 0.0)
        rescale = jnp.exp(row_top - new_top)
        row_total = row_total * rescale + jnp.sum(expo, axis=(2, 4))
        weights = expo.astype(jnp.bfloat16).reshape(
            kv_heads, group_count, block_width, shard_rows * SECOND_WINDOW
        )
        mixture = jnp.einsum(
            "gmjx,jgd->gmxd",
            weights,
            block_values.reshape(block_width, kv_heads, HEAD_SIZE),
            preferred_element_type=jnp.float32,
        )
        mixture = mixture.reshape(kv_heads, group_count, shard_rows, SECOND_WINDOW, HEAD_SIZE)
        accumulated = accumulated * rescale[..., None] + jnp.sum(mixture * secondary_values, axis=3)
        return (new_top, row_total, accumulated)

    running = (
        jnp.full((kv_heads, group_count, shard_rows), NEGATIVE, jnp.float32),
        jnp.zeros((kv_heads, group_count, shard_rows), jnp.float32),
        jnp.zeros((kv_heads, group_count, shard_rows, HEAD_SIZE), jnp.float32),
    )
    running = absorb(running, keys_first, primary_value_array, shard_start)
    running = absorb(running, near_keys, near_values, shard_start - shard_rows)
    held_keys, held_values = (near_keys, near_values)
    doubled_span = 1
    while doubled_span < block_reach:
        if doubled_span == 1:
            sending_keys, sending_values, step_by = (keys_first, primary_value_array, 2)
        else:
            sending_keys, sending_values, step_by = (held_keys, held_values, doubled_span)
        arrived_keys, arrived_values = shifted((sending_keys, sending_values), "ctx", step_by)
        running = absorb(
            running, arrived_keys, arrived_values, shard_start - 2 * doubled_span * shard_rows
        )
        held_keys = jnp.concatenate([arrived_keys, held_keys], axis=0)
        held_values = jnp.concatenate([arrived_values, held_values], axis=0)
        doubled_span = doubled_span * 2
    row_top, row_total, accumulated = running
    attention = (
        (accumulated / row_total[..., None])
        .transpose(2, 0, 1, 3)
        .reshape(shard_rows, q_heads * HEAD_SIZE)
    )
    attention = attention.astype(jnp.bfloat16)
    partial_value = jnp.dot(attention, out_weight, preferred_element_type=jnp.float32)
    return summed_on_arrival(partial_value.astype(jnp.bfloat16), "head", 1).astype(jnp.bfloat16)


def solution(mesh):
    in_specs = (
        P("ctx", "head"),
        P("ctx", "head"),
        P("ctx", "head"),
        P("ctx", "head"),
        P("ctx", "head"),
        P("head", None),
    )
    out_specs = P("ctx", "head")
    return jax.shard_map(body, mesh=mesh, in_specs=in_specs, out_specs=out_specs, check_vma=False)
```

profile of v0, /device:TPU:24, one launch (start us, length us, event | category | flops | bytes accessed | tf_op | source)
XLA Modules:
  0.0 162.8 jit_solution(16950134609985023952)
XLA Ops:
  0.0 1.5 copy.122
  1.5 1.9 %collective-permute-start.2 = (bf16[64,256]{0,1:T(8,128)(2,1)}, bf16[64,256]{0,1:T(8,128)(2,1)}, u32[]{:S(2)}, u32[]{:S(2)}) collective-permute-start(bf16[64,256]{0,1:T(8,128)(2,1)} %copy.122), channel_id=1, source_target_pairs={{0,2},{2,4},{4,6},{6,8},{8,10},{10,12},{12,14},{14,16},{16,18},{18... | collective-permute-start | bytes 98312 | tf_op jit(solution)/shard_map/ppermute | solution.py:19
  3.4 3.8 %collective-permute-start.4 = (bf16[64,256]{0,1:T(8,128)(2,1)}, bf16[64,256]{0,1:T(8,128)(2,1)}, u32[]{:S(2)}, u32[]{:S(2)}) collective-permute-start(bf16[64,256]{0,1:T(8,128)(2,1)} %copy.122), channel_id=1, source_target_pairs={{0,4},{2,6},{4,8},{6,10},{8,12},{10,14},{12,16},{14,18},{16,20},{1... | collective-permute-start | bytes 98312 | tf_op jit(solution)/shard_map/ppermute | solution.py:19
  7.2 1.5 copy.125
  8.7 3.6 %collective-permute-start.3 = (bf16[64,256]{0,1:T(8,128)(2,1)}, bf16[64,256]{0,1:T(8,128)(2,1)}, u32[]{:S(2)}, u32[]{:S(2)}) collective-permute-start(bf16[64,256]{0,1:T(8,128)(2,1)} %copy.125), channel_id=1, source_target_pairs={{0,2},{2,4},{4,6},{6,8},{8,10},{10,12},{12,14},{14,16},{16,18},{18... | collective-permute-start | bytes 98312 | tf_op jit(solution)/shard_map/ppermute | solution.py:19
  12.4 3.8 %collective-permute-start.5 = (bf16[64,256]{0,1:T(8,128)(2,1)}, bf16[64,256]{0,1:T(8,128)(2,1)}, u32[]{:S(2)}, u32[]{:S(2)}) collective-permute-start(bf16[64,256]{0,1:T(8,128)(2,1)} %copy.125), channel_id=1, source_target_pairs={{0,4},{2,6},{4,8},{6,10},{8,12},{10,14},{12,16},{14,18},{16,20},{1... | collective-permute-start | bytes 98312 | tf_op jit(solution)/shard_map/ppermute | solution.py:19
  16.9 1.9 %collective-permute-start = (bf16[16,256]{1,0:T(8,128)(2,1)S(1)}, bf16[16,256]{1,0:T(8,128)(2,1)S(1)}, u32[]{:S(2)}, u32[]{:S(2)}) collective-permute-start(bf16[16,256]{1,0:T(8,128)(2,1)S(1)} %slice.96), channel_id=1, source_target_pairs={{0,2},{2,4},{4,6},{6,8},{8,10},{10,12},{12,14},{14,16},{16,18},{18... | collective-permute-start | bytes 24584 | tf_op jit(solution)/shard_map/ppermute | solution.py:19
  20.1 1.4 reshape.723
  21.5 1.4 reshape.724
  23.5 1.4 stack.134
  26.1 1.0 reshape.740
  30.6 5.1 %collective-permute-start.1 = (bf16[16,256]{1,0:T(8,128)(2,1)S(1)}, bf16[16,256]{1,0:T(8,128)(2,1)S(1)}, u32[]{:S(2)}, u32[]{:S(2)}) collective-permute-start(bf16[16,256]{1,0:T(8,128)(2,1)S(1)} %slice.112), channel_id=1, source_target_pairs={{0,2},{2,4},{4,6},{6,8},{8,10},{10,12},{12,14},{14,16},{16,18},{18... | collective-permute-start | bytes 24584 | tf_op jit(solution)/shard_map/ppermute | solution.py:19
  48.0 1.5 fusion.2
  49.4 1.4 constant_dynamic-update-slice_fusion.34
  50.8 1.4 constant_dynamic-update-slice_fusion.33
  52.2 1.4 constant_dynamic-update-slice_fusion.32
  53.6 1.4 constant_dynamic-update-slice_fusion.31
  55.0 1.4 constant_dynamic-update-slice_fusion.30
  56.4 1.4 constant_dynamic-update-slice_fusion.29
  57.8 1.4 constant_dynamic-update-slice_fusion.28
  59.1 1.4 constant_dynamic-update-slice_fusion.27
  60.5 1.4 constant_dynamic-update-slice_fusion.26
  61.9 1.4 constant_dynamic-update-slice_fusion.25
  63.3 1.4 constant_dynamic-update-slice_fusion.24
  67.2 2.8 %fusion.13 = (f32[2,4,1024]{2,1,0:T(4,128)}, f32[2,4,1024,64]{2,3,1,0:T(8,128)}) fusion(pred[64,1024]{1,0:T(8,128)(4,1)S(1)} %copy-done.8, bf16[2,4,1024,128]{3,2,1,0:T(8,128)(2,1)S(1)} %fusion.2, bf16[64,2,128,1]{2,1,0,3:T(2,128)(2,1)S(1)} %bitcast.293), kind=kOutput, calls=%fused_computation.34 | convolution fusion | flops 135258112 | bytes 4325376 | tf_op jit(solution)/shard_map/gmxd,jgd->gmjx/dot_general | solution.py:81
  70.5 1.6 reduce_max.64
  72.0 1.6 copy.120
  73.6 1.1 reduce_max.65
  74.8 3.1 %fusion.10 = (f32[2,4,1024]{2,1,0:T(4,128)S(1)}, f32[2,4,1024,64]{2,3,1,0:T(8,128)}) fusion(pred[64,1024]{1,0:T(8,128)(4,1)} %copy.121, bf16[2,4,1024,128]{3,2,1,0:T(8,128)(2,1)S(1)} %fusion.2, bf16[64,2,128,1]{0,2,3,1:T(8,128)(2,1)} %bitcast.70), kind=kOutput, calls=%fused_computation.29 | convolution fusion | flops 135258112 | bytes 4325376 | tf_op jit(solution)/shard_map/gmxd,jgd->gmjx/dot_general | solution.py:81
  77.9 3.1 %fusion.7 = (f32[2,4,1024]{2,1,0:T(4,128)S(1)}, f32[2,4,1024,64]{2,3,1,0:T(8,128)}) fusion(pred[64,1024]{1,0:T(8,128)(4,1)S(1)} %copy-done.6, bf16[2,4,1024,128]{3,2,1,0:T(8,128)(2,1)S(1)} %fusion.2, bf16[64,2,128,1]{0,2,3,1:T(8,128)(2,1)} %bitcast.72), kind=kOutput, calls=%fused_computation.24 | convolution fusion | flops 135258112 | bytes 4325376 | tf_op jit(solution)/shard_map/gmxd,jgd->gmjx/dot_general | solution.py:81
  82.5 2.2 %collective-permute-start.6 = (bf16[128,256]{0,1:T(8,128)(2,1)S(1)}, bf16[128,256]{0,1:T(8,128)(2,1)S(1)}, u32[]{:S(2)}, u32[]{:S(2)}) collective-permute-start(bf16[128,256]{0,1:T(8,128)(2,1)S(1)} %pad_maximum_fusion.2), channel_id=1, source_target_pairs={{0,4},{2,6},{4,8},{6,10},{8,12},{10,14},{12,16},{14,18},{16,20},{1... | collective-permute-start | bytes 196616 | tf_op jit(solution)/shard_map/ppermute | solution.py:19
  85.7 2.9 %collective-permute-start.7 = (bf16[128,256]{0,1:T(8,128)(2,1)S(1)}, bf16[128,256]{0,1:T(8,128)(2,1)S(1)}, u32[]{:S(2)}, u32[]{:S(2)}) collective-permute-start(bf16[128,256]{0,1:T(8,128)(2,1)S(1)} %pad_maximum_fusion.3), channel_id=1, source_target_pairs={{0,4},{2,6},{4,8},{6,10},{8,12},{10,14},{12,16},{14,18},{16,20},{1... | collective-permute-start | bytes 196616 | tf_op jit(solution)/shard_map/ppermute | solution.py:19
  88.7 3.0 %collective-permute-done.6 = bf16[128,256]{0,1:T(8,128)(2,1)S(1)} collective-permute-done((bf16[128,256]{0,1:T(8,128)(2,1)S(1)}, bf16[128,256]{0,1:T(8,128)(2,1)S(1)}, u32[]{:S(2)}, u32[]{:S(2)}) %collective-permute-start.6) | collective-permute-done | bytes 65568 | tf_op jit(solution)/shard_map/ppermute | solution.py:19
  92.7 1.9 %collective-permute-start.8 = (bf16[256,256]{0,1:T(8,128)(2,1)S(1)}, bf16[256,256]{0,1:T(8,128)(2,1)S(1)}, u32[]{:S(2)}, u32[]{:S(2)}) collective-permute-start(bf16[256,256]{0,1:T(8,128)(2,1)S(1)} %pad_maximum_fusion), channel_id=1, source_target_pairs={{0,8},{2,10},{4,12},{6,14},{8,16},{10,18},{12,20},{14,22},{16,24},... | collective-permute-start | bytes 393224 | tf_op jit(solution)/shard_map/ppermute | solution.py:19
  94.6 2.8 %select_reduce_fusion.1 = (f32[2,4,1024]{2,1,0:T(4,128)S(1)}, f32[2,128,4,1024]{3,1,2,0:T(8,128)}) fusion(pred[128,1024]{1,0:T(8,128)(4,1)S(1)} %copy.135, bf16[128,2,128,1]{0,2,3,1:T(8,128)(2,1)S(1)} %bitcast.289, bf16[2,4,1024,128]{3,2,1,0:T(8,128)(2,1)S(1)} %fusion.2), kind=kOutput, calls=%fused_computation.16 | convolution fusion | flops 270524416 | bytes 6520832 | tf_op jit(solution)/shard_map/gmxd,jgd->gmjx/dot_general | solution.py:81
  97.7 1.6 pad_maximum_fusion.1
  99.3 4.0 %collective-permute-start.9 = (bf16[256,256]{0,1:T(8,128)(2,1)}, bf16[256,256]{0,1:T(8,128)(2,1)S(1)}, u32[]{:S(2)}, u32[]{:S(2)}) collective-permute-start(bf16[256,256]{0,1:T(8,128)(2,1)} %pad_maximum_fusion.1), channel_id=1, source_target_pairs={{0,8},{2,10},{4,12},{6,14},{8,16},{10,18},{12,20},{14,22},{16,24},... | collective-permute-start | bytes 393224 | tf_op jit(solution)/shard_map/ppermute | solution.py:19
  103.6 4.7 %select_reduce_fusion = (f32[2,4,1024]{2,1,0:T(4,128)S(1)}, f32[2,256,4,1024]{3,1,2,0:T(8,128)}) fusion(pred[256,1024]{1,0:T(8,128)(4,1)S(1)} %copy.139, bf16[256,2,128,1]{0,2,3,1:T(8,128)(2,1)S(1)} %bitcast.291, bf16[2,4,1024,128]{3,2,1,0:T(8,128)(2,1)S(1)} %fusion.2), kind=kOutput, calls=%fused_computation.3 | convolution fusion | flops 541057024 | bytes 10911744 | tf_op jit(solution)/shard_map/gmxd,jgd->gmjx/dot_general | solution.py:81
  108.9 2.1 %fusion.19 = f32[2,4,1024]{2,1,0:T(4,128)S(1)} fusion(f32[2,4,1024,64]{2,3,1,0:T(8,128)} %get-tuple-element.66, f32[2,4,1024]{2,1,0:T(4,128)S(1)} %sub.156, pred[64,1024]{1,0:T(8,128)(4,1)S(1)} %copy-done.9), kind=kLoop, calls=%fused_computation.40 | loop fusion | flops 1564672 | bytes 2228224 | tf_op jit(solution)/shard_map/reduce_sum | solution.py:96
  113.2 3.0 %bitcast_reduce_fusion.1 = f32[2,4,1024]{2,1,0:T(4,128)S(1)} fusion(f32[2,128,4,1024]{3,1,2,0:T(8,128)} %get-tuple-element.60, f32[2,4,1024]{2,1,0:T(4,128)S(1)} %sub.174, pred[128,1024]{1,0:T(8,128)(4,1)S(1)} %copy.135), kind=kLoop, calls=%fused_computation.6 | loop fusion | flops 3137536 | bytes 4390912 | tf_op jit(solution)/shard_map/reduce_sum | solution.py:96
  116.2 5.0 %bitcast_reduce_fusion = f32[2,4,1024]{2,1,0:T(4,128)S(1)} fusion(f32[2,256,4,1024]{3,1,2,0:T(8,128)} %get-tuple-element.58, f32[2,4,1024]{2,1,0:T(4,128)S(1)} %sub.180, pred[256,1024]{1,0:T(8,128)(4,1)S(1)} %copy.139), kind=kLoop, calls=%fused_computation | loop fusion | flops 6283264 | bytes 8716288 | tf_op jit(solution)/shard_map/reduce_sum | solution.py:96
  122.5 5.7 %fusion = f32[2,4,1024,128]{3,2,1,0:T(8,128)S(1)} fusion(bf16[256,2,128,1]{0,2,3,1:T(8,128)(2,1)S(1)} %bitcast.290, f32[2,256,4,1024]{3,1,2,0:T(8,128)} %get-tuple-element.58, f32[2,4,1024]{2,1,0:T(4,128)S(1)} %sub.180, pred[256,1024]{1,0:T(8,128)(4,1)S(1)} %copy.139), kind=kOutput, calls=%fused_computation.5 | convolution fusion | flops 543162368 | bytes 13008896 | tf_op jit(solution)/shard_map/gmjx,jgd->gmxd/dot_general | solution.py:100
  128.2 1.1 fusion.6
  129.4 3.9 %fusion.25 = f32[2,4,1024,128]{3,2,1,0:T(8,128)} fusion(bf16[64,2,128,1]{0,2,3,1:T(8,128)(2,1)} %bitcast.73, f32[2,4,1024,64]{2,3,1,0:T(8,128)S(1)} %copy-done.2, f32[2,4,1024]{2,1,0:T(4,128)S(1)} %sub.168, pred[64,1024]{1,0:T(8,128)(4,1)S(1)} %copy-done.6), kind=kOutput, calls=%fused_computation.46 | convolution fusion | flops 135790592 | bytes 6422528 | tf_op jit(solution)/shard_map/gmjx,jgd->gmxd/dot_general | solution.py:100
  133.3 3.1 %fusion.29 = f32[2,4,1024,128]{3,2,1,0:T(8,128)} fusion(f32[2,4,1024,64]{2,3,1,0:T(8,128)S(1)} %copy-done.1, f32[2,4,1024]{2,1,0:T(4,128)S(1)} %sub.156, pred[64,1024]{1,0:T(8,128)(4,1)S(1)} %copy-done.9, bf16[64,2,128,1]{2,1,0,3:T(2,128)(2,1)S(1)} %bitcast.292), kind=kOutput, calls=%fused_computation.48 | convolution fusion | flops 135790592 | bytes 6422528 | tf_op jit(solution)/shard_map/gmjx,jgd->gmxd/dot_general | solution.py:100
  136.5 7.2 %multiply_reduce_fusion.4 = (f32[2,4,64,128]{3,2,1,0:T(8,128)S(1)}, f32[2,4,64,128]{3,2,1,0:T(8,128)S(1)}, f32[2,4,64,128]{3,2,1,0:T(8,128)S(1)}, f32[2,4,64,128]{3,2,1,0:T(8,128)S(1)}, f32[2,4,64,128]{3,2,1,0:T(8,128)S(1)}) fusion(f32[2,64,16,128]{3,2,1,0:T(8,128)S(1)} %copy-done.5, f32[2,4,1024,128]{3,2,1,0:T(8,128)} %fusion.29, ...), kind=kOutput, calls=%fused_computation.19 | convolution fusion | flops 145948672 | bytes 21364736 | tf_op jit(solution)/shard_map/gmjx,jgd->gmxd/dot_general | solution.py:100
  144.4 5.0 %convolution_convert_fusion = bf16[64,4096]{1,0:T(8,128)(2,1)S(1)} fusion(bf16[64,1024]{1,0:T(8,128)(2,1)S(1)} %convert_element_type.70, bf16[1024,4096]{1,0:T(8,128)(2,1)} %param.11), kind=kOutput, calls=%fused_computation.4 | convolution fusion | flops 537133056 | bytes 9043968 | tf_op jit(solution)/shard_map/dot_general | solution.py:138
  149.4 12.6 %all_to_all.5 = bf16[2,64,2048]{2,1,0:T(8,128)(2,1)S(1)} all-to-all(bf16[2,64,2048]{2,1,0:T(8,128)(2,1)S(1)} %bitcast.285), channel_id=1, replica_groups=mesh['ctx'=128,'head'=2] {'head'}, dimensions={0} | all-to-all | bytes 1048576 | tf_op jit(solution)/shard_map/all_to_all | solution.py:29
  (173 shorter events, 31.7 us)
Async XLA Ops:
  0.0 35.7 %copy-start.11 = (bf16[64,256]{1,0:T(8,128)(2,1)S(1)}, bf16[64,256]{1,0:T(8,128)(2,1)}, u32[]{:S(2)}) copy-start(bf16[64,256]{1,0:T(8,128)(2,1)} %param.9) | copy-start | bytes 98308
  1.5 73.3 %collective-permute-start.2 = (bf16[64,256]{0,1:T(8,128)(2,1)}, bf16[64,256]{0,1:T(8,128)(2,1)}, u32[]{:S(2)}, u32[]{:S(2)}) collective-permute-start(bf16[64,256]{0,1:T(8,128)(2,1)} %copy.122), channel_id=1, source_target_pairs={{0,2},{2,4},{4,6},{6,8},{8,10},{10,12},{12,14},{14,16},{16,18},{18... | collective-permute-start | bytes 98312 | tf_op jit(solution)/shard_map/ppermute | solution.py:19
  3.4 74.5 %collective-permute-start.4 = (bf16[64,256]{0,1:T(8,128)(2,1)}, bf16[64,256]{0,1:T(8,128)(2,1)}, u32[]{:S(2)}, u32[]{:S(2)}) collective-permute-start(bf16[64,256]{0,1:T(8,128)(2,1)} %copy.122), channel_id=1, source_target_pairs={{0,4},{2,6},{4,8},{6,10},{8,12},{10,14},{12,16},{14,18},{16,20},{1... | collective-permute-start | bytes 98312 | tf_op jit(solution)/shard_map/ppermute | solution.py:19
  8.7 76.0 %collective-permute-start.3 = (bf16[64,256]{0,1:T(8,128)(2,1)}, bf16[64,256]{0,1:T(8,128)(2,1)}, u32[]{:S(2)}, u32[]{:S(2)}) collective-permute-start(bf16[64,256]{0,1:T(8,128)(2,1)} %copy.125), channel_id=1, source_target_pairs={{0,2},{2,4},{4,6},{6,8},{8,10},{10,12},{12,14},{14,16},{16,18},{18... | collective-permute-start | bytes 98312 | tf_op jit(solution)/shard_map/ppermute | solution.py:19
  12.4 72.4 %collective-permute-start.5 = (bf16[64,256]{0,1:T(8,128)(2,1)}, bf16[64,256]{0,1:T(8,128)(2,1)}, u32[]{:S(2)}, u32[]{:S(2)}) collective-permute-start(bf16[64,256]{0,1:T(8,128)(2,1)} %copy.125), channel_id=1, source_target_pairs={{0,4},{2,6},{4,8},{6,10},{8,12},{10,14},{12,16},{14,18},{16,20},{1... | collective-permute-start | bytes 98312 | tf_op jit(solution)/shard_map/ppermute | solution.py:19
  16.9 13.7 %collective-permute-start = (bf16[16,256]{1,0:T(8,128)(2,1)S(1)}, bf16[16,256]{1,0:T(8,128)(2,1)S(1)}, u32[]{:S(2)}, u32[]{:S(2)}) collective-permute-start(bf16[16,256]{1,0:T(8,128)(2,1)S(1)} %slice.96), channel_id=1, source_target_pairs={{0,2},{2,4},{4,6},{6,8},{8,10},{10,12},{12,14},{14,16},{16,18},{18... | collective-permute-start | bytes 24584 | tf_op jit(solution)/shard_map/ppermute | solution.py:19
  30.6 8.0 %collective-permute-start.1 = (bf16[16,256]{1,0:T(8,128)(2,1)S(1)}, bf16[16,256]{1,0:T(8,128)(2,1)S(1)}, u32[]{:S(2)}, u32[]{:S(2)}) collective-permute-start(bf16[16,256]{1,0:T(8,128)(2,1)S(1)} %slice.112), channel_id=1, source_target_pairs={{0,2},{2,4},{4,6},{6,8},{8,10},{10,12},{12,14},{14,16},{16,18},{18... | collective-permute-start | bytes 24584 | tf_op jit(solution)/shard_map/ppermute | solution.py:19
  36.4 2.1 %copy-start.12 = (bf16[64,256]{1,0:T(8,128)(2,1)S(1)}, bf16[64,256]{1,0:T(8,128)(2,1)}, u32[]{:S(2)}) copy-start(bf16[64,256]{1,0:T(8,128)(2,1)} %param.10) | copy-start | bytes 98308
  47.9 16.8 %copy-start.18 = (bf16[64,1,2,128]{3,2,0,1:T(2,128)(2,1)S(1)}, bf16[64,1,2,128]{3,2,0,1:T(2,128)(2,1)}, u32[]{:S(2)}) copy-start(bf16[64,1,2,128]{3,2,0,1:T(2,128)(2,1)} %stack.131) | copy-start | bytes 98308
  47.9 17.4 %copy-start.16 = (bf16[64,1,2,128]{3,2,0,1:T(2,128)(2,1)S(1)}, bf16[64,1,2,128]{3,2,0,1:T(2,128)(2,1)}, u32[]{:S(2)}) copy-start(bf16[64,1,2,128]{3,2,0,1:T(2,128)(2,1)} %stack.132) | copy-start | bytes 98308
  47.9 18.0 %copy-start.17 = (bf16[64,1,2,128]{3,2,0,1:T(2,128)(2,1)S(1)}, bf16[64,1,2,128]{3,2,0,1:T(2,128)(2,1)}, u32[]{:S(2)}) copy-start(bf16[64,1,2,128]{3,2,0,1:T(2,128)(2,1)} %stack.133) | copy-start | bytes 98308
  47.9 18.6 %copy-start.15 = (bf16[64,1,2,128]{3,2,0,1:T(2,128)(2,1)S(1)}, bf16[64,1,2,128]{3,2,0,1:T(2,128)(2,1)}, u32[]{:S(2)}) copy-start(bf16[64,1,2,128]{3,2,0,1:T(2,128)(2,1)} %stack.134) | copy-start | bytes 98308
  47.9 19.3 %copy-start.8 = (pred[64,1024]{1,0:T(8,128)(4,1)S(1)}, pred[64,1024]{1,0:T(8,128)(4,1)}, u32[]{:S(2)}) copy-start(pred[64,1024]{1,0:T(8,128)(4,1)} %copy.115) | copy-start | bytes 196612
  47.9 19.3 %copy-start.14 = (bf16[64,2,128]{2,1,0:T(2,128)(2,1)S(1)}, bf16[64,2,128]{2,1,0:T(2,128)(2,1)}, u32[]{:S(2)}) copy-start(bf16[64,2,128]{2,1,0:T(2,128)(2,1)} %reshape.723) | copy-start | bytes 98308
  67.2 2.8 %copy-start.10 = (bf16[64,16,2,128]{3,2,0,1:T(2,128)(2,1)S(1)}, bf16[64,16,2,128]{3,2,0,1:T(2,128)(2,1)}, u32[]{:S(2)}) copy-start(bf16[64,16,2,128]{3,2,0,1:T(2,128)(2,1)} %constant_dynamic-update-slice_fusion.20) | copy-start | bytes 1572868
  74.8 3.2 %copy-start.6 = (pred[64,1024]{1,0:T(8,128)(4,1)S(1)}, pred[64,1024]{1,0:T(8,128)(4,1)}, u32[]{:S(2)}) copy-start(pred[64,1024]{1,0:T(8,128)(4,1)} %copy.128) | copy-start | bytes 196612
  82.5 9.2 %collective-permute-start.6 = (bf16[128,256]{0,1:T(8,128)(2,1)S(1)}, bf16[128,256]{0,1:T(8,128)(2,1)S(1)}, u32[]{:S(2)}, u32[]{:S(2)}) collective-permute-start(bf16[128,256]{0,1:T(8,128)(2,1)S(1)} %pad_maximum_fusion.2), channel_id=1, source_target_pairs={{0,4},{2,6},{4,8},{6,10},{8,12},{10,14},{12,16},{14,18},{16,20},{1... | collective-permute-start | bytes 196616 | tf_op jit(solution)/shard_map/ppermute | solution.py:19
  85.7 12.0 %collective-permute-start.7 = (bf16[128,256]{0,1:T(8,128)(2,1)S(1)}, bf16[128,256]{0,1:T(8,128)(2,1)S(1)}, u32[]{:S(2)}, u32[]{:S(2)}) collective-permute-start(bf16[128,256]{0,1:T(8,128)(2,1)S(1)} %pad_maximum_fusion.3), channel_id=1, source_target_pairs={{0,4},{2,6},{4,8},{6,10},{8,12},{10,14},{12,16},{14,18},{16,20},{1... | collective-permute-start | bytes 196616 | tf_op jit(solution)/shard_map/ppermute | solution.py:19
  92.7 11.0 %collective-permute-start.8 = (bf16[256,256]{0,1:T(8,128)(2,1)S(1)}, bf16[256,256]{0,1:T(8,128)(2,1)S(1)}, u32[]{:S(2)}, u32[]{:S(2)}) collective-permute-start(bf16[256,256]{0,1:T(8,128)(2,1)S(1)} %pad_maximum_fusion), channel_id=1, source_target_pairs={{0,8},{2,10},{4,12},{6,14},{8,16},{10,18},{12,20},{14,22},{16,24},... | collective-permute-start | bytes 393224 | tf_op jit(solution)/shard_map/ppermute | solution.py:19
  99.3 23.1 %collective-permute-start.9 = (bf16[256,256]{0,1:T(8,128)(2,1)}, bf16[256,256]{0,1:T(8,128)(2,1)S(1)}, u32[]{:S(2)}, u32[]{:S(2)}) collective-permute-start(bf16[256,256]{0,1:T(8,128)(2,1)} %pad_maximum_fusion.1), channel_id=1, source_target_pairs={{0,8},{2,10},{4,12},{6,14},{8,16},{10,18},{12,20},{14,22},{16,24},... | collective-permute-start | bytes 393224 | tf_op jit(solution)/shard_map/ppermute | solution.py:19
  103.6 5.3 %copy-start.9 = (pred[64,1024]{1,0:T(8,128)(4,1)S(1)}, pred[64,1024]{1,0:T(8,128)(4,1)}, u32[]{:S(2)}) copy-start(pred[64,1024]{1,0:T(8,128)(4,1)} %copy.115) | copy-start | bytes 196612
  108.3 3.1 %copy-start.3 = (f32[2,4,1024,64]{2,3,1,0:T(8,128)S(1)}, f32[2,4,1024,64]{2,3,1,0:T(8,128)}, u32[]{:S(2)}) copy-start(f32[2,4,1024,64]{2,3,1,0:T(8,128)} %get-tuple-element.64) | copy-start | bytes 6291460
  108.3 3.1 %copy-start.7 = (pred[64,1024]{1,0:T(8,128)(4,1)S(1)}, pred[64,1024]{1,0:T(8,128)(4,1)}, u32[]{:S(2)}) copy-start(pred[64,1024]{1,0:T(8,128)(4,1)} %copy.121) | copy-start | bytes 196612
  116.2 5.0 %copy-start.2 = (f32[2,4,1024,64]{2,3,1,0:T(8,128)S(1)}, f32[2,4,1024,64]{2,3,1,0:T(8,128)}, u32[]{:S(2)}) copy-start(f32[2,4,1024,64]{2,3,1,0:T(8,128)} %get-tuple-element.62) | copy-start | bytes 6291460
  122.5 5.7 %copy-start = (f32[2,128,4,1024]{3,1,2,0:T(8,128)S(1)}, f32[2,128,4,1024]{3,1,2,0:T(8,128)}, u32[]{:S(2)}) copy-start(f32[2,128,4,1024]{3,1,2,0:T(8,128)} %get-tuple-element.60) | copy-start | bytes 12582916
  129.4 3.9 %copy-start.1 = (f32[2,4,1024,64]{2,3,1,0:T(8,128)S(1)}, f32[2,4,1024,64]{2,3,1,0:T(8,128)}, u32[]{:S(2)}) copy-start(f32[2,4,1024,64]{2,3,1,0:T(8,128)} %get-tuple-element.66) | copy-start | bytes 6291460
  129.4 3.9 %copy-start.13 = (bf16[64,2,128]{2,1,0:T(2,128)(2,1)S(1)}, bf16[64,2,128]{2,1,0:T(2,128)(2,1)}, u32[]{:S(2)}) copy-start(bf16[64,2,128]{2,1,0:T(2,128)(2,1)} %reshape.724) | copy-start | bytes 98308
  133.3 3.2 %copy-start.4 = (f32[2,4,1024,64]{2,3,1,0:T(8,128)S(1)}, f32[2,4,1024,64]{2,3,1,0:T(8,128)}, u32[]{:S(2)}) copy-start(f32[2,4,1024,64]{2,3,1,0:T(8,128)} %get-tuple-element.64) | copy-start | bytes 6291460
  133.3 3.2 %copy-start.5 = (f32[2,64,16,128]{3,2,1,0:T(8,128)S(1)}, f32[2,64,16,128]{3,2,1,0:T(8,128)}, u32[]{:S(2)}) copy-start(f32[2,64,16,128]{3,2,1,0:T(8,128)} %copy.120) | copy-start | bytes 3145732
where the time goes:
time: 165 us; the launch traced here: 163 us
  local copies, waits for them, and re-layouts  48.8 us (30%)
  matrix products  42.6 us (26%)
  starting transfers between devices  31.3 us (19%)
  other arithmetic  22.6 us (14%)
  blocking collectives  12.6 us (8%)
  waiting for transfers between devices  4.06 us (2%)
    ppermute x10, starting transfers between devices, shifted(): lax.ppermute(value, axis, [(source, source + steps) for source in range(i...  31.3 us
    unnamed x72, local copies, waits for them, and re-layouts  21.3 us
    dot_general x5, matrix products, absorb(): jnp.einsum('gmjx,jgd->gmxd', weights, block_values.reshape(block_width, k...  21.1 us
    dot_general x5, matrix products, absorb(): jnp.einsum('gmxd,jgd->gmjx', products, head_keys, preferred_element_type=...  16.5 us
    all_to_all x1, blocking collectives, summed_on_arrival(): lax.all_to_all(parts, axis, split_axis=0, concat_axis=0, tiled=True)  12.6 us
    reduce_sum x10, other arithmetic, absorb(): row_total = row_total * rescale + jnp.sum(expo, axis=(2, 4))  11.6 us
    another operation x17, local copies, waits for them, and re-layouts, body(): jnp.stack([joined_values[offset + 1:offset + 1 + shard_rows] for offset i...  10.6 us
    dot_general x1, matrix products, body(): jnp.dot(attention, out_weight, preferred_element_type=jnp.float32)  4.95 us
  transfers between devices with their start and end apart: 10, of which 3 were waited for; matrix products, arithmetic and copies ran while one was open for 52% of the time, Pallas kernels for 0%

commit v1 on v0

v1 whole, which is shorter than its diff:
```python
import functools
import math

import jax
import jax.numpy as jnp
from jax import lax
from jax.experimental import pallas as pl
from jax.experimental.pallas import tpu as pltpu
from jax.sharding import PartitionSpec as P

HEAD = 128
FIRST = 512
SECOND = 16
LOG2E = 1.4426950408889634
NEG = -1e30


def core_swap(value, count):
    return lax.ppermute(value, "ctx", [(s, s ^ 1) for s in range(count)])


def chip_shift(value, count, even, odd):
    pairs = [(s, s + 2 * (even if s % 2 == 0 else odd)) for s in range(count)]
    return lax.ppermute(value, "ctx", [(a, b) for a, b in pairs if b < count])


def head_swap(value):
    return lax.ppermute(value, "head", [(0, 1), (1, 0)])


def attend_kernel(
    where_ref, q_ref, k_ref, v_ref, ks_ref, vs_ref, x1_ref, y_ref, yp_ref, z_ref, zp_ref, w_hbm,
    mine_ref, other_ref,
    kbuf, vbuf, vt, ksw, svw, acc, att, wbuf, sem,
):
    shard = where_ref[0]
    core = where_ref[1]
    side = where_ref[2]
    rows = q_ref.shape[0]
    kv_heads = k_ref.shape[1] // HEAD
    group = q_ref.shape[1] // k_ref.shape[1]
    half = w_hbm.shape[1] // 2
    reach = FIRST + rows
    lanes = SECOND * rows

    def w_copy(slot, which):
        cols = pl.ds(pl.multiple_of(which * half, 128), half)
        return pltpu.make_async_copy(w_hbm.at[:, cols], wbuf.at[slot], sem.at[slot])

    w_copy(0, 1 - side).start()
    w_copy(1, side).start()

    first_block = shard - core - FIRST // rows
    key_row = jnp.broadcast_to(k_ref[0:1, :], (rows, k_ref.shape[1]))

    def place(block, keys, values):
        good = first_block + block >= 0
        at = pl.ds(pl.multiple_of(block * rows, rows), rows)
        kbuf[at, :] = jnp.where(good, keys, key_row)
        vbuf[at, :] = jnp.where(good, values, jnp.zeros_like(values))

    def place_chip(pair, flip, ref, stride):
        for slot in range(2):
            block = 2 * pair + jnp.where(flip == 1, 1 - slot, slot)
            at = slot * stride
            place(block, ref[at : at + rows, :], ref[at + rows : at + 2 * rows, :])

    tall = y_ref.shape[0] // 2
    place_chip(3 - core, core, y_ref, tall)
    place_chip(2 + core, 1 - core, yp_ref, tall)
    place_chip(1 - core, core, z_ref, 2 * rows)
    place_chip(core, 1 - core, zp_ref, 2 * rows)
    place(8 + core, k_ref[...], v_ref[...])
    place(9 - core, x1_ref[0:rows, :], x1_ref[rows : 2 * rows, :])

    window = pl.ds(pl.multiple_of(core * rows, rows), reach)
    col_block = first_block + core + lax.broadcasted_iota(jnp.int32, (16, reach), 1) // rows
    ones = jnp.where(col_block >= 0, 1.0, 0.0).astype(jnp.bfloat16)

    lane = lax.broadcasted_iota(jnp.int32, (HEAD, 128), 1)
    low = lane < rows

    y_tail = tall + 2 * rows
    x_tail = 2 * rows
    for g in range(kv_heads):
        cols = slice(g * HEAD, (g + 1) * HEAD)
        vt[g, 0:HEAD, :] = vbuf[window, cols].T
        vt[g, HEAD : HEAD + 16, :] = ones
        for own, out, offset in ((ks_ref, ksw, 0), (vs_ref, svw, SECOND)):
            near = y_ref[y_tail + offset : y_tail + offset + SECOND, cols].astype(jnp.float32)
            twin = x1_ref[x_tail + offset : x_tail + offset + SECOND, cols].astype(jnp.float32)
            mine = own[:, cols].astype(jnp.float32)
            tail = jnp.where(core == 1, twin, near)
            stand_in = jnp.broadcast_to(mine[0:1, :], tail.shape) if offset == 0 else jnp.zeros_like(tail)
            tail = jnp.where(shard == 0, stand_in, tail)
            rest = jnp.zeros((128 - SECOND - rows, HEAD), jnp.float32)
            tokens = jnp.concatenate([tail, mine, rest], axis=0).T
            for pair in range(SECOND // 2):
                near_part = pltpu.roll(tokens, (128 - (2 * pair + 1)) % 128, 1)
                far_part = pltpu.roll(tokens, (rows - (2 * pair + 2)) % 128, 1)
                out[g, :, pair * 128 : (pair + 1) * 128] = jnp.where(low, near_part, far_part)

    width = 256
    key_id = lax.broadcasted_iota(jnp.int32, (rows, width), 0)
    token_id = lax.broadcasted_iota(jnp.int32, (rows, width), 1) % rows
    mask_own = jnp.where(key_id <= token_id, 0.0, NEG)
    mask_far = jnp.where(key_id > token_id, 0.0, NEG)
    scale = LOG2E / math.sqrt(HEAD)

    pair_lane = lax.broadcasted_iota(jnp.int32, (1, 128), 1)

    def one_head(h, _):
        g = h // group
        cols = pl.ds(pl.multiple_of(h * HEAD, HEAD), HEAD)
        q = q_ref[:, cols].astype(jnp.float32) * scale
        qt = jnp.concatenate([q, q], axis=0).T
        qt2 = jnp.concatenate([qt] * (width // 128), axis=1)
        keys = kbuf[window, pl.ds(pl.multiple_of(g * HEAD, HEAD), HEAD)]
        values = vt[g]
        tops, totals = [], []
        for c in range(lanes // width):
            at = slice(c * width, (c + 1) * width)
            products = (qt2 * ksw[g, :, at]).astype(jnp.bfloat16)
            s = jnp.dot(keys, products, preferred_element_type=jnp.float32)
            far = s[:rows] + mask_far
            mid = s[rows : reach - rows]
            own = s[reach - rows :] + mask_own
            top = jnp.maximum(jnp.max(mid, axis=0, keepdims=True), jnp.max(own, axis=0, keepdims=True))
            top = jnp.maximum(top, jnp.max(far, axis=0, keepdims=True))
            weights = jnp.concatenate(
                [jnp.exp2(part - top).astype(jnp.bfloat16) for part in (far, mid, own)], axis=0
            )
            mixed = jnp.dot(values, weights, preferred_element_type=jnp.float32)
            acc[:, at] = mixed[:HEAD] * svw[g, :, at]
            tops.append(top)
            totals.append(mixed[HEAD : HEAD + 1])
        top = jnp.concatenate(tops, axis=1)
        total = jnp.concatenate(totals, axis=1)
        tiles = [slice(i * 128, (i + 1) * 128) for i in range(lanes // 128)]
        peak = functools.reduce(jnp.maximum, [top[:, t] for t in tiles])
        peak = jnp.maximum(peak, pltpu.roll(peak, rows, 1))
        out = jnp.zeros((HEAD, 128), jnp.float32)
        norm = jnp.zeros((1, 128), jnp.float32)
        for i, t in enumerate(tiles):
            offset = 2 * i + pair_lane // rows
            fine = (shard > 0) | (pair_lane % rows + offset >= SECOND - 1)
            grow = jnp.exp2(top[:, t] - peak)
            out = out + acc[:, t] * grow
            norm = norm + jnp.where(fine, total[:, t] * grow, 0.0)
        out = out + pltpu.roll(out, rows, 1)
        norm = norm + pltpu.roll(norm, rows, 1)
        att[:, cols] = (out / norm).T[:rows].astype(jnp.bfloat16)
        return 0

    lax.fori_loop(0, kv_heads * group, one_head, 0)

    w_copy(0, 1 - side).wait()
    other_ref[...] = jnp.dot(att[...], wbuf[0], preferred_element_type=jnp.float32).astype(jnp.bfloat16)
    w_copy(1, side).wait()
    mine_ref[...] = jnp.dot(att[...], wbuf[1], preferred_element_type=jnp.float32)


def attend(where, *arrays):
    queries, keys, out_weight = arrays[0], arrays[1], arrays[-1]
    rows, wide = queries.shape
    narrow = keys.shape[1]
    kv_heads = narrow // HEAD
    depth, features = out_weight.shape
    reach, lanes = FIRST + rows, SECOND * rows
    vmem = pl.BlockSpec(memory_space=pltpu.VMEM)
    return pl.pallas_call(
        attend_kernel,
        out_shape=(
            jax.ShapeDtypeStruct((rows, features // 2), jnp.float32),
            jax.ShapeDtypeStruct((rows, features // 2), jnp.bfloat16),
        ),
        in_specs=[pl.BlockSpec(memory_space=pltpu.SMEM)]
        + [vmem] * (len(arrays) - 1)
        + [pl.BlockSpec(memory_space=pl.ANY)],
        out_specs=(vmem, vmem),
        scratch_shapes=[
            pltpu.VMEM((reach + rows, narrow), jnp.bfloat16),
            pltpu.VMEM((reach + rows, narrow), jnp.bfloat16),
            pltpu.VMEM((kv_heads, HEAD + 16, reach), jnp.bfloat16),
            pltpu.VMEM((kv_heads, HEAD, lanes), jnp.float32),
            pltpu.VMEM((kv_heads, HEAD, lanes), jnp.float32),
            pltpu.VMEM((HEAD, lanes), jnp.float32),
            pltpu.VMEM((rows, wide), jnp.bfloat16),
            pltpu.VMEM((2, depth, features // 2), jnp.bfloat16),
            pltpu.SemaphoreType.DMA((2,)),
        ],
        compiler_params=pltpu.CompilerParams(vmem_limit_bytes=40 << 20),
        name="attend",
    )(where, *arrays)


def body(queries, keys_first, primary_value_array, keys_second, secondary_value_array, out_weight):
    count = lax.axis_size("ctx")
    rows = queries.shape[0]
    shard = lax.axis_index("ctx")
    where = jnp.stack([shard, shard % 2, lax.axis_index("head")]).astype(jnp.int32)
    packed = jnp.concatenate(
        [
            keys_first,
            primary_value_array,
            keys_second[rows - SECOND :],
            secondary_value_array[rows - SECOND :],
        ],
        axis=0,
    )
    twin = core_swap(packed, count)
    near_load = jnp.concatenate([packed, twin], axis=0)
    far_load = jnp.concatenate([packed[: 2 * rows], twin[: 2 * rows]], axis=0)
    near = chip_shift(near_load, count, 1, 2)
    far = chip_shift(far_load, count, 3, 4)
    near_twin = core_swap(near, count)
    far_twin = core_swap(far, count)
    mine, other = attend(
        where,
        queries,
        keys_first,
        primary_value_array,
        keys_second,
        secondary_value_array,
        twin,
        near,
        near_twin,
        far,
        far_twin,
        out_weight,
    )
    return (mine + head_swap(other).astype(jnp.float32)).astype(jnp.bfloat16)


def solution(mesh):
    in_specs = (P("ctx", "head"),) * 5 + (P("head", None),)
    return jax.shard_map(body, mesh=mesh, in_specs=in_specs, out_specs=P("ctx", "head"), check_vma=False)
```

time: 165 us -> 71.1 us (0.43)
  matrix products: 42.6 us -> 0 us
  local copies, waits for them, and re-layouts: 48.8 us -> 10.2 us
  Pallas kernels: 0 us -> 23.1 us
  other arithmetic: 22.6 us -> 2.39 us
  starting transfers between devices: 31.3 us -> 14.4 us
  waiting for transfers between devices: 4.06 us -> 20.2 us
  blocking collectives: 12.6 us -> 0 us
    dot_general x11 -> x0, matrix products: 42.6 us -> none  [the longest x5 21.1 us: absorb(): jnp.einsum('gmjx,jgd->gmxd', weights, block_values.reshape(block_width, k...]
    pallas_call x0 -> x1, Pallas kernels: none -> 23.1 us  [attend(): pl.pallas_call(attend_kernel, out_shape=(jax.ShapeDtypeStruct((rows, feat...]
    ppermute x10 -> x6, starting transfers between devices: 31.3 us -> 14.4 us  [the longest x2 11.6 us: chip_shift(): return lax.ppermute(value, 'ctx', [(a, b) for a, b in pairs if b < count])]
    ppermute x10 -> x6, waiting for transfers between devices: 4.06 us -> 20.2 us  [the longest x2 10.5 us: chip_shift(): return lax.ppermute(value, 'ctx', [(a, b) for a, b in pairs if b < count])]
    all_to_all x1 -> x0, blocking collectives: 12.6 us -> none  [summed_on_arrival(): lax.all_to_all(parts, axis, split_axis=0, concat_axis=0, tiled=True)]
    reduce_sum x11 -> x0, other arithmetic: 12.5 us -> none  [the longest x10 11.6 us: absorb(): row_total = row_total * rescale + jnp.sum(expo, axis=(2, 4))]
    another operation x34 -> x0, local copies, waits for them, and re-layouts: 11.7 us -> none  [the longest x17 10.6 us: body(): jnp.stack([joined_values[offset + 1:offset + 1 + shard_rows] for offset i...]
    unnamed x72 -> x16, local copies, waits for them, and re-layouts: 21.3 us -> 10.2 us
  transfers between devices with their start and end apart: 10 -> 6, of which waited for: 3 -> 5; matrix products, arithmetic and copies ran while one was open for 52% -> 1% of each run, Pallas kernels for 0% -> 0%
where the time goes in v1:
time: 71.1 us; the launch traced here: 70.3 us
  Pallas kernels  23.1 us (32%)
  waiting for transfers between devices  20.2 us (28%)
  starting transfers between devices  14.4 us (20%)
  local copies, waits for them, and re-layouts  10.2 us (14%)
  other arithmetic  2.39 us (3%)
    pallas_call x1, Pallas kernels, attend(): pl.pallas_call(attend_kernel, out_shape=(jax.ShapeDtypeStruct((rows, feat...  23.1 us
    ppermute x2, starting transfers between devices, chip_shift(): return lax.ppermute(value, 'ctx', [(a, b) for a, b in pairs if b < count])  11.6 us
    ppermute x2, waiting for transfers between devices, chip_shift(): return lax.ppermute(value, 'ctx', [(a, b) for a, b in pairs if b < count])  10.5 us
    unnamed x16, local copies, waits for them, and re-layouts  10.2 us
    ppermute x1, waiting for transfers between devices, head_swap(): return lax.ppermute(value, 'head', [(0, 1), (1, 0)])  7.11 us
    ppermute x1, starting transfers between devices, head_swap(): return lax.ppermute(value, 'head', [(0, 1), (1, 0)])  2.84 us
    ppermute x3, waiting for transfers between devices, core_swap(): return lax.ppermute(value, 'ctx', [(s, s ^ 1) for s in range(count)])  2.54 us
  transfers between devices with their start and end apart: 6, of which 5 were waited for; matrix products, arithmetic and copies ran while one was open for 1% of the time, Pallas kernels for 0%

profile of v1, /device:TPU:24, one launch (start us, length us, event | category | flops | bytes accessed | tf_op | source)
XLA Modules:
  0.0 70.3 jit_solution(1063175361654681164)
XLA Ops:
  0.0 0.8 %constant_dynamic-update-slice_fusion.4 = bf16[320,256]{1,0:T(8,128)(2,1)S(1)} fusion(bf16[64,256]{1,0:T(8,128)(2,1)} %k_ref.1), kind=kLoop, calls=%fused_computation.7 | loop fusion | bytes 65536
  0.8 0.8 %constant_dynamic-update-slice_fusion.3 = bf16[320,256]{1,0:T(8,128)(2,1)S(1)} fusion(bf16[320,256]{1,0:T(8,128)(2,1)S(1)} %constant_dynamic-update-slice_fusion.4, bf16[64,256]{1,0:T(8,128)(2,1)} %v_ref.1), kind=kLoop, calls=%fused_computation.6 | loop fusion | bytes 65536
  1.5 0.7 constant_dynamic-update-slice_fusion.2
  2.2 0.7 constant_dynamic-update-slice_fusion.1
  2.9 0.8 %pad_maximum_fusion.1 = bf16[160,256]{1,0:T(8,128)(2,1)S(1)} fusion(bf16[16,256]{1,0:T(8,128)(2,1)S(1)} %get-tuple-element.10, bf16[16,256]{1,0:T(8,128)(2,1)S(1)} %get-tuple-element.12, bf16[64,256]{1,0:T(8,128)(2,1)} %v_ref.1, bf16[64,256]{1,0:T(8,128)(2,1)} %k_ref.1), kind=kLoop, calls=%fused_computation.2 | loop fusion | flops 327680 | bytes 163840 | tf_op jit(solution)/shard_map/concatenate | solution.py:202
  3.7 0.0 collective-permute-start
  3.7 1.3 %collective-permute-done.x1_ref = bf16[160,256]{1,0:T(8,128)(2,1)S(1)} collective-permute-done((bf16[160,256]{1,0:T(8,128)(2,1)S(1)}, bf16[160,256]{1,0:T(8,128)(2,1)S(1)}, u32[]{:S(2)}, u32[]{:S(2)}) %collective-permute-start) | collective-permute-done | bytes 81952 | tf_op jit(solution)/shard_map/ppermute | solution.py:19
  5.0 3.8 %collective-permute-start.1 = (bf16[320,256]{1,0:T(8,128)(2,1)S(1)}, bf16[320,256]{1,0:T(8,128)(2,1)S(1)}, u32[]{:S(2)}, u32[]{:S(2)}) collective-permute-start(bf16[320,256]{1,0:T(8,128)(2,1)S(1)} %constant_dynamic-update-slice_fusion), channel_id=1, source_target_pairs={{0,4},{2,10},{4,8},{6,14},{8,12},{10,18},{12,16},{14,22},{16,20},{... | collective-permute-start | bytes 491528 | tf_op jit(solution)/shard_map/ppermute | solution.py:24
  8.8 0.8 %pad_maximum_fusion = bf16[256,256]{1,0:T(8,128)(2,1)S(1)} fusion(bf16[128,256]{1,0:T(8,128)(2,1)S(1)} %slice.14, bf16[64,256]{1,0:T(8,128)(2,1)} %v_ref.1, bf16[64,256]{1,0:T(8,128)(2,1)} %k_ref.1), kind=kLoop, calls=%fused_computation.1 | loop fusion | flops 393216 | bytes 262144 | tf_op jit(solution)/shard_map/concatenate | solution.py:213
  9.6 7.7 %collective-permute-start.3 = (bf16[256,256]{1,0:T(8,128)(2,1)S(1)}, bf16[256,256]{1,0:T(8,128)(2,1)S(1)}, u32[]{:S(2)}, u32[]{:S(2)}) collective-permute-start(bf16[256,256]{1,0:T(8,128)(2,1)S(1)} %pad_maximum_fusion), channel_id=1, source_target_pairs={{0,12},{2,18},{4,16},{6,22},{8,20},{10,26},{12,24},{14,30},{16,28}... | collective-permute-start | bytes 393224 | tf_op jit(solution)/shard_map/ppermute | solution.py:24
  17.4 2.7 %collective-permute-done.1.y_ref = bf16[320,256]{1,0:T(8,128)(2,1)S(1)} collective-permute-done((bf16[320,256]{1,0:T(8,128)(2,1)S(1)}, bf16[320,256]{1,0:T(8,128)(2,1)S(1)}, u32[]{:S(2)}, u32[]{:S(2)}) %collective-permute-start.1) | collective-permute-done | bytes 163872 | tf_op jit(solution)/shard_map/ppermute | solution.py:24
  20.1 0.0 collective-permute-start.2
  20.1 7.8 %collective-permute-done.3.z_ref = bf16[256,256]{1,0:T(8,128)(2,1)S(1)} collective-permute-done((bf16[256,256]{1,0:T(8,128)(2,1)S(1)}, bf16[256,256]{1,0:T(8,128)(2,1)S(1)}, u32[]{:S(2)}, u32[]{:S(2)}) %collective-permute-start.3) | collective-permute-done | bytes 131104 | tf_op jit(solution)/shard_map/ppermute | solution.py:24
  27.9 0.0 collective-permute-start.4
  27.9 0.1 pad_add_fusion.where_ref
  28.0 1.3 %collective-permute-done.4.zp_ref = bf16[256,256]{1,0:T(8,128)(2,1)S(1)} collective-permute-done((bf16[256,256]{1,0:T(8,128)(2,1)S(1)}, bf16[256,256]{1,0:T(8,128)(2,1)S(1)}, u32[]{:S(2)}, u32[]{:S(2)}) %collective-permute-start.4) | collective-permute-done | bytes 131104 | tf_op jit(solution)/shard_map/ppermute | solution.py:19
  29.2 0.0 collective-permute-done.2.yp_ref
  29.2 0.0 copy-start
  29.2 3.4 %copy-done = bf16[1024,4096]{1,0:T(8,128)(2,1)S(1)} copy-done((bf16[1024,4096]{1,0:T(8,128)(2,1)S(1)}, bf16[1024,4096]{1,0:T(8,128)(2,1)}, u32[]{:S(2)}) %copy-start) | copy-done | bytes 8388632
  32.6 0.0 copy-start.1
  32.6 0.8 %copy-done.1 = bf16[64,256]{1,0:T(8,128)(2,1)S(1)} copy-done((bf16[64,256]{1,0:T(8,128)(2,1)S(1)}, bf16[64,256]{1,0:T(8,128)(2,1)}, u32[]{:S(2)}) %copy-start.1) | copy-done | bytes 32792
  33.4 0.0 copy-start.2
  33.4 0.8 %copy-done.2 = bf16[64,256]{1,0:T(8,128)(2,1)S(1)} copy-done((bf16[64,256]{1,0:T(8,128)(2,1)S(1)}, bf16[64,256]{1,0:T(8,128)(2,1)}, u32[]{:S(2)}) %copy-start.2) | copy-done | bytes 32792
  34.1 0.0 copy-start.3
  34.1 0.9 %copy-done.3 = bf16[64,1024]{1,0:T(8,128)(2,1)S(1)} copy-done((bf16[64,1024]{1,0:T(8,128)(2,1)S(1)}, bf16[64,1024]{1,0:T(8,128)(2,1)}, u32[]{:S(2)}) %copy-start.3) | copy-done | bytes 131096
  35.0 0.0 copy-start.4
  35.0 0.8 %copy-done.4 = bf16[64,256]{1,0:T(8,128)(2,1)S(1)} copy-done((bf16[64,256]{1,0:T(8,128)(2,1)S(1)}, bf16[64,256]{1,0:T(8,128)(2,1)}, u32[]{:S(2)}) %copy-start.4) | copy-done | bytes 32792
  35.8 0.0 copy-start.5
  35.8 0.8 %copy-done.5 = bf16[64,256]{1,0:T(8,128)(2,1)S(1)} copy-done((bf16[64,256]{1,0:T(8,128)(2,1)S(1)}, bf16[64,256]{1,0:T(8,128)(2,1)}, u32[]{:S(2)}) %copy-start.5) | copy-done | bytes 32792
  36.6 23.1 %attend.1 = (f32[64,2048]{1,0:T(8,128)S(1)}, bf16[64,2048]{1,0:T(8,128)(2,1)S(1)}) custom-call(s32[3]{0:T(128)S(1)} %pad_add_fusion.where_ref, bf16[64,1024]{1,0:T(8,128)(2,1)S(1)} %copy-done.3, bf16[64,256]{1,0:T(8,128)(2,1)S(1)} %copy-done.1, bf16[64,256]{1,0:T(8,128)(2,1)S(1)} %copy-done.2, bf16[64,256]{1,0:T(8,128)(2,1)S(1)} %copy-done.4, ...), custom_call_target="tpu_custom_call" | custom-call | tf_op jit(solution)/shard_map/attend/pallas_call | solution.py:171
  59.6 2.8 %collective-permute-start.5 = (bf16[64,2048]{1,0:T(8,128)(2,1)S(1)}, bf16[64,2048]{1,0:T(8,128)(2,1)S(1)}, u32[]{:S(2)}, u32[]{:S(2)}) collective-permute-start(bf16[64,2048]{1,0:T(8,128)(2,1)S(1)} %get-tuple-element.8), channel_id=1, source_target_pairs={{0,1},{1,0},{2,3},{3,2},{4,5},{5,4},{6,7},{7,6},{8,9},{9,8},{10,11... | collective-permute-start | bytes 786440 | tf_op jit(solution)/shard_map/ppermute | solution.py:28
  62.5 7.1 %collective-permute-done.5 = bf16[64,2048]{1,0:T(8,128)(2,1)S(1)} collective-permute-done((bf16[64,2048]{1,0:T(8,128)(2,1)S(1)}, bf16[64,2048]{1,0:T(8,128)(2,1)S(1)}, u32[]{:S(2)}, u32[]{:S(2)}) %collective-permute-start.5) | collective-permute-done | bytes 262176 | tf_op jit(solution)/shard_map/ppermute | solution.py:28
  69.6 0.8 %add_convert_fusion = bf16[64,2048]{1,0:T(8,128)(2,1)} fusion(f32[64,2048]{1,0:T(8,128)S(1)} %get-tuple-element.7, bf16[64,2048]{1,0:T(8,128)(2,1)S(1)} %collective-permute-done.5), kind=kLoop, calls=%fused_computation | loop fusion | flops 393216 | bytes 1048576 | tf_op jit(solution)/shard_map/convert_element_type | solution.py:232
  (2 shorter events, 0.0 us)
Async XLA Ops:
  3.7 1.3 %collective-permute-start = (bf16[160,256]{1,0:T(8,128)(2,1)S(1)}, bf16[160,256]{1,0:T(8,128)(2,1)S(1)}, u32[]{:S(2)}, u32[]{:S(2)}) collective-permute-start(bf16[160,256]{1,0:T(8,128)(2,1)S(1)} %pad_maximum_fusion.1), channel_id=1, source_target_pairs={{0,2},{2,0},{4,6},{6,4},{8,10},{10,8},{12,14},{14,12},{16,18},{18,... | collective-permute-start | bytes 245768 | tf_op jit(solution)/shard_map/ppermute | solution.py:19
  5.0 15.1 %collective-permute-start.1 = (bf16[320,256]{1,0:T(8,128)(2,1)S(1)}, bf16[320,256]{1,0:T(8,128)(2,1)S(1)}, u32[]{:S(2)}, u32[]{:S(2)}) collective-permute-start(bf16[320,256]{1,0:T(8,128)(2,1)S(1)} %constant_dynamic-update-slice_fusion), channel_id=1, source_target_pairs={{0,4},{2,10},{4,8},{6,14},{8,12},{10,18},{12,16},{14,22},{16,20},{... | collective-permute-start | bytes 491528 | tf_op jit(solution)/shard_map/ppermute | solution.py:24
  9.6 18.3 %collective-permute-start.3 = (bf16[256,256]{1,0:T(8,128)(2,1)S(1)}, bf16[256,256]{1,0:T(8,128)(2,1)S(1)}, u32[]{:S(2)}, u32[]{:S(2)}) collective-permute-start(bf16[256,256]{1,0:T(8,128)(2,1)S(1)} %pad_maximum_fusion), channel_id=1, source_target_pairs={{0,12},{2,18},{4,16},{6,22},{8,20},{10,26},{12,24},{14,30},{16,28}... | collective-permute-start | bytes 393224 | tf_op jit(solution)/shard_map/ppermute | solution.py:24
  20.1 9.1 %collective-permute-start.2 = (bf16[320,256]{1,0:T(8,128)(2,1)S(1)}, bf16[320,256]{1,0:T(8,128)(2,1)S(1)}, u32[]{:S(2)}, u32[]{:S(2)}) collective-permute-start(bf16[320,256]{1,0:T(8,128)(2,1)S(1)} %collective-permute-done.1.y_ref), channel_id=1, source_target_pairs={{0,2},{2,0},{4,6},{6,4},{8,10},{10,8},{12,14},{14,12},{16,18},{18,... | collective-permute-start | bytes 491528 | tf_op jit(solution)/shard_map/ppermute | solution.py:19
  27.9 1.3 %collective-permute-start.4 = (bf16[256,256]{1,0:T(8,128)(2,1)S(1)}, bf16[256,256]{1,0:T(8,128)(2,1)S(1)}, u32[]{:S(2)}, u32[]{:S(2)}) collective-permute-start(bf16[256,256]{1,0:T(8,128)(2,1)S(1)} %collective-permute-done.3.z_ref), channel_id=1, source_target_pairs={{0,2},{2,0},{4,6},{6,4},{8,10},{10,8},{12,14},{14,12},{16,18},{18,... | collective-permute-start | bytes 393224 | tf_op jit(solution)/shard_map/ppermute | solution.py:19
  29.2 3.4 %copy-start = (bf16[1024,4096]{1,0:T(8,128)(2,1)S(1)}, bf16[1024,4096]{1,0:T(8,128)(2,1)}, u32[]{:S(2)}) copy-start(bf16[1024,4096]{1,0:T(8,128)(2,1)} %w_hbm.1) | copy-start | bytes 25165828
  32.6 0.8 %copy-start.1 = (bf16[64,256]{1,0:T(8,128)(2,1)S(1)}, bf16[64,256]{1,0:T(8,128)(2,1)}, u32[]{:S(2)}) copy-start(bf16[64,256]{1,0:T(8,128)(2,1)} %k_ref.1) | copy-start | bytes 98308
  33.4 0.8 %copy-start.2 = (bf16[64,256]{1,0:T(8,128)(2,1)S(1)}, bf16[64,256]{1,0:T(8,128)(2,1)}, u32[]{:S(2)}) copy-start(bf16[64,256]{1,0:T(8,128)(2,1)} %v_ref.1) | copy-start | bytes 98308
  34.1 0.9 %copy-start.3 = (bf16[64,1024]{1,0:T(8,128)(2,1)S(1)}, bf16[64,1024]{1,0:T(8,128)(2,1)}, u32[]{:S(2)}) copy-start(bf16[64,1024]{1,0:T(8,128)(2,1)} %q_ref.1) | copy-start | bytes 393220
  35.0 0.8 %copy-start.4 = (bf16[64,256]{1,0:T(8,128)(2,1)S(1)}, bf16[64,256]{1,0:T(8,128)(2,1)}, u32[]{:S(2)}) copy-start(bf16[64,256]{1,0:T(8,128)(2,1)} %ks_ref.1) | copy-start | bytes 98308
  35.8 0.8 %copy-start.5 = (bf16[64,256]{1,0:T(8,128)(2,1)S(1)}, bf16[64,256]{1,0:T(8,128)(2,1)}, u32[]{:S(2)}) copy-start(bf16[64,256]{1,0:T(8,128)(2,1)} %vs_ref.1) | copy-start | bytes 98308
  59.6 9.9 %collective-permute-start.5 = (bf16[64,2048]{1,0:T(8,128)(2,1)S(1)}, bf16[64,2048]{1,0:T(8,128)(2,1)S(1)}, u32[]{:S(2)}, u32[]{:S(2)}) collective-permute-start(bf16[64,2048]{1,0:T(8,128)(2,1)S(1)} %get-tuple-element.8), channel_id=1, source_target_pairs={{0,1},{1,0},{2,3},{3,2},{4,5},{5,4},{6,7},{7,6},{8,9},{9,8},{10,11... | collective-permute-start | bytes 786440 | tf_op jit(solution)/shard_map/ppermute | solution.py:28

commit v2 on v1

v2 whole, which is shorter than its diff:
```python
import functools
import math

import jax
import jax.numpy as jnp
from jax import lax
from jax.experimental import pallas as pl
from jax.experimental.pallas import tpu as pltpu
from jax.sharding import PartitionSpec as P


HEAD = 128
FIRST = 512
SECOND = 16
LOG2E = 1.4426950408889634
NEG = -1e30
WIDTH = 256
ANY = pl.BlockSpec(memory_space=pl.ANY)
VMEM = pl.BlockSpec(memory_space=pltpu.VMEM)
SMEM = pl.BlockSpec(memory_space=pltpu.SMEM)
GRANT = pltpu.CompilerParams(vmem_limit_bytes=20 << 20)
SMALL = pltpu.CompilerParams(vmem_limit_bytes=2 << 20)


def core_swap(value, count):
    return lax.ppermute(value, "ctx", [(s, s ^ 1) for s in range(count)])


def chip_shift(value, count, even, odd):
    pairs = [(s, s + 2 * (even if s % 2 == 0 else odd)) for s in range(count)]
    return lax.ppermute(value, "ctx", [(a, b) for a, b in pairs if b < count])


def head_swap(value):
    return lax.ppermute(value, "head", [(0, 1), (1, 0)])


def pack_kernel(k_ref, v_ref, ks_ref, vs_ref, out_ref, sem):
    rows = k_ref.shape[0]
    tail = pl.ds(rows - SECOND, SECOND)
    parts = (
        (k_ref, out_ref.at[pl.ds(0, rows)]),
        (v_ref, out_ref.at[pl.ds(rows, rows)]),
        (ks_ref.at[tail], out_ref.at[pl.ds(2 * rows, SECOND)]),
        (vs_ref.at[tail], out_ref.at[pl.ds(2 * rows + SECOND, SECOND)]),
    )
    copies = [pltpu.make_async_copy(a, b, sem.at[i]) for i, (a, b) in enumerate(parts)]
    for copy in copies:
        copy.start()
    for copy in copies:
        copy.wait()


def pack(k, v, ks, vs):
    rows, wide = k.shape
    return pl.pallas_call(
        pack_kernel,
        out_shape=jax.ShapeDtypeStruct((2 * rows + 2 * SECOND, wide), k.dtype),
        in_specs=[ANY] * 4,
        out_specs=VMEM,
        scratch_shapes=[pltpu.SemaphoreType.DMA((4,))],
        compiler_params=SMALL,
        name="pack",
    )(k, v, ks, vs)


def join_kernel(own_ref, twin_ref, near_ref, far_ref):
    tall = own_ref.shape[0]
    short = far_ref.shape[0] // 2
    near_ref[0:tall] = own_ref[...]
    near_ref[tall : 2 * tall] = twin_ref[...]
    far_ref[0:short] = own_ref[0:short]
    far_ref[short : 2 * short] = twin_ref[0:short]


def join(own, twin):
    tall, wide = own.shape
    return pl.pallas_call(
        join_kernel,
        out_shape=(
            jax.ShapeDtypeStruct((2 * tall, wide), own.dtype),
            jax.ShapeDtypeStruct((2 * (tall - 2 * SECOND), wide), own.dtype),
        ),
        in_specs=[VMEM] * 2,
        out_specs=(VMEM, VMEM),
        compiler_params=SMALL,
        name="join",
    )(own, twin)


def windows(where_ref, ks, vs, x1, y, ksw, svw, kv_heads, rows):
    shard, core = where_ref[0], where_ref[1]
    lanes = SECOND * rows
    tall = y.shape[0] // 2
    token = lax.broadcasted_iota(jnp.int32, (128, lanes), 0)
    pair = lax.broadcasted_iota(jnp.int32, (128, lanes), 1)
    pick = (token == pair % rows + pair // rows + 1).astype(jnp.bfloat16)
    for own, out, at in ((ks, ksw, 0), (vs, svw, SECOND)):
        near = y[tall + 2 * rows + at : tall + 2 * rows + at + SECOND, :]
        twin = x1[2 * rows + at : 2 * rows + at + SECOND, :]
        mine = own[...].astype(jnp.float32)
        tail = jnp.where(core == 1, twin.astype(jnp.float32), near.astype(jnp.float32))
        tail = jnp.where(shard == 0, jnp.zeros_like(tail), tail)
        rest = jnp.zeros((128 - SECOND - rows, mine.shape[1]), jnp.float32)
        tokens = jnp.concatenate([tail, mine, rest], axis=0)
        for g in range(kv_heads):
            turned = tokens[:, g * HEAD : (g + 1) * HEAD].T.astype(jnp.bfloat16)
            out[g] = jnp.dot(turned, pick, preferred_element_type=jnp.float32).astype(out.dtype)


def turn_queries(q, qt, heads):
    scale = LOG2E / math.sqrt(HEAD)
    for h in range(heads):
        part = q[:, h * HEAD : (h + 1) * HEAD].astype(jnp.float32) * scale
        qt[h] = jnp.concatenate([part, part], axis=0).T


def stage_masks(where_ref, kcat, paug, start, span, first_block, mask_at, later_ok, rows, kv_heads):
    lanes = SECOND * rows
    row = lax.broadcasted_iota(jnp.int32, (span, HEAD), 0)
    col = lax.broadcasted_iota(jnp.int32, (span, HEAD), 1)
    gone = jnp.where(first_block + row // rows < 0, NEG, 0.0)
    extra = jnp.where(col == rows, gone, jnp.where(col == rows + 1, 1.0, 0.0))
    extra = jnp.where((col < rows) & (row - mask_at == col), 1.0, extra).astype(jnp.bfloat16)
    window = pl.ds(pl.multiple_of(start, rows), span)
    for g in range(kv_heads):
        kcat[g, window, HEAD : 2 * HEAD] = extra
    feature = lax.broadcasted_iota(jnp.int32, (HEAD, lanes), 0)
    pair = lax.broadcasted_iota(jnp.int32, (HEAD, lanes), 1)
    token = pair % rows
    hidden = (feature <= token) if later_ok else (feature > token)
    bias = jnp.where((feature < rows) & hidden, NEG, 0.0)
    bias = jnp.where(feature == rows, 1.0, bias)
    early = (where_ref[0] == 0) & (token + pair // rows < SECOND - 1)
    bias = jnp.where((feature == rows + 1) & early, NEG, bias)
    paug[...] = bias.astype(jnp.bfloat16)


def stage_values(vbuf, vt, start, span, rows, kv_heads):
    window = pl.ds(pl.multiple_of(start, rows), span)
    for g in range(kv_heads):
        vt[g] = vbuf[window, g * HEAD : (g + 1) * HEAD].T


def run_heads(kcat, start, span, qt, ksw, svw, paug, vt, sbufs, wbufs, tops, totals, acc, stat, group, heads, rows, finish):
    lanes = SECOND * rows
    chunks = lanes // WIDTH
    window = pl.ds(pl.multiple_of(start, rows), span)

    def score(h, c):
        g = h // group
        at = slice(c * WIDTH, (c + 1) * WIDTH)
        q = qt[h]
        products = jnp.concatenate([q] * (WIDTH // 128), axis=1) * ksw[g, :, at].astype(jnp.float32)
        products = jnp.concatenate([products.astype(jnp.bfloat16), paug[:, at]], axis=0)
        s = jnp.dot(kcat[g, window, :], products, preferred_element_type=jnp.float32)
        sbufs[c % 2][...] = s
        tops[c % 2][...] = jnp.max(s, axis=0, keepdims=True)

    def soften(c):
        e = jnp.exp2(sbufs[c % 2][...] - tops[c % 2][...])
        wbufs[c % 2][...] = e.astype(jnp.bfloat16)
        totals[c % 2][0:1, :] = jnp.sum(e, axis=0, keepdims=True)
        totals[c % 2][1:2, :] = tops[c % 2][...]

    def mix(h, c):
        g = h // group
        at = slice(c * WIDTH, (c + 1) * WIDTH)
        mixed = jnp.dot(vt[g], wbufs[c % 2][...], preferred_element_type=jnp.float32)
        acc[h % 2, :, at] = mixed * svw[g, :, at].astype(jnp.float32)
        stat[h % 2, :, at] = totals[c % 2][...]

    def combine(h):
        slot = h % 2
        tiles = [slice(i * 128, (i + 1) * 128) for i in range(lanes // 128)]
        top = [stat[slot, 1:2, t] for t in tiles]
        peak = functools.reduce(jnp.maximum, top)
        peak = jnp.maximum(peak, pltpu.roll(peak, rows, 1))
        out, norm = None, None
        for i, t in enumerate(tiles):
            grow = jnp.exp2(top[i] - peak)
            more, plus = acc[slot, :, t] * grow, stat[slot, 0:1, t] * grow
            out, norm = (more, plus) if out is None else (out + more, norm + plus)
        out = out + pltpu.roll(out, rows, 1)
        norm = norm + pltpu.roll(norm, rows, 1)
        finish(h, out, peak, norm)

    def one_head(h, _):
        later = jnp.minimum(h + 1, heads - 1)
        combine(jnp.maximum(h - 1, 0))
        for c in range(chunks):
            mix(h, c)
            soften((c + 1) % chunks)
            score(h if c + 2 < chunks else later, (c + 2) % chunks)
        return 0

    acc[...] = jnp.zeros_like(acc)
    stat[...] = jnp.zeros_like(stat)
    score(0, 0)
    score(0, 1)
    soften(0)
    lax.fori_loop(0, heads, one_head, 0)
    combine(heads - 1)


def start_all(pairs, sem):
    copies = [pltpu.make_async_copy(a, b, sem.at[i]) for i, (a, b) in enumerate(pairs)]
    for copy in copies:
        copy.start()
    return copies


def block_copies(ref, row, rows, block, kcat, vbuf):
    at = pl.ds(pl.multiple_of(block * rows, rows), rows)
    keys = ref.at[pl.ds(row, rows)]
    pairs = [(keys.at[:, pl.ds(g * HEAD, HEAD)], kcat.at[g, at, pl.ds(0, HEAD)]) for g in range(kcat.shape[0])]
    return pairs + [(ref.at[pl.ds(row + rows, rows)], vbuf.at[at])]


def chip_blocks(ref, stride, rows, pair, flip, kcat, vbuf):
    pairs = []
    for slot in range(2):
        block = 2 * pair + jnp.where(flip == 1, 1 - slot, slot)
        pairs += block_copies(ref, slot * stride, rows, block, kcat, vbuf)
    return pairs


def near_kernel(
    where_ref, q_hbm, x0_hbm, ks_hbm, vs_hbm, x1_hbm, y_hbm, yp_hbm,
    out_ref, peak_ref, norm_ref, ksw, svw, qt,
    q, ks, vs, x1, y, kcat, vbuf, vt, paug, s0, s1, w0, w1, t0, t1, n0, n1, acc, stat, sem,
):
    shard, core = where_ref[0], where_ref[1]
    rows, wide = q_hbm.shape
    kv_heads, heads = kcat.shape[0], wide // HEAD
    blocks = vbuf.shape[0] // rows
    span = (blocks - 1) * rows
    tall = y_hbm.shape[0] // 2
    pairs = [(q_hbm, q), (ks_hbm, ks), (vs_hbm, vs), (x1_hbm, x1), (y_hbm, y)]
    pairs += block_copies(x0_hbm, 0, rows, blocks - 2 + core, kcat, vbuf)
    pairs += block_copies(x1_hbm, 0, rows, blocks - 1 - core, kcat, vbuf)
    pairs += chip_blocks(y_hbm, tall, rows, 1 - core, core, kcat, vbuf)
    pairs += chip_blocks(yp_hbm, tall, rows, core, 1 - core, kcat, vbuf)
    copies = start_all(pairs, sem)
    start = core * rows
    stage_masks(where_ref, kcat, paug, start, span, shard - (blocks - 2), span - rows, False, rows, kv_heads)
    for copy in copies:
        copy.wait()
    windows(where_ref, ks, vs, x1, y, ksw, svw, kv_heads, rows)
    turn_queries(q, qt, heads)
    stage_values(vbuf, vt, start, span, rows, kv_heads)

    def finish(h, out, peak, norm):
        out_ref[h] = out
        peak_ref[h] = jnp.broadcast_to(peak, (8, 128))
        norm_ref[h] = jnp.broadcast_to(norm, (8, 128))

    run_heads(
        kcat, start, span, qt, ksw, svw, paug, vt, (s0, s1), (w0, w1), (t0, t1), (n0, n1), acc, stat,
        heads // kv_heads, heads, rows, finish,
    )


def far_kernel(
    where_ref, y_hbm, z_hbm, zp_hbm, acc1_ref, peak1_ref, norm1_ref, ksw, svw, qt, w_hbm,
    mine_ref, other_ref,
    kcat, vbuf, vt, paug, s0, s1, w0, w1, t0, t1, n0, n1, acc, stat, att, wbuf, sem, wsem,
):
    shard, core, side = where_ref[0], where_ref[1], where_ref[2]
    rows, wide = att.shape
    kv_heads, heads = kcat.shape[0], wide // HEAD
    half = w_hbm.shape[1] // 2
    blocks = vbuf.shape[0] // rows
    span = (blocks - 1) * rows
    tall = y_hbm.shape[0] // 2
    pairs = chip_blocks(z_hbm, 2 * rows, rows, 1 - core, core, kcat, vbuf)
    pairs += chip_blocks(zp_hbm, 2 * rows, rows, core, 1 - core, kcat, vbuf)
    pairs += block_copies(y_hbm, tall, rows, blocks - 1, kcat, vbuf)
    copies = start_all(pairs, sem)

    def w_copy(slot, which):
        cols = pl.ds(pl.multiple_of(which * half, 128), half)
        return pltpu.make_async_copy(w_hbm.at[:, cols], wbuf.at[slot], wsem.at[slot])

    w_copy(0, 1 - side).start()
    w_copy(1, side).start()
    start = core * rows
    stage_masks(where_ref, kcat, paug, start, span, shard - FIRST // rows, 0, True, rows, kv_heads)
    for copy in copies:
        copy.wait()
    stage_values(vbuf, vt, start, span, rows, kv_heads)

    def finish(h, out, peak, norm):
        before = peak1_ref[h][0:1]
        both = jnp.maximum(peak, before)
        grow, grow1 = jnp.exp2(peak - both), jnp.exp2(before - both)
        norm = norm * grow + norm1_ref[h][0:1] * grow1
        out = (out * grow + acc1_ref[h] * grow1) / norm
        att[:, pl.ds(pl.multiple_of(h * HEAD, HEAD), HEAD)] = out.T[:rows].astype(jnp.bfloat16)

    run_heads(
        kcat, start, span, qt, ksw, svw, paug, vt, (s0, s1), (w0, w1), (t0, t1), (n0, n1), acc, stat,
        heads // kv_heads, heads, rows, finish,
    )
    w_copy(0, 1 - side).wait()
    other_ref[...] = jnp.dot(att[...], wbuf[0], preferred_element_type=jnp.float32).astype(jnp.bfloat16)
    w_copy(1, side).wait()
    mine_ref[...] = jnp.dot(att[...], wbuf[1], preferred_element_type=jnp.float32)


def common_scratch(rows, kv_heads, blocks):
    lanes, span = SECOND * rows, (blocks - 1) * rows
    return [
        pltpu.VMEM((kv_heads, blocks * rows, 2 * HEAD), jnp.bfloat16),
        pltpu.VMEM((blocks * rows, kv_heads * HEAD), jnp.bfloat16),
        pltpu.VMEM((kv_heads, HEAD, span), jnp.bfloat16),
        pltpu.VMEM((HEAD, lanes), jnp.bfloat16),
        pltpu.VMEM((span, WIDTH), jnp.float32),
        pltpu.VMEM((span, WIDTH), jnp.float32),
        pltpu.VMEM((span, WIDTH), jnp.bfloat16),
        pltpu.VMEM((span, WIDTH), jnp.bfloat16),
        pltpu.VMEM((1, WIDTH), jnp.float32),
        pltpu.VMEM((1, WIDTH), jnp.float32),
        pltpu.VMEM((2, WIDTH), jnp.float32),
        pltpu.VMEM((2, WIDTH), jnp.float32),
        pltpu.VMEM((2, HEAD, lanes), jnp.float32),
        pltpu.VMEM((2, 2, lanes), jnp.float32),
    ]


def attend_near(where, q, x0, ks, vs, x1, y, yp):
    rows, wide = q.shape
    kv_heads, heads, lanes = ks.shape[1] // HEAD, wide // HEAD, SECOND * rows
    return pl.pallas_call(
        near_kernel,
        out_shape=(
            jax.ShapeDtypeStruct((heads, HEAD, 128), jnp.float32),
            jax.ShapeDtypeStruct((heads, 8, 128), jnp.float32),
            jax.ShapeDtypeStruct((heads, 8, 128), jnp.float32),
            jax.ShapeDtypeStruct((kv_heads, HEAD, lanes), jnp.bfloat16),
            jax.ShapeDtypeStruct((kv_heads, HEAD, lanes), jnp.bfloat16),
            jax.ShapeDtypeStruct((heads, HEAD, 128), jnp.float32),
        ),
        in_specs=[SMEM] + [ANY] * 7,
        out_specs=(VMEM,) * 6,
        scratch_shapes=[pltpu.VMEM(a.shape, a.dtype) for a in (q, ks, vs, x1, y)]
        + common_scratch(rows, kv_heads, 6)
        + [pltpu.SemaphoreType.DMA((23,))],
        compiler_params=GRANT,
        cost_estimate=pl.CostEstimate(flops=8_000_000_000, transcendentals=4_000_000, bytes_accessed=16_000_000),
        name="near",
    )(where, q, x0, ks, vs, x1, y, yp)


def attend_far(where, y, z, zp, acc1, peak1, norm1, ksw, svw, qt, w):
    kv_heads, heads = ksw.shape[0], qt.shape[0]
    rows = ksw.shape[2] // SECOND
    depth, features = w.shape
    return pl.pallas_call(
        far_kernel,
        out_shape=(
            jax.ShapeDtypeStruct((rows, features // 2), jnp.float32),
            jax.ShapeDtypeStruct((rows, features // 2), jnp.bfloat16),
        ),
        in_specs=[SMEM] + [ANY] * 3 + [VMEM] * 6 + [ANY],
        out_specs=(VMEM, VMEM),
        scratch_shapes=common_scratch(rows, kv_heads, 5)
        + [
            pltpu.VMEM((rows, heads * HEAD), jnp.bfloat16),
            pltpu.VMEM((2, depth, features // 2), jnp.bfloat16),
            pltpu.SemaphoreType.DMA((15,)),
            pltpu.SemaphoreType.DMA((2,)),
        ],
        compiler_params=GRANT,
        name="far",
    )(where, y, z, zp, acc1, peak1, norm1, ksw, svw, qt, w)


def body(queries, keys_first, primary_value_array, keys_second, secondary_value_array, out_weight):
    count = lax.axis_size("ctx")
    queries, keys_first, primary_value_array, keys_second, secondary_value_array, out_weight = (
        pltpu.with_memory_space_constraint(a, pltpu.HBM)
        for a in (queries, keys_first, primary_value_array, keys_second, secondary_value_array, out_weight)
    )
    shard = lax.axis_index("ctx")
    where = jnp.stack([shard, shard % 2, lax.axis_index("head")]).astype(jnp.int32)
    packed = pack(keys_first, primary_value_array, keys_second, secondary_value_array)
    twin = core_swap(packed, count)
    near_load, far_load = join(packed, twin)
    near = chip_shift(near_load, count, 1, 2)
    far = chip_shift(far_load, count, 3, 4)
    near_twin = core_swap(near, count)
    sums = attend_near(where, queries, packed, keys_second, secondary_value_array, twin, near, near_twin)
    far_twin = core_swap(far, count)
    mine, other = attend_far(where, near, far, far_twin, *sums, out_weight)
    other = head_swap(other)
    return (mine + other.astype(jnp.float32)).astype(jnp.bfloat16)


def solution(mesh):
    in_specs = (P("ctx", "head"),) * 5 + (P("head", None),)
    return jax.shard_map(body, mesh=mesh, in_specs=in_specs, out_specs=P("ctx", "head"), check_vma=False)
```

time: 71.1 us -> 60.7 us (0.85)
  waiting for transfers between devices: 20.2 us -> 31.2 us
  local copies, waits for them, and re-layouts: 10.2 us -> 0 us
  Pallas kernels: 23.1 us -> 17.5 us
  starting transfers between devices: 14.4 us -> 10.9 us
  other arithmetic: 2.39 us -> 0.83 us
    ppermute x2, waiting for transfers between devices: 10.5 us -> 22.9 us  [chip_shift(): return lax.ppermute(value, 'ctx', [(a, b) for a, b in pairs if b < count])]
    unnamed x16 -> x0, local copies, waits for them, and re-layouts: 10.2 us -> none
    pallas_call x1 -> x4, Pallas kernels: 23.1 us -> 17.5 us  [the longest x1 8.68 us: attend_far(): pl.pallas_call(far_kernel, out_shape=(jax.ShapeDtypeStruct((rows, feature...]
    ppermute x2, starting transfers between devices: 11.6 us -> 6.22 us  [chip_shift(): return lax.ppermute(value, 'ctx', [(a, b) for a, b in pairs if b < count])]
    ppermute x3, starting transfers between devices: 0.01 us -> 1.89 us  [core_swap(): return lax.ppermute(value, 'ctx', [(s, s ^ 1) for s in range(count)])]
    concatenate x2 -> x0, other arithmetic: 1.57 us -> none  [the longest x1 0.79 us: body(): far_load = jnp.concatenate([packed[:2 * rows], twin[:2 * rows]], axis=0)]
    ppermute x3, waiting for transfers between devices: 2.54 us -> 1.27 us  [core_swap(): return lax.ppermute(value, 'ctx', [(s, s ^ 1) for s in range(count)])]
  transfers between devices with their start and end apart: 6 -> 6, of which waited for: 5 -> 4; matrix products, arithmetic and copies ran while one was open for 1% -> 0% of each run, Pallas kernels for 0% -> 13%
where the time goes in v2:
time: 60.7 us; the launch traced here: 60.5 us
  waiting for transfers between devices  31.2 us (51%)
  Pallas kernels  17.5 us (29%)
  starting transfers between devices  10.9 us (18%)
  other arithmetic  0.83 us (1%)
    ppermute x2, waiting for transfers between devices, chip_shift(): return lax.ppermute(value, 'ctx', [(a, b) for a, b in pairs if b < count])  22.9 us
    pallas_call x1, Pallas kernels, attend_far(): pl.pallas_call(far_kernel, out_shape=(jax.ShapeDtypeStruct((rows, feature...  8.68 us
    pallas_call x1, Pallas kernels, attend_near(): pl.pallas_call(near_kernel, out_shape=(jax.ShapeDtypeStruct((heads, HEAD,...  7.95 us
    ppermute x1, waiting for transfers between devices, head_swap(): return lax.ppermute(value, 'head', [(0, 1), (1, 0)])  7 us
    ppermute x2, starting transfers between devices, chip_shift(): return lax.ppermute(value, 'ctx', [(a, b) for a, b in pairs if b < count])  6.22 us
    ppermute x1, starting transfers between devices, head_swap(): return lax.ppermute(value, 'head', [(0, 1), (1, 0)])  2.81 us
    ppermute x3, starting transfers between devices, core_swap(): return lax.ppermute(value, 'ctx', [(s, s ^ 1) for s in range(count)])  1.89 us
    ppermute x3, waiting for transfers between devices, core_swap(): return lax.ppermute(value, 'ctx', [(s, s ^ 1) for s in range(count)])  1.27 us
  transfers between devices with their start and end apart: 6, of which 4 were waited for; matrix products, arithmetic and copies ran while one was open for 0% of the time, Pallas kernels for 13%

profile of v2, /device:TPU:24, one launch (start us, length us, event | category | flops | bytes accessed | tf_op | source)
XLA Modules:
  0.0 60.5 jit_solution(16415136511137264778)
XLA Ops:
  0.0 0.8 %pack.1.own_ref.x0_hbm = bf16[160,256]{1,0:T(8,128)(2,1)S(1)} custom-call(bf16[64,256]{1,0:T(8,128)(2,1)} %k_ref.1, bf16[64,256]{1,0:T(8,128)(2,1)} %v_ref.1, bf16[64,256]{1,0:T(8,128)(2,1)} %ks_hbm.1, bf16[64,256]{1,0:T(8,128)(2,1)} %vs_hbm.1), custom_call_target="tpu_custom_call" | custom-call | tf_op jit(solution)/shard_map/pack/pallas_call | solution.py:56
  0.8 0.1 collective-permute-start
  0.9 1.3 %collective-permute-done.twin_ref.x1_hbm = bf16[160,256]{1,0:T(8,128)(2,1)S(1)} collective-permute-done((bf16[160,256]{1,0:T(8,128)(2,1)S(1)}, bf16[160,256]{1,0:T(8,128)(2,1)S(1)}, u32[]{:S(2)}, u32[]{:S(2)}) %collective-permute-start) | collective-permute-done | bytes 81952 | tf_op jit(solution)/shard_map/ppermute | solution.py:26
  2.2 3.8 %collective-permute-start.1 = (bf16[320,256]{1,0:T(8,128)(2,1)S(1)}, bf16[320,256]{1,0:T(8,128)(2,1)S(1)}, u32[]{:S(2)}, u32[]{:S(2)}) collective-permute-start(bf16[320,256]{1,0:T(8,128)(2,1)S(1)} %get-tuple-element.15), channel_id=1, source_target_pairs={{0,4},{2,10},{4,8},{6,14},{8,12},{10,18},{12,16},{14,22},{16,20},{... | collective-permute-start | bytes 491528 | tf_op jit(solution)/shard_map/ppermute | solution.py:31
  6.0 11.3 %collective-permute-done.1.y_hbm = bf16[320,256]{1,0:T(8,128)(2,1)S(1)} collective-permute-done((bf16[320,256]{1,0:T(8,128)(2,1)S(1)}, bf16[320,256]{1,0:T(8,128)(2,1)S(1)}, u32[]{:S(2)}, u32[]{:S(2)}) %collective-permute-start.1) | collective-permute-done | bytes 163872 | tf_op jit(solution)/shard_map/ppermute | solution.py:31
  17.3 0.0 collective-permute-start.4
  17.4 2.4 %collective-permute-start.2 = (bf16[256,256]{1,0:T(8,128)(2,1)S(1)}, bf16[256,256]{1,0:T(8,128)(2,1)S(1)}, u32[]{:S(2)}, u32[]{:S(2)}) collective-permute-start(bf16[256,256]{1,0:T(8,128)(2,1)S(1)} %get-tuple-element.16), channel_id=1, source_target_pairs={{0,12},{2,18},{4,16},{6,22},{8,20},{10,26},{12,24},{14,30},{16,28}... | collective-permute-start | bytes 393224 | tf_op jit(solution)/shard_map/ppermute | solution.py:31
  19.8 0.1 pad_add_fusion.where_ref
  19.8 11.6 %collective-permute-done.2.z_hbm = bf16[256,256]{1,0:T(8,128)(2,1)S(1)} collective-permute-done((bf16[256,256]{1,0:T(8,128)(2,1)S(1)}, bf16[256,256]{1,0:T(8,128)(2,1)S(1)}, u32[]{:S(2)}, u32[]{:S(2)}) %collective-permute-start.2) | collective-permute-done | bytes 131104 | tf_op jit(solution)/shard_map/ppermute | solution.py:31
  31.4 1.8 %collective-permute-start.3 = (bf16[256,256]{1,0:T(8,128)(2,1)S(1)}, bf16[256,256]{1,0:T(8,128)(2,1)S(1)}, u32[]{:S(2)}, u32[]{:S(2)}) collective-permute-start(bf16[256,256]{1,0:T(8,128)(2,1)S(1)} %collective-permute-done.2.z_hbm), channel_id=1, source_target_pairs={{0,2},{2,0},{4,6},{6,4},{8,10},{10,8},{12,14},{14,12},{16,18},{18,... | collective-permute-start | bytes 393224 | tf_op jit(solution)/shard_map/ppermute | solution.py:26
  33.2 0.0 collective-permute-done.4.yp_hbm
  33.2 8.0 %near.1 = (f32[8,128,128]{2,1,0:T(8,128)S(1)}, f32[8,8,128]{2,1,0:T(8,128)S(1)}, f32[8,8,128]{2,1,0:T(8,128)S(1)}, bf16[2,128,1024]{2,1,0:T(8,128)(2,1)S(1)}, bf...) custom-call(s32[3]{0:T(128)S(1)} %pad_add_fusion.where_ref, bf16[64,1024]{1,0:T(8,128)(2,1)} %q_hbm.1, ...), custom_call_target="tpu_custom_call" | custom-call | flops 8000000000 | bytes 16000000 | tf_op jit(solution)/shard_map/near/pallas_call | solution.py:334
  41.2 0.0 collective-permute-done.3.zp_hbm
  41.2 8.7 %far.1 = (f32[64,2048]{1,0:T(8,128)S(1)}, bf16[64,2048]{1,0:T(8,128)(2,1)S(1)}) custom-call(s32[3]{0:T(128)S(1)} %pad_add_fusion.where_ref, bf16[320,256]{1,0:T(8,128)(2,1)S(1)} %collective-permute-done.1.y_hbm, bf16[256,256]{1,0:T(8,128)(2,1)S(1)} %collective-permute-done.2.z_hbm, bf16[256,256]{1,0:T(8,128)(2,1)S(1)} %collective-permute-done.3.zp_hbm, ...), custom_call_target="tpu_custom_call" | custom-call | tf_op jit(solution)/shard_map/far/pallas_call | solution.py:359
  49.9 2.8 %collective-permute-start.5 = (bf16[64,2048]{1,0:T(8,128)(2,1)S(1)}, bf16[64,2048]{1,0:T(8,128)(2,1)S(1)}, u32[]{:S(2)}, u32[]{:S(2)}) collective-permute-start(bf16[64,2048]{1,0:T(8,128)(2,1)S(1)} %get-tuple-element.24), channel_id=1, source_target_pairs={{0,1},{1,0},{2,3},{3,2},{4,5},{5,4},{6,7},{7,6},{8,9},{9,8},{10,11... | collective-permute-start | bytes 786440 | tf_op jit(solution)/shard_map/ppermute | solution.py:35
  52.7 7.0 %collective-permute-done.5 = bf16[64,2048]{1,0:T(8,128)(2,1)S(1)} collective-permute-done((bf16[64,2048]{1,0:T(8,128)(2,1)S(1)}, bf16[64,2048]{1,0:T(8,128)(2,1)S(1)}, u32[]{:S(2)}, u32[]{:S(2)}) %collective-permute-start.5) | collective-permute-done | bytes 262176 | tf_op jit(solution)/shard_map/ppermute | solution.py:35
  59.7 0.8 %add_convert_fusion = bf16[64,2048]{1,0:T(8,128)(2,1)} fusion(f32[64,2048]{1,0:T(8,128)S(1)} %get-tuple-element.23, bf16[64,2048]{1,0:T(8,128)(2,1)S(1)} %collective-permute-done.5), kind=kLoop, calls=%fused_computation | loop fusion | flops 393216 | bytes 1048576 | tf_op jit(solution)/shard_map/convert_element_type | solution.py:397
  (1 shorter events, 0.0 us)
Async XLA Ops:
  0.8 1.4 %collective-permute-start = (bf16[160,256]{1,0:T(8,128)(2,1)S(1)}, bf16[160,256]{1,0:T(8,128)(2,1)S(1)}, u32[]{:S(2)}, u32[]{:S(2)}) collective-permute-start(bf16[160,256]{1,0:T(8,128)(2,1)S(1)} %pack.1.own_ref.x0_hbm), channel_id=1, source_target_pairs={{0,2},{2,0},{4,6},{6,4},{8,10},{10,8},{12,14},{14,12},{16,18},{18,... | collective-permute-start | bytes 245768 | tf_op jit(solution)/shard_map/ppermute | solution.py:26
  2.2 15.1 %collective-permute-start.1 = (bf16[320,256]{1,0:T(8,128)(2,1)S(1)}, bf16[320,256]{1,0:T(8,128)(2,1)S(1)}, u32[]{:S(2)}, u32[]{:S(2)}) collective-permute-start(bf16[320,256]{1,0:T(8,128)(2,1)S(1)} %get-tuple-element.15), channel_id=1, source_target_pairs={{0,4},{2,10},{4,8},{6,14},{8,12},{10,18},{12,16},{14,22},{16,20},{... | collective-permute-start | bytes 491528 | tf_op jit(solution)/shard_map/ppermute | solution.py:31
  17.3 15.9 %collective-permute-start.4 = (bf16[320,256]{1,0:T(8,128)(2,1)S(1)}, bf16[320,256]{1,0:T(8,128)(2,1)S(1)}, u32[]{:S(2)}, u32[]{:S(2)}) collective-permute-start(bf16[320,256]{1,0:T(8,128)(2,1)S(1)} %collective-permute-done.1.y_hbm), channel_id=1, source_target_pairs={{0,2},{2,0},{4,6},{6,4},{8,10},{10,8},{12,14},{14,12},{16,18},{18,... | collective-permute-start | bytes 491528 | tf_op jit(solution)/shard_map/ppermute | solution.py:26
  17.4 14.1 %collective-permute-start.2 = (bf16[256,256]{1,0:T(8,128)(2,1)S(1)}, bf16[256,256]{1,0:T(8,128)(2,1)S(1)}, u32[]{:S(2)}, u32[]{:S(2)}) collective-permute-start(bf16[256,256]{1,0:T(8,128)(2,1)S(1)} %get-tuple-element.16), channel_id=1, source_target_pairs={{0,12},{2,18},{4,16},{6,22},{8,20},{10,26},{12,24},{14,30},{16,28}... | collective-permute-start | bytes 393224 | tf_op jit(solution)/shard_map/ppermute | solution.py:31
  31.4 9.8 %collective-permute-start.3 = (bf16[256,256]{1,0:T(8,128)(2,1)S(1)}, bf16[256,256]{1,0:T(8,128)(2,1)S(1)}, u32[]{:S(2)}, u32[]{:S(2)}) collective-permute-start(bf16[256,256]{1,0:T(8,128)(2,1)S(1)} %collective-permute-done.2.z_hbm), channel_id=1, source_target_pairs={{0,2},{2,0},{4,6},{6,4},{8,10},{10,8},{12,14},{14,12},{16,18},{18,... | collective-permute-start | bytes 393224 | tf_op jit(solution)/shard_map/ppermute | solution.py:26
  49.9 9.8 %collective-permute-start.5 = (bf16[64,2048]{1,0:T(8,128)(2,1)S(1)}, bf16[64,2048]{1,0:T(8,128)(2,1)S(1)}, u32[]{:S(2)}, u32[]{:S(2)}) collective-permute-start(bf16[64,2048]{1,0:T(8,128)(2,1)S(1)} %get-tuple-element.24), channel_id=1, source_target_pairs={{0,1},{1,0},{2,3},{3,2},{4,5},{5,4},{6,7},{7,6},{8,9},{9,8},{10,11... | collective-permute-start | bytes 786440 | tf_op jit(solution)/shard_map/ppermute | solution.py:35

commit v3 on v2

v3 whole, which is shorter than its diff:
```python
import functools
import math

import jax
import jax.numpy as jnp
from jax import lax
from jax.experimental import pallas as pl
from jax.experimental.pallas import tpu as pltpu
from jax.sharding import PartitionSpec as P


HEAD = 128
FIRST = 512
SECOND = 16
LOG2E = 1.4426950408889634
NEG = -1e30
WIDTH = 256
UNROLL = 4
NEAR = 5
ANY = pl.BlockSpec(memory_space=pl.ANY)
VMEM = pl.BlockSpec(memory_space=pltpu.VMEM)
SMEM = pl.BlockSpec(memory_space=pltpu.SMEM)
GRANT = pltpu.CompilerParams(vmem_limit_bytes=20 << 20)
SMALL = pltpu.CompilerParams(vmem_limit_bytes=2 << 20)


def core_swap(value, count):
    return lax.ppermute(value, "ctx", [(s, s ^ 1) for s in range(count)])


def chip_shift(value, count, even, odd):
    pairs = [(s, s + 2 * (even if s % 2 == 0 else odd)) for s in range(count)]
    return lax.ppermute(value, "ctx", [(a, b) for a, b in pairs if b < count])


def head_swap(value):
    return lax.ppermute(value, "head", [(0, 1), (1, 0)])


def pack_kernel(k_ref, v_ref, ks_ref, vs_ref, out_ref, sem):
    rows = k_ref.shape[0]
    tail = pl.ds(rows - SECOND, SECOND)
    parts = (
        (k_ref, out_ref.at[pl.ds(0, rows)]),
        (v_ref, out_ref.at[pl.ds(rows, rows)]),
        (ks_ref.at[tail], out_ref.at[pl.ds(2 * rows, SECOND)]),
        (vs_ref.at[tail], out_ref.at[pl.ds(2 * rows + SECOND, SECOND)]),
    )
    copies = [pltpu.make_async_copy(a, b, sem.at[i]) for i, (a, b) in enumerate(parts)]
    for copy in copies:
        copy.start()
    for copy in copies:
        copy.wait()


def pack(k, v, ks, vs):
    rows, wide = k.shape
    return pl.pallas_call(
        pack_kernel,
        out_shape=jax.ShapeDtypeStruct((2 * rows + 2 * SECOND, wide), k.dtype),
        in_specs=[ANY] * 4,
        out_specs=VMEM,
        scratch_shapes=[pltpu.SemaphoreType.DMA((4,))],
        compiler_params=SMALL,
        name="pack",
    )(k, v, ks, vs)


def join_kernel(own_ref, twin_ref, near_ref, far_ref):
    short = far_ref.shape[0] // 2
    for ref in (near_ref, far_ref):
        ref[0:short] = own_ref[0:short]
        ref[short : 2 * short] = twin_ref[0:short]
    near_ref[2 * short :] = twin_ref[short:]


def join(own, twin):
    tall, wide = own.shape
    short = tall - 2 * SECOND
    return pl.pallas_call(
        join_kernel,
        out_shape=(
            jax.ShapeDtypeStruct((tall + short, wide), own.dtype),
            jax.ShapeDtypeStruct((2 * short, wide), own.dtype),
        ),
        in_specs=[VMEM] * 2,
        out_specs=(VMEM, VMEM),
        compiler_params=SMALL,
        name="join",
    )(own, twin)


def lane_token(lane):
    few = WIDTH // SECOND
    return few * (lane // WIDTH) + lane % few, (lane % WIDTH) // few


def prep_kernel(where_ref, q_hbm, qt_ref, pick_ref, near_bias_ref, far_bias_ref, near_extra_ref, far_extra_ref, q, sem):
    shard = where_ref[0]
    copy = pltpu.make_async_copy(q_hbm, q, sem)
    copy.start()
    rows = q.shape[0]
    shape = pick_ref.shape
    feature = lax.broadcasted_iota(jnp.int32, shape, 0)
    token, offset = lane_token(lax.broadcasted_iota(jnp.int32, shape, 1))
    pick_ref[...] = (feature == token + offset + 1).astype(jnp.bfloat16)
    early = (shard == 0) & (token + offset < SECOND - 1)
    last = jnp.where(feature == rows, 1.0, jnp.where((feature == rows + 1) & early, NEG, 0.0))
    for ref, hidden in ((near_bias_ref, feature > token), (far_bias_ref, feature <= token)):
        ref[...] = jnp.where((feature < rows) & hidden, NEG, last).astype(jnp.bfloat16)
    for ref, first, cut in (
        (near_extra_ref, shard + 1 - near_extra_ref.shape[0] // rows, near_extra_ref.shape[0] - rows),
        (far_extra_ref, shard - FIRST // rows, 0),
    ):
        row = lax.broadcasted_iota(jnp.int32, ref.shape, 0)
        col = lax.broadcasted_iota(jnp.int32, ref.shape, 1)
        gone = jnp.where(first + row // rows < 0, NEG, 0.0)
        extra = jnp.where(col == rows, gone, jnp.where(col == rows + 1, 1.0, 0.0))
        ref[...] = jnp.where((col < rows) & (row - cut == col), 1.0, extra).astype(jnp.bfloat16)
    copy.wait()
    scale = LOG2E / math.sqrt(HEAD)
    few = WIDTH // SECOND
    for h in range(qt_ref.shape[0]):
        part = q[:, h * HEAD : (h + 1) * HEAD].astype(jnp.float32) * scale
        for c in range(qt_ref.shape[1]):
            qt_ref[h, c] = jnp.concatenate([part[c * few : (c + 1) * few]] * (128 // few), axis=0).T


def prep(where, q):
    rows, wide = q.shape
    heads, lanes, chunks = wide // HEAD, SECOND * rows, SECOND * rows // WIDTH
    return pl.pallas_call(
        prep_kernel,
        out_shape=(
            jax.ShapeDtypeStruct((heads, chunks, HEAD, 128), jnp.float32),
            *[jax.ShapeDtypeStruct((HEAD, lanes), jnp.bfloat16)] * 3,
            jax.ShapeDtypeStruct((NEAR * rows, HEAD), jnp.bfloat16),
            jax.ShapeDtypeStruct((FIRST + rows - NEAR * rows, HEAD), jnp.bfloat16),
        ),
        in_specs=[SMEM, ANY],
        out_specs=(VMEM,) * 6,
        scratch_shapes=[pltpu.VMEM(q.shape, q.dtype), pltpu.SemaphoreType.DMA(())],
        compiler_params=GRANT,
        name="prep",
    )(where, q)


def windows(where_ref, ks, vs, x1, y, pick, ksw, svw, rows):
    shard, core = where_ref[0], where_ref[1]
    for own, out, at in ((ks, ksw, 0), (vs, svw, SECOND)):
        near = y[4 * rows + at : 4 * rows + at + SECOND, :]
        twin = x1[2 * rows + at : 2 * rows + at + SECOND, :]
        mine = own[...].astype(jnp.float32)
        tail = jnp.where(core == 1, twin.astype(jnp.float32), near.astype(jnp.float32))
        tail = jnp.where(shard == 0, jnp.zeros_like(tail), tail)
        rest = jnp.zeros((128 - SECOND - rows, mine.shape[1]), jnp.float32)
        tokens = jnp.concatenate([tail, mine, rest], axis=0)
        for g in range(out.shape[0]):
            turned = tokens[:, g * HEAD : (g + 1) * HEAD].T.astype(jnp.bfloat16)
            out[g] = jnp.dot(turned, pick[...], preferred_element_type=jnp.float32)


def stage(kcat, vbuf, vt, extra, start, span):
    window = pl.ds(pl.multiple_of(start, 16), span)
    for g in range(kcat.shape[0]):
        kcat[g, window, HEAD : 2 * HEAD] = extra[...]
        vt[g] = vbuf[window, g * HEAD : (g + 1) * HEAD].T


def run_heads(kcat, start, qt, ksw, svw, bias, vt, sbuf, wbuf, tops, grows, out, peak, norm, before=None):
    kv_heads = ksw.shape[0]
    heads, chunks = qt.shape[:2]
    group = heads // kv_heads
    steps = group * chunks
    window = pl.ds(pl.multiple_of(start, 16), vt.shape[2])
    tiles = [slice(i * 128, (i + 1) * 128) for i in range(WIDTH // 128)]

    def place(step, g):
        step = jnp.minimum(step, steps - 1)
        c = step // group
        return g * group + step % group, c, pl.ds(pl.multiple_of(c * WIDTH, WIDTH), WIDTH)

    def score(step, turn):
        for g in range(kv_heads):
            h, c, at = place(step, g)
            products = jnp.concatenate([qt[h, c]] * len(tiles), axis=1) * ksw[g, :, at]
            products = jnp.concatenate([products.astype(jnp.bfloat16), bias[:, at]], axis=0)
            s = jnp.dot(kcat[g, window, :], products, preferred_element_type=jnp.float32)
            sbuf[turn][g][...] = s
            top = jnp.max(s, axis=0, keepdims=True)
            tops[turn][g][...] = functools.reduce(jnp.maximum, [top[:, t] for t in tiles])

    def soften(step, turn):
        for g in range(kv_heads):
            h, c, _ = place(step, g)
            top = tops[turn][g][...]
            if before is not None:
                top = jnp.maximum(top, before[1][c, pl.ds(h, 1), :])
                grow = jnp.exp2(before[1][c, pl.ds(h, 1), :] - top)
                grows[turn][g][...] = grow
            e = jnp.exp2(sbuf[turn][g][...] - jnp.concatenate([top] * len(tiles), axis=1))
            wbuf[turn][g][...] = e.astype(jnp.bfloat16)
            total = jnp.sum(e, axis=0, keepdims=True)
            total = functools.reduce(jnp.add, [total[:, t] for t in tiles])
            if before is not None:
                total = total + before[2][c, pl.ds(h, 1), :] * grow
            peak[c, pl.ds(h, 1), :] = top
            norm[c, pl.ds(h, 1), :] = total

    def mix(step, turn):
        for g in range(kv_heads):
            h, c, at = place(step, g)
            mixed = jnp.dot(vt[g], wbuf[turn][g][...], preferred_element_type=jnp.float32)
            mixed = mixed * svw[g, :, at]
            sums = functools.reduce(jnp.add, [mixed[:, t] for t in tiles])
            if before is not None:
                sums = sums + before[0][h, c] * grows[turn][g][...]
            out[h, c] = sums

    def several(i, _):
        for turn in range(UNROLL):
            step = UNROLL * i + turn
            mix(step, turn % 2)
            soften(step + 1, (turn + 1) % 2)
            score(step + 2, turn % 2)
        return 0

    score(0, 0)
    score(1, 1)
    soften(0, 0)
    lax.fori_loop(0, steps // UNROLL, several, 0)


def start_all(pairs, sem):
    copies = [pltpu.make_async_copy(a, b, sem.at[i]) for i, (a, b) in enumerate(pairs)]
    for copy in copies:
        copy.start()
    return copies


def block_copies(ref, row, rows, block, kcat, vbuf):
    at = pl.ds(pl.multiple_of(block * rows, rows), rows)
    keys = ref.at[pl.ds(row, rows)]
    pairs = [(keys.at[:, pl.ds(g * HEAD, HEAD)], kcat.at[g, at, pl.ds(0, HEAD)]) for g in range(kcat.shape[0])]
    return pairs + [(ref.at[pl.ds(row + rows, rows)], vbuf.at[at])]


def chip_blocks(ref, rows, pair, flip, kcat, vbuf):
    pairs = []
    for slot in range(2):
        block = 2 * pair + jnp.where(flip == 1, 1 - slot, slot)
        pairs += block_copies(ref, slot * 2 * rows, rows, block, kcat, vbuf)
    return pairs


def near_kernel(
    where_ref, x0_hbm, ks_hbm, vs_hbm, x1_hbm, y_hbm, yp_hbm, qt, pick, bias, extra,
    out_ref, peak_ref, norm_ref, ksw, svw,
    ks, vs, x1, y, kcat, vbuf, vt, sbuf, wbuf, tops, grows, sem,
):
    core = where_ref[1]
    rows = ks.shape[0]
    blocks = vbuf.shape[0] // rows
    pairs = [(ks_hbm, ks), (vs_hbm, vs), (x1_hbm, x1), (y_hbm, y)]
    pairs += block_copies(x0_hbm, 0, rows, blocks - 2 + core, kcat, vbuf)
    pairs += block_copies(x1_hbm, 0, rows, blocks - 1 - core, kcat, vbuf)
    pairs += chip_blocks(y_hbm, rows, 1 - core, core, kcat, vbuf)
    pairs += chip_blocks(yp_hbm, rows, core, 1 - core, kcat, vbuf)
    for copy in start_all(pairs, sem):
        copy.wait()
    windows(where_ref, ks, vs, x1, y, pick, ksw, svw, rows)
    stage(kcat, vbuf, vt, extra, core * rows, NEAR * rows)
    run_heads(kcat, core * rows, qt, ksw, svw, bias, vt, sbuf, wbuf, tops, grows, out_ref, peak_ref, norm_ref)


def far_kernel(
    where_ref, y_hbm, z_hbm, zp_hbm, acc1_ref, peak1_ref, norm1_ref, ksw, svw, qt, bias, extra, w_hbm,
    other_ref, att,
    kcat, vbuf, vt, sbuf, wbuf, tops, grows, out, peak, norm, weight, sem, wsem,
):
    core, side = where_ref[1], where_ref[2]
    rows = att.shape[0]
    half = w_hbm.shape[1] // 2
    blocks = vbuf.shape[0] // rows
    pairs = chip_blocks(z_hbm, rows, 1 - core, core, kcat, vbuf)
    pairs += chip_blocks(zp_hbm, rows, core, 1 - core, kcat, vbuf)
    pairs += block_copies(y_hbm, 2 * rows, rows, blocks - 1, kcat, vbuf)
    copies = start_all(pairs, sem)
    cols = pl.ds(pl.multiple_of((1 - side) * half, 128), half)
    fetch = pltpu.make_async_copy(w_hbm.at[:, cols], weight, wsem)
    fetch.start()
    for copy in copies:
        copy.wait()
    stage(kcat, vbuf, vt, extra, core * rows, (blocks - 1) * rows)
    run_heads(
        kcat, core * rows, qt, ksw, svw, bias, vt, sbuf, wbuf, tops, grows, out, peak, norm, (acc1_ref, peak1_ref, norm1_ref)
    )
    heads, chunks = qt.shape[:2]
    few = WIDTH // SECOND
    shifts = [few << i for i in range((128 // few).bit_length() - 1)]
    for c in range(chunks):
        top = peak[c]
        most = top
        for shift in shifts:
            most = jnp.maximum(most, pltpu.roll(most, shift, 1))
        grow = jnp.exp2(top - most)
        total = norm[c] * grow
        for shift in shifts:
            total = total + pltpu.roll(total, shift, 1)
        grow = grow / total
        for h in range(heads):
            part = (out[h, c] * grow[h : h + 1]).T
            part = functools.reduce(jnp.add, [part[i : i + few] for i in range(0, 128, few)])
            att[c * few : (c + 1) * few, h * HEAD : (h + 1) * HEAD] = part.astype(jnp.bfloat16)
    fetch.wait()
    other_ref[...] = jnp.dot(att[...], weight[...], preferred_element_type=jnp.float32).astype(jnp.bfloat16)


def own_kernel(where_ref, att, w_hbm, mine_ref, weight, sem):
    half = w_hbm.shape[1] // 2
    cols = pl.ds(pl.multiple_of(where_ref[2] * half, 128), half)
    fetch = pltpu.make_async_copy(w_hbm.at[:, cols], weight, sem)
    fetch.start()
    fetch.wait()
    mine_ref[...] = jnp.dot(att[...], weight[...], preferred_element_type=jnp.float32)


def common_scratch(rows, kv_heads, blocks, span):
    def twice(shape, dtype):
        return [[pltpu.VMEM(shape, dtype)] * kv_heads] * 2

    return [
        pltpu.VMEM((kv_heads, blocks * rows, 2 * HEAD), jnp.bfloat16),
        pltpu.VMEM((blocks * rows, kv_heads * HEAD), jnp.bfloat16),
        pltpu.VMEM((kv_heads, HEAD, span), jnp.bfloat16),
        twice((span, WIDTH), jnp.float32),
        twice((span, WIDTH), jnp.bfloat16),
        twice((1, 128), jnp.float32),
        twice((1, 128), jnp.float32),
    ]


def sums_like(qt):
    heads, chunks = qt.shape[:2]
    return [
        jax.ShapeDtypeStruct((heads, chunks, HEAD, 128), jnp.float32),
        *[jax.ShapeDtypeStruct((chunks, heads, 128), jnp.float32)] * 2,
    ]


def attend_near(where, x0, ks, vs, x1, y, yp, qt, pick, bias, extra):
    rows, lanes = ks.shape[0], pick.shape[1]
    kv_heads = ks.shape[1] // HEAD
    return pl.pallas_call(
        near_kernel,
        out_shape=(*sums_like(qt), *[jax.ShapeDtypeStruct((kv_heads, HEAD, lanes), jnp.float32)] * 2),
        in_specs=[SMEM] + [ANY] * 6 + [VMEM] * 4,
        out_specs=(VMEM,) * 5,
        scratch_shapes=[pltpu.VMEM(a.shape, a.dtype) for a in (ks, vs, x1, y)]
        + common_scratch(rows, kv_heads, NEAR + 1, NEAR * rows)
        + [pltpu.SemaphoreType.DMA((22,))],
        compiler_params=GRANT,
        name="near",
    )(where, x0, ks, vs, x1, y, yp, qt, pick, bias, extra)


def attend_far(where, y, z, zp, acc1, peak1, norm1, ksw, svw, qt, bias, extra, w):
    kv_heads, (heads, chunks) = ksw.shape[0], qt.shape[:2]
    rows = ksw.shape[2] // SECOND
    depth, features = w.shape
    span = extra.shape[0]
    return pl.pallas_call(
        far_kernel,
        out_shape=(
            jax.ShapeDtypeStruct((rows, features // 2), jnp.bfloat16),
            jax.ShapeDtypeStruct((rows, heads * HEAD), jnp.bfloat16),
        ),
        in_specs=[SMEM] + [ANY] * 3 + [VMEM] * 8 + [ANY],
        out_specs=(VMEM, VMEM),
        scratch_shapes=common_scratch(rows, kv_heads, span // rows + 1, span)
        + [
            *(pltpu.VMEM(a.shape, a.dtype) for a in (acc1, peak1, norm1)),
            pltpu.VMEM((depth, features // 2), jnp.bfloat16),
            pltpu.SemaphoreType.DMA((15,)),
            pltpu.SemaphoreType.DMA(()),
        ],
        compiler_params=GRANT,
        name="far",
    )(where, y, z, zp, acc1, peak1, norm1, ksw, svw, qt, bias, extra, w)


def project_own(where, att, w):
    rows, (depth, features) = att.shape[0], w.shape
    return pl.pallas_call(
        own_kernel,
        out_shape=jax.ShapeDtypeStruct((rows, features // 2), jnp.float32),
        in_specs=[SMEM, VMEM, ANY],
        out_specs=VMEM,
        scratch_shapes=[pltpu.VMEM((depth, features // 2), jnp.bfloat16), pltpu.SemaphoreType.DMA(())],
        compiler_params=GRANT,
        name="own",
    )(where, att, w)


def body(queries, keys_first, primary_value_array, keys_second, secondary_value_array, out_weight):
    count = lax.axis_size("ctx")
    queries, keys_first, primary_value_array, keys_second, secondary_value_array, out_weight = (
        pltpu.with_memory_space_constraint(a, pltpu.HBM)
        for a in (queries, keys_first, primary_value_array, keys_second, secondary_value_array, out_weight)
    )
    shard = lax.axis_index("ctx")
    where = jnp.stack([shard, shard % 2, lax.axis_index("head")]).astype(jnp.int32)
    packed = pack(keys_first, primary_value_array, keys_second, secondary_value_array)
    twin = core_swap(packed, count)
    near_load, far_load = join(packed, twin)
    near = chip_shift(near_load, count, 1, 2)
    far = chip_shift(far_load, count, 3, 4)
    qt, pick, near_bias, far_bias, near_extra, far_extra = prep(where, queries)
    near_twin = core_swap(near, count)
    sums = attend_near(
        where, packed, keys_second, secondary_value_array, twin, near, near_twin, qt, pick, near_bias, near_extra
    )
    far_twin = core_swap(far, count)
    other, attention = attend_far(where, near, far, far_twin, *sums, qt, far_bias, far_extra, out_weight)
    other = head_swap(other)
    mine = project_own(where, attention, out_weight)
    return (mine + other.astype(jnp.float32)).astype(jnp.bfloat16)


def solution(mesh):
    in_specs = (P("ctx", "head"),) * 5 + (P("head", None),)
    return jax.shard_map(body, mesh=mesh, in_specs=in_specs, out_specs=P("ctx", "head"), check_vma=False)
```

time: 60.7 us -> 51.2 us (0.84)
  waiting for transfers between devices: 31.2 us -> 15.7 us
  starting transfers between devices: 10.9 us -> 14.6 us
  Pallas kernels: 17.5 us -> 19.6 us
    ppermute x2, waiting for transfers between devices: 22.9 us -> 10.7 us  [chip_shift(): return lax.ppermute(value, 'ctx', [(a, b) for a, b in pairs if b < count])]
    ppermute x2, starting transfers between devices: 6.22 us -> 11.6 us  [chip_shift(): return lax.ppermute(value, 'ctx', [(a, b) for a, b in pairs if b < count])]
    pallas_call x2 -> x4, Pallas kernels: 7.97 us -> 12 us  [the longest x1 6.31 us: attend_near(): pl.pallas_call(near_kernel, out_shape=(*sums_like(qt), *[jax.ShapeDtypeSt...]
    ppermute x1, waiting for transfers between devices: 7 us -> 3.77 us  [head_swap(): return lax.ppermute(value, 'head', [(0, 1), (1, 0)])]
    pallas_call x1, Pallas kernels: 8.68 us -> 6.87 us  [attend_far(): pl.pallas_call(far_kernel, out_shape=(jax.ShapeDtypeStruct((rows, feature...]
    ppermute x3, starting transfers between devices: 1.89 us -> 0.1 us  [core_swap(): return lax.ppermute(value, 'ctx', [(s, s ^ 1) for s in range(count)])]
  transfers between devices with their start and end apart: 6 -> 6, of which waited for: 4 -> 4; matrix products, arithmetic and copies ran while one was open for 0% -> 0% of each run, Pallas kernels for 13% -> 23%
where the time goes in v3:
time: 51.2 us; the launch traced here: 50.9 us
  Pallas kernels  19.6 us (38%)
  waiting for transfers between devices  15.7 us (31%)
  starting transfers between devices  14.6 us (29%)
  other arithmetic  0.84 us (2%)
    ppermute x2, starting transfers between devices, chip_shift(): return lax.ppermute(value, 'ctx', [(a, b) for a, b in pairs if b < count])  11.6 us
    ppermute x2, waiting for transfers between devices, chip_shift(): return lax.ppermute(value, 'ctx', [(a, b) for a, b in pairs if b < count])  10.7 us
    pallas_call x1, Pallas kernels, attend_far(): pl.pallas_call(far_kernel, out_shape=(jax.ShapeDtypeStruct((rows, feature...  6.87 us
    pallas_call x1, Pallas kernels, attend_near(): pl.pallas_call(near_kernel, out_shape=(*sums_like(qt), *[jax.ShapeDtypeSt...  6.31 us
    ppermute x1, waiting for transfers between devices, head_swap(): return lax.ppermute(value, 'head', [(0, 1), (1, 0)])  3.77 us
    pallas_call x1, Pallas kernels, project_own(): pl.pallas_call(own_kernel, out_shape=jax.ShapeDtypeStruct((rows, features...  3.58 us
    ppermute x1, starting transfers between devices, head_swap(): return lax.ppermute(value, 'head', [(0, 1), (1, 0)])  2.94 us
    pallas_call x1, Pallas kernels, prep(): pl.pallas_call(prep_kernel, out_shape=(jax.ShapeDtypeStruct((heads, chunk...  2.06 us
  transfers between devices with their start and end apart: 6, of which 4 were waited for; matrix products, arithmetic and copies ran while one was open for 0% of the time, Pallas kernels for 23%

profile of v3, /device:TPU:24, one launch (start us, length us, event | category | flops | bytes accessed | tf_op | source)
XLA Modules:
  0.0 50.9 jit_solution(12122243770044523929)
XLA Ops:
  0.0 0.8 %pack.1.own_ref.x0_hbm = bf16[160,256]{1,0:T(8,128)(2,1)S(1)} custom-call(bf16[64,256]{1,0:T(8,128)(2,1)} %k_ref.1, bf16[64,256]{1,0:T(8,128)(2,1)} %v_ref.1, bf16[64,256]{1,0:T(8,128)(2,1)} %ks_hbm.1, bf16[64,256]{1,0:T(8,128)(2,1)} %vs_hbm.1), custom_call_target="tpu_custom_call" | custom-call | tf_op jit(solution)/shard_map/pack/pallas_call | solution.py:58
  0.8 0.1 collective-permute-start
  0.9 1.3 %collective-permute-done.twin_ref.x1_hbm = bf16[160,256]{1,0:T(8,128)(2,1)S(1)} collective-permute-done((bf16[160,256]{1,0:T(8,128)(2,1)S(1)}, bf16[160,256]{1,0:T(8,128)(2,1)S(1)}, u32[]{:S(2)}, u32[]{:S(2)}) %collective-permute-start) | collective-permute-done | bytes 81952 | tf_op jit(solution)/shard_map/ppermute | solution.py:28
  2.2 3.8 %collective-permute-start.1 = (bf16[288,256]{1,0:T(8,128)(2,1)S(1)}, bf16[288,256]{1,0:T(8,128)(2,1)S(1)}, u32[]{:S(2)}, u32[]{:S(2)}) collective-permute-start(bf16[288,256]{1,0:T(8,128)(2,1)S(1)} %get-tuple-element.20), channel_id=1, source_target_pairs={{0,4},{2,10},{4,8},{6,14},{8,12},{10,18},{12,16},{14,22},{16,20},{... | collective-permute-start | bytes 442376 | tf_op jit(solution)/shard_map/ppermute | solution.py:33
  6.0 7.7 %collective-permute-start.2 = (bf16[256,256]{1,0:T(8,128)(2,1)S(1)}, bf16[256,256]{1,0:T(8,128)(2,1)S(1)}, u32[]{:S(2)}, u32[]{:S(2)}) collective-permute-start(bf16[256,256]{1,0:T(8,128)(2,1)S(1)} %get-tuple-element.21), channel_id=1, source_target_pairs={{0,12},{2,18},{4,16},{6,22},{8,20},{10,26},{12,24},{14,30},{16,28}... | collective-permute-start | bytes 393224 | tf_op jit(solution)/shard_map/ppermute | solution.py:33
  13.8 3.1 %collective-permute-done.1.y_hbm = bf16[288,256]{1,0:T(8,128)(2,1)S(1)} collective-permute-done((bf16[288,256]{1,0:T(8,128)(2,1)S(1)}, bf16[288,256]{1,0:T(8,128)(2,1)S(1)}, u32[]{:S(2)}, u32[]{:S(2)}) %collective-permute-start.1) | collective-permute-done | bytes 147488 | tf_op jit(solution)/shard_map/ppermute | solution.py:33
  16.8 0.0 collective-permute-start.4
  16.9 7.6 %collective-permute-done.2.z_hbm = bf16[256,256]{1,0:T(8,128)(2,1)S(1)} collective-permute-done((bf16[256,256]{1,0:T(8,128)(2,1)S(1)}, bf16[256,256]{1,0:T(8,128)(2,1)S(1)}, u32[]{:S(2)}, u32[]{:S(2)}) %collective-permute-start.2) | collective-permute-done | bytes 131104 | tf_op jit(solution)/shard_map/ppermute | solution.py:33
  24.5 0.0 collective-permute-start.3
  24.5 0.1 pad_add_fusion.where_ref
  24.6 2.1 %prep.1 = (f32[8,4,128,128]{3,2,1,0:T(8,128)S(1)}, bf16[128,1024]{1,0:T(8,128)(2,1)S(1)}, bf16[128,1024]{1,0:T(8,128)(2,1)S(1)}, bf16[128,1024]{1,0:T(8,128)(2,1...) custom-call(s32[3]{0:T(128)S(1)} %pad_add_fusion.where_ref, bf16[64,1024]{1,0:T(8,128)(2,1)} %q_hbm.1), custom_call_target="tpu_custom_call" | custom-call | tf_op jit(solution)/shard_map/prep/pallas_call | solution.py:132
  26.6 0.0 collective-permute-done.4.yp_hbm
  26.6 6.3 %near.1 = (f32[8,4,128,128]{3,2,1,0:T(8,128)S(1)}, f32[4,8,128]{2,1,0:T(8,128)S(1)}, f32[4,8,128]{2,1,0:T(8,128)S(1)}, f32[2,128,1024]{2,1,0:T(8,128)S(1)}, f32[2,128,1024]{2,1,0:T(8,128)S(1)}) custom-call(s32[3]{0:T(128)S(1)} %pad_add_fusion.where_ref, bf16[160,256]{1,0:T(8,128)(2,1)S(1)} %pack.1.own_ref.x0_hbm, bf16[64,256]{1,0:T(8,128)(2,1)} %ks_hbm.1, ...), custom_call_target="tpu_custom_call" | custom-call | tf_op jit(solution)/shard_map/near/pallas_call | solution.py:354
  33.0 0.0 collective-permute-done.3.zp_hbm
  33.0 6.9 %far.1 = (bf16[64,2048]{1,0:T(8,128)(2,1)S(1)}, bf16[64,1024]{1,0:T(8,128)(2,1)S(1)}) custom-call(s32[3]{0:T(128)S(1)} %pad_add_fusion.where_ref, bf16[288,256]{1,0:T(8,128)(2,1)S(1)} %collective-permute-done.1.y_hbm, bf16[256,256]{1,0:T(8,128)(2,1)S(1)} %collective-permute-done.2.z_hbm, bf16[256,256]{1,0:T(8,128)(2,1)S(1)} %collective-permute-done.3.zp_hbm, ...), custom_call_target="tpu_custom_call" | custom-call | tf_op jit(solution)/shard_map/far/pallas_call | solution.py:372
  39.8 2.9 %collective-permute-start.5 = (bf16[64,2048]{1,0:T(8,128)(2,1)S(1)}, bf16[64,2048]{1,0:T(8,128)(2,1)S(1)}, u32[]{:S(2)}, u32[]{:S(2)}) collective-permute-start(bf16[64,2048]{1,0:T(8,128)(2,1)S(1)} %get-tuple-element.34), channel_id=1, source_target_pairs={{0,1},{1,0},{2,3},{3,2},{4,5},{5,4},{6,7},{7,6},{8,9},{9,8},{10,11... | collective-permute-start | bytes 786440 | tf_op jit(solution)/shard_map/ppermute | solution.py:37
  42.8 3.6 %own.1 = f32[64,2048]{1,0:T(8,128)S(1)} custom-call(s32[3]{0:T(128)S(1)} %pad_add_fusion.where_ref, bf16[64,1024]{1,0:T(8,128)(2,1)S(1)} %get-tuple-element.33.att, bf16[1024,4096]{1,0:T(8,128)(2,1)} %w_hbm.3), custom_call_target="tpu_custom_call" | custom-call | tf_op jit(solution)/shard_map/own/pallas_call | solution.py:394
  46.4 3.8 %collective-permute-done.5 = bf16[64,2048]{1,0:T(8,128)(2,1)S(1)} collective-permute-done((bf16[64,2048]{1,0:T(8,128)(2,1)S(1)}, bf16[64,2048]{1,0:T(8,128)(2,1)S(1)}, u32[]{:S(2)}, u32[]{:S(2)}) %collective-permute-start.5) | collective-permute-done | bytes 262176 | tf_op jit(solution)/shard_map/ppermute | solution.py:37
  50.1 0.8 %add_convert_fusion = bf16[64,2048]{1,0:T(8,128)(2,1)} fusion(f32[64,2048]{1,0:T(8,128)S(1)} %own.1, bf16[64,2048]{1,0:T(8,128)(2,1)S(1)} %collective-permute-done.5), kind=kLoop, calls=%fused_computation | loop fusion | flops 393216 | bytes 1048576 | tf_op jit(solution)/shard_map/convert_element_type | solution.py:427
  (1 shorter events, 0.0 us)
Async XLA Ops:
  0.8 1.4 %collective-permute-start = (bf16[160,256]{1,0:T(8,128)(2,1)S(1)}, bf16[160,256]{1,0:T(8,128)(2,1)S(1)}, u32[]{:S(2)}, u32[]{:S(2)}) collective-permute-start(bf16[160,256]{1,0:T(8,128)(2,1)S(1)} %pack.1.own_ref.x0_hbm), channel_id=1, source_target_pairs={{0,2},{2,0},{4,6},{6,4},{8,10},{10,8},{12,14},{14,12},{16,18},{18,... | collective-permute-start | bytes 245768 | tf_op jit(solution)/shard_map/ppermute | solution.py:28
  2.2 14.6 %collective-permute-start.1 = (bf16[288,256]{1,0:T(8,128)(2,1)S(1)}, bf16[288,256]{1,0:T(8,128)(2,1)S(1)}, u32[]{:S(2)}, u32[]{:S(2)}) collective-permute-start(bf16[288,256]{1,0:T(8,128)(2,1)S(1)} %get-tuple-element.20), channel_id=1, source_target_pairs={{0,4},{2,10},{4,8},{6,14},{8,12},{10,18},{12,16},{14,22},{16,20},{... | collective-permute-start | bytes 442376 | tf_op jit(solution)/shard_map/ppermute | solution.py:33
  6.0 18.4 %collective-permute-start.2 = (bf16[256,256]{1,0:T(8,128)(2,1)S(1)}, bf16[256,256]{1,0:T(8,128)(2,1)S(1)}, u32[]{:S(2)}, u32[]{:S(2)}) collective-permute-start(bf16[256,256]{1,0:T(8,128)(2,1)S(1)} %get-tuple-element.21), channel_id=1, source_target_pairs={{0,12},{2,18},{4,16},{6,22},{8,20},{10,26},{12,24},{14,30},{16,28}... | collective-permute-start | bytes 393224 | tf_op jit(solution)/shard_map/ppermute | solution.py:33
  16.8 9.8 %collective-permute-start.4 = (bf16[288,256]{1,0:T(8,128)(2,1)S(1)}, bf16[288,256]{1,0:T(8,128)(2,1)S(1)}, u32[]{:S(2)}, u32[]{:S(2)}) collective-permute-start(bf16[288,256]{1,0:T(8,128)(2,1)S(1)} %collective-permute-done.1.y_hbm), channel_id=1, source_target_pairs={{0,2},{2,0},{4,6},{6,4},{8,10},{10,8},{12,14},{14,12},{16,18},{18,... | collective-permute-start | bytes 442376 | tf_op jit(solution)/shard_map/ppermute | solution.py:28
  24.5 8.5 %collective-permute-start.3 = (bf16[256,256]{1,0:T(8,128)(2,1)S(1)}, bf16[256,256]{1,0:T(8,128)(2,1)S(1)}, u32[]{:S(2)}, u32[]{:S(2)}) collective-permute-start(bf16[256,256]{1,0:T(8,128)(2,1)S(1)} %collective-permute-done.2.z_hbm), channel_id=1, source_target_pairs={{0,2},{2,0},{4,6},{6,4},{8,10},{10,8},{12,14},{14,12},{16,18},{18,... | collective-permute-start | bytes 393224 | tf_op jit(solution)/shard_map/ppermute | solution.py:28
  39.8 10.3 %collective-permute-start.5 = (bf16[64,2048]{1,0:T(8,128)(2,1)S(1)}, bf16[64,2048]{1,0:T(8,128)(2,1)S(1)}, u32[]{:S(2)}, u32[]{:S(2)}) collective-permute-start(bf16[64,2048]{1,0:T(8,128)(2,1)S(1)} %get-tuple-element.34), channel_id=1, source_target_pairs={{0,1},{1,0},{2,3},{3,2},{4,5},{5,4},{6,7},{7,6},{8,9},{9,8},{10,11... | collective-permute-start | bytes 786440 | tf_op jit(solution)/shard_map/ppermute | solution.py:37

commit v4 on v3

--- a/solution.py
+++ b/solution.py
@@ -16,6 +16,7 @@
 NEG = -1e30
 WIDTH = 256
 UNROLL = 4
+FAR = 3
 NEAR = 5
 ANY = pl.BlockSpec(memory_space=pl.ANY)
 VMEM = pl.BlockSpec(memory_space=pltpu.VMEM)
@@ -167,17 +168,17 @@
         vt[g] = vbuf[window, g * HEAD : (g + 1) * HEAD].T
 
 
-def run_heads(kcat, start, qt, ksw, svw, bias, vt, sbuf, wbuf, tops, grows, out, peak, norm, before=None):
+def run_heads(kcat, start, qt, ksw, svw, bias, vt, sbuf, wbuf, tops, grows, out, peak, norm, span, first=0, before=None):
     kv_heads = ksw.shape[0]
-    heads, chunks = qt.shape[:2]
+    heads, chunks = out.shape[:2]
     group = heads // kv_heads
     steps = group * chunks
-    window = pl.ds(pl.multiple_of(start, 16), vt.shape[2])
+    window = pl.ds(pl.multiple_of(start, 16), span)
     tiles = [slice(i * 128, (i + 1) * 128) for i in range(WIDTH // 128)]
 
     def place(step, g):
         step = jnp.minimum(step, steps - 1)
-        c = step // group
+        c = first + step // group
         return g * group + step % group, c, pl.ds(pl.multiple_of(c * WIDTH, WIDTH), WIDTH)
 
     def score(step, turn):
@@ -204,8 +205,8 @@
             total = functools.reduce(jnp.add, [total[:, t] for t in tiles])
             if before is not None:
                 total = total + before[2][c, pl.ds(h, 1), :] * grow
-            peak[c, pl.ds(h, 1), :] = top
-            norm[c, pl.ds(h, 1), :] = total
+            peak[c - first, pl.ds(h, 1), :] = top
+            norm[c - first, pl.ds(h, 1), :] = total
 
     def mix(step, turn):
         for g in range(kv_heads):
@@ -215,7 +216,7 @@
             sums = functools.reduce(jnp.add, [mixed[:, t] for t in tiles])
             if before is not None:
                 sums = sums + before[0][h, c] * grows[turn][g][...]
-            out[h, c] = sums
+            out[h, c - first] = sums
 
     def several(i, _):
         for turn in range(UNROLL):
@@ -270,32 +271,11 @@
         copy.wait()
     windows(where_ref, ks, vs, x1, y, pick, ksw, svw, rows)
     stage(kcat, vbuf, vt, extra, core * rows, NEAR * rows)
-    run_heads(kcat, core * rows, qt, ksw, svw, bias, vt, sbuf, wbuf, tops, grows, out_ref, peak_ref, norm_ref)
-
-
-def far_kernel(
-    where_ref, y_hbm, z_hbm, zp_hbm, acc1_ref, peak1_ref, norm1_ref, ksw, svw, qt, bias, extra, w_hbm,
-    other_ref, att,
-    kcat, vbuf, vt, sbuf, wbuf, tops, grows, out, peak, norm, weight, sem, wsem,
-):
-    core, side = where_ref[1], where_ref[2]
-    rows = att.shape[0]
-    half = w_hbm.shape[1] // 2
-    blocks = vbuf.shape[0] // rows
-    pairs = chip_blocks(z_hbm, rows, 1 - core, core, kcat, vbuf)
-    pairs += chip_blocks(zp_hbm, rows, core, 1 - core, kcat, vbuf)
-    pairs += block_copies(y_hbm, 2 * rows, rows, blocks - 1, kcat, vbuf)
-    copies = start_all(pairs, sem)
-    cols = pl.ds(pl.multiple_of((1 - side) * half, 128), half)
-    fetch = pltpu.make_async_copy(w_hbm.at[:, cols], weight, wsem)
-    fetch.start()
-    for copy in copies:
-        copy.wait()
-    stage(kcat, vbuf, vt, extra, core * rows, (blocks - 1) * rows)
-    run_heads(
-        kcat, core * rows, qt, ksw, svw, bias, vt, sbuf, wbuf, tops, grows, out, peak, norm, (acc1_ref, peak1_ref, norm1_ref)
-    )
-    heads, chunks = qt.shape[:2]
+    run_heads(kcat, core * rows, qt, ksw, svw, bias, vt, sbuf, wbuf, tops, grows, out_ref, peak_ref, norm_ref, NEAR * rows)
+
+
+def finish_heads(out, peak, norm, att):
+    heads, chunks = out.shape[:2]
     few = WIDTH // SECOND
     shifts = [few << i for i in range((128 // few).bit_length() - 1)]
     for c in range(chunks):
@@ -312,27 +292,68 @@
             part = (out[h, c] * grow[h : h + 1]).T
             part = functools.reduce(jnp.add, [part[i : i + few] for i in range(0, 128, few)])
             att[c * few : (c + 1) * few, h * HEAD : (h + 1) * HEAD] = part.astype(jnp.bfloat16)
-    fetch.wait()
+
+
+def far_kernel(
+    where_ref, y_hbm, z_hbm, zp_hbm, acc1_ref, peak1_ref, norm1_ref, ksw, svw, qt, bias, extra, w_hbm,
+    other_ref, att, kcat, vt, weight, own_weight,
+    vbuf, sbuf, wbuf, tops, grows, out, peak, norm, sem, wsem,
+):
+    core, side = where_ref[1], where_ref[2]
+    span = extra.shape[0]
+    rows = vbuf.shape[0] - span
+    half = w_hbm.shape[1] // 2
+    blocks = vbuf.shape[0] // rows
+    pairs = chip_blocks(z_hbm, rows, 1 - core, core, kcat, vbuf)
+    pairs += chip_blocks(zp_hbm, rows, core, 1 - core, kcat, vbuf)
+    pairs += block_copies(y_hbm, 2 * rows, rows, blocks - 1, kcat, vbuf)
+    copies = start_all(pairs, sem)
+    fetches = []
+    for i, (which, to) in enumerate(((1 - side, weight), (side, own_weight))):
+        cols = pl.ds(pl.multiple_of(which * half, 128), half)
+        fetches.append(pltpu.make_async_copy(w_hbm.at[:, cols], to, wsem.at[i]))
+        fetches[-1].start()
+    for copy in copies:
+        copy.wait()
+    stage(kcat, vbuf, vt, extra, core * rows, span)
+    before = (acc1_ref, peak1_ref, norm1_ref)
+    run_heads(kcat, core * rows, qt, ksw, svw, bias, vt, sbuf, wbuf, tops, grows, out, peak, norm, span, 0, before)
+    finish_heads(out, peak, norm, att)
+    fetches[0].wait()
     other_ref[...] = jnp.dot(att[...], weight[...], preferred_element_type=jnp.float32).astype(jnp.bfloat16)
-
-
-def own_kernel(where_ref, att, w_hbm, mine_ref, weight, sem):
-    half = w_hbm.shape[1] // 2
-    cols = pl.ds(pl.multiple_of(where_ref[2] * half, 128), half)
-    fetch = pltpu.make_async_copy(w_hbm.at[:, cols], weight, sem)
-    fetch.start()
-    fetch.wait()
-    mine_ref[...] = jnp.dot(att[...], weight[...], preferred_element_type=jnp.float32)
-
-
-def common_scratch(rows, kv_heads, blocks, span):
+    fetches[1].wait()
+
+
+def rest_kernel(
+    where_ref, kcat, vt, acc1_ref, peak1_ref, norm1_ref, ksw, svw, qt, bias, weight,
+    other_ref, att,
+    sbuf, wbuf, tops, grows, out, peak, norm,
+):
+    core = where_ref[1]
+    span = vt.shape[2]
+    rows = kcat.shape[1] - span
+    before = (acc1_ref, peak1_ref, norm1_ref)
+    run_heads(kcat, core * rows, qt, ksw, svw, bias, vt, sbuf, wbuf, tops, grows, out, peak, norm, span, FAR, before)
+    finish_heads(out, peak, norm, att)
+    other_ref[...] = jnp.dot(att[...], weight[...], preferred_element_type=jnp.float32).astype(jnp.bfloat16)
+
+
+def own_kernel(att, rest, weight, mine_ref):
+    both = jnp.concatenate([att[...], rest[...]], axis=0)
+    mine_ref[...] = jnp.dot(both, weight[...], preferred_element_type=jnp.float32)
+
+
+def add_kernel(mine_ref, far_ref, rest_ref, out_ref):
+    tall = far_ref.shape[0]
+    out_ref[:tall] = (mine_ref[:tall] + far_ref[...].astype(jnp.float32)).astype(out_ref.dtype)
+    out_ref[tall:] = (mine_ref[tall:] + rest_ref[...].astype(jnp.float32)).astype(out_ref.dtype)
+
+
+def step_scratch(kv_heads, span):
     def twice(shape, dtype):
         return [[pltpu.VMEM(shape, dtype)] * kv_heads] * 2
 
     return [
-        pltpu.VMEM((kv_heads, blocks * rows, 2 * HEAD), jnp.bfloat16),
-        pltpu.VMEM((blocks * rows, kv_heads * HEAD), jnp.bfloat16),
-        pltpu.VMEM((kv_heads, HEAD, span), jnp.bfloat16),
         twice((span, WIDTH), jnp.float32),
         twice((span, WIDTH), jnp.bfloat16),
         twice((1, 128), jnp.float32),
@@ -340,24 +361,32 @@
     ]
 
 
-def sums_like(qt):
-    heads, chunks = qt.shape[:2]
+def sums_like(heads, chunks):
     return [
         jax.ShapeDtypeStruct((heads, chunks, HEAD, 128), jnp.float32),
         *[jax.ShapeDtypeStruct((chunks, heads, 128), jnp.float32)] * 2,
     ]
 
 
+def vmem_like(shapes):
+    return [pltpu.VMEM(a.shape, a.dtype) for a in shapes]
+
+
 def attend_near(where, x0, ks, vs, x1, y, yp, qt, pick, bias, extra):
     rows, lanes = ks.shape[0], pick.shape[1]
     kv_heads = ks.shape[1] // HEAD
     return pl.pallas_call(
         near_kernel,
-        out_shape=(*sums_like(qt), *[jax.ShapeDtypeStruct((kv_heads, HEAD, lanes), jnp.float32)] * 2),
+        out_shape=(*sums_like(*qt.shape[:2]), *[jax.ShapeDtypeStruct((kv_heads, HEAD, lanes), jnp.float32)] * 2),
         in_specs=[SMEM] + [ANY] * 6 + [VMEM] * 4,
         out_specs=(VMEM,) * 5,
         scratch_shapes=[pltpu.VMEM(a.shape, a.dtype) for a in (ks, vs, x1, y)]
-        + common_scratch(rows, kv_heads, NEAR + 1, NEAR * rows)
+        + [
+            pltpu.VMEM((kv_heads, (NEAR + 1) * rows, 2 * HEAD), jnp.bfloat16),
+            pltpu.VMEM(((NEAR + 1) * rows, kv_heads * HEAD), jnp.bfloat16),
+            pltpu.VMEM((kv_heads, HEAD, NEAR * rows), jnp.bfloat16),
+        ]
+        + step_scratch(kv_heads, NEAR * rows)
         + [pltpu.SemaphoreType.DMA((22,))],
         compiler_params=GRANT,
         name="near",
@@ -365,41 +394,50 @@
 
 
 def attend_far(where, y, z, zp, acc1, peak1, norm1, ksw, svw, qt, bias, extra, w):
-    kv_heads, (heads, chunks) = ksw.shape[0], qt.shape[:2]
-    rows = ksw.shape[2] // SECOND
+    kv_heads, heads = ksw.shape[0], qt.shape[0]
     depth, features = w.shape
-    span = extra.shape[0]
+    span, few, rows = extra.shape[0], WIDTH // SECOND, ksw.shape[2] // SECOND
     return pl.pallas_call(
         far_kernel,
         out_shape=(
-            jax.ShapeDtypeStruct((rows, features // 2), jnp.bfloat16),
-            jax.ShapeDtypeStruct((rows, heads * HEAD), jnp.bfloat16),
+            jax.ShapeDtypeStruct((FAR * few, features // 2), jnp.bfloat16),
+            jax.ShapeDtypeStruct((FAR * few, heads * HEAD), jnp.bfloat16),
+            jax.ShapeDtypeStruct((kv_heads, span + rows, 2 * HEAD), jnp.bfloat16),
+            jax.ShapeDtypeStruct((kv_heads, HEAD, span), jnp.bfloat16),
+            *[jax.ShapeDtypeStruct((depth, features // 2), jnp.bfloat16)] * 2,
         ),
         in_specs=[SMEM] + [ANY] * 3 + [VMEM] * 8 + [ANY],
-        out_specs=(VMEM, VMEM),
-        scratch_shapes=common_scratch(rows, kv_heads, span // rows + 1, span)
-        + [
-            *(pltpu.VMEM(a.shape, a.dtype) for a in (acc1, peak1, norm1)),
-            pltpu.VMEM((depth, features // 2), jnp.bfloat16),
-            pltpu.SemaphoreType.DMA((15,)),
-            pltpu.SemaphoreType.DMA(()),
-        ],
+        out_specs=(VMEM,) * 6,
+        scratch_shapes=[pltpu.VMEM((span + rows, kv_heads * HEAD), jnp.bfloat16)]
+        + step_scratch(kv_heads, span)
+        + vmem_like(sums_like(heads, FAR))
+        + [pltpu.SemaphoreType.DMA((15,)), pltpu.SemaphoreType.DMA((2,))],
         compiler_params=GRANT,
         name="far",
     )(where, y, z, zp, acc1, peak1, norm1, ksw, svw, qt, bias, extra, w)
 
 
-def project_own(where, att, w):
-    rows, (depth, features) = att.shape[0], w.shape
-    return pl.pallas_call(
-        own_kernel,
-        out_shape=jax.ShapeDtypeStruct((rows, features // 2), jnp.float32),
-        in_specs=[SMEM, VMEM, ANY],
-        out_specs=VMEM,
-        scratch_shapes=[pltpu.VMEM((depth, features // 2), jnp.bfloat16), pltpu.SemaphoreType.DMA(())],
+def attend_rest(where, kcat, vt, acc1, peak1, norm1, ksw, svw, qt, bias, weight):
+    kv_heads, (heads, chunks) = ksw.shape[0], qt.shape[:2]
+    left = (chunks - FAR) * (WIDTH // SECOND)
+    return pl.pallas_call(
+        rest_kernel,
+        out_shape=(
+            jax.ShapeDtypeStruct((left, weight.shape[1]), jnp.bfloat16),
+            jax.ShapeDtypeStruct((left, heads * HEAD), jnp.bfloat16),
+        ),
+        in_specs=[SMEM] + [VMEM] * 10,
+        out_specs=(VMEM,) * 2,
+        scratch_shapes=step_scratch(kv_heads, vt.shape[2]) + vmem_like(sums_like(heads, chunks - FAR)),
         compiler_params=GRANT,
-        name="own",
-    )(where, att, w)
+        name="rest",
+    )(where, kcat, vt, acc1, peak1, norm1, ksw, svw, qt, bias, weight)
+
+
+def simple(kernel, out, *arrays):
+    return pl.pallas_call(
+        kernel, out_shape=out, in_specs=[VMEM] * len(arrays), out_specs=VMEM, compiler_params=GRANT
+    )(*arrays)
 
 
 def body(queries, keys_first, primary_value_array, keys_second, secondary_value_array, out_weight):
@@ -421,10 +459,16 @@
         where, packed, keys_second, secondary_value_array, twin, near, near_twin, qt, pick, near_bias, near_extra
     )
     far_twin = core_swap(far, count)
-    other, attention = attend_far(where, near, far, far_twin, *sums, qt, far_bias, far_extra, out_weight)
+    other, attention, kcat, vt, weight, own_weight = attend_far(
+        where, near, far, far_twin, *sums, qt, far_bias, far_extra, out_weight
+    )
     other = head_swap(other)
-    mine = project_own(where, attention, out_weight)
-    return (mine + other.astype(jnp.float32)).astype(jnp.bfloat16)
+    other_rest, attention_rest = attend_rest(where, kcat, vt, *sums, qt, far_bias, weight)
+    other_rest = head_swap(other_rest)
+    half = jax.ShapeDtypeStruct((queries.shape[0], own_weight.shape[1]), jnp.float32)
+    mine = simple(own_kernel, half, attention, attention_rest, own_weight)
+    half = jax.ShapeDtypeStruct(half.shape, jnp.bfloat16)
+    return simple(add_kernel, half, mine, other, other_rest)
 
 
 def solution(mesh):

time: 51.2 us -> 51.4 us (level)
  other arithmetic: 0.84 us -> 0.08 us
  starting transfers between devices: 14.6 us -> 15.3 us
    convert_element_type x1 -> x0, other arithmetic: 0.77 us -> none  [body(): return (mine + other.astype(jnp.float32)).astype(jnp.bfloat16)]
    ppermute x1 -> x2, starting transfers between devices: 2.94 us -> 3.63 us  [head_swap(): return lax.ppermute(value, 'head', [(0, 1), (1, 0)])]
    ppermute x1 -> x2, waiting for transfers between devices: 3.77 us -> 4.25 us  [head_swap(): return lax.ppermute(value, 'head', [(0, 1), (1, 0)])]
    pallas_call x3 -> x5, Pallas kernels: 16.8 us -> 16.5 us  [the longest x1 6.31 us: attend_near(): pl.pallas_call(near_kernel, out_shape=(*sums_like(*qt.shape[:2]), *[jax.S...]
  transfers between devices with their start and end apart: 6 -> 7, of which waited for: 4 -> 4; matrix products, arithmetic and copies ran while one was open for 0% -> 0% of each run, Pallas kernels for 23% -> 23%
where the time goes in v4:
time: 51.4 us; the launch traced here: 51.1 us
  Pallas kernels  19.4 us (38%)
  waiting for transfers between devices  16.2 us (32%)
  starting transfers between devices  15.3 us (30%)
    ppermute x2, starting transfers between devices, chip_shift(): return lax.ppermute(value, 'ctx', [(a, b) for a, b in pairs if b < count])  11.6 us
    ppermute x2, waiting for transfers between devices, chip_shift(): return lax.ppermute(value, 'ctx', [(a, b) for a, b in pairs if b < count])  10.7 us
    pallas_call x1, Pallas kernels, attend_near(): pl.pallas_call(near_kernel, out_shape=(*sums_like(*qt.shape[:2]), *[jax.S...  6.31 us
    pallas_call x1, Pallas kernels, attend_far(): pl.pallas_call(far_kernel, out_shape=(jax.ShapeDtypeStruct((FAR * few, fe...  5.85 us
    ppermute x2, waiting for transfers between devices, head_swap(): return lax.ppermute(value, 'head', [(0, 1), (1, 0)])  4.25 us
    ppermute x2, starting transfers between devices, head_swap(): return lax.ppermute(value, 'head', [(0, 1), (1, 0)])  3.63 us
    pallas_call x1, Pallas kernels, attend_rest(): pl.pallas_call(rest_kernel, out_shape=(jax.ShapeDtypeStruct((left, weight...  2.77 us
    pallas_call x1, Pallas kernels, prep(): pl.pallas_call(prep_kernel, out_shape=(jax.ShapeDtypeStruct((heads, chunk...  2.06 us
  transfers between devices with their start and end apart: 7, of which 4 were waited for; matrix products, arithmetic and copies ran while one was open for 0% of the time, Pallas kernels for 23%

profile of v4, /device:TPU:24, one launch (start us, length us, event | category | flops | bytes accessed | tf_op | source)
XLA Modules:
  0.0 51.1 jit_solution(2249799043972365243)
XLA Ops:
  0.0 0.8 %pack.1.own_ref.x0_hbm = bf16[160,256]{1,0:T(8,128)(2,1)S(1)} custom-call(bf16[64,256]{1,0:T(8,128)(2,1)} %k_ref.1, bf16[64,256]{1,0:T(8,128)(2,1)} %v_ref.1, bf16[64,256]{1,0:T(8,128)(2,1)} %ks_hbm.1, bf16[64,256]{1,0:T(8,128)(2,1)} %vs_hbm.1), custom_call_target="tpu_custom_call" | custom-call | tf_op jit(solution)/shard_map/pack/pallas_call | solution.py:59
  0.8 0.1 collective-permute-start
  0.9 1.3 %collective-permute-done.twin_ref.x1_hbm = bf16[160,256]{1,0:T(8,128)(2,1)S(1)} collective-permute-done((bf16[160,256]{1,0:T(8,128)(2,1)S(1)}, bf16[160,256]{1,0:T(8,128)(2,1)S(1)}, u32[]{:S(2)}, u32[]{:S(2)}) %collective-permute-start) | collective-permute-done | bytes 81952 | tf_op jit(solution)/shard_map/ppermute | solution.py:29
  2.2 3.8 %collective-permute-start.1 = (bf16[288,256]{1,0:T(8,128)(2,1)S(1)}, bf16[288,256]{1,0:T(8,128)(2,1)S(1)}, u32[]{:S(2)}, u32[]{:S(2)}) collective-permute-start(bf16[288,256]{1,0:T(8,128)(2,1)S(1)} %get-tuple-element.26), channel_id=1, source_target_pairs={{0,4},{2,10},{4,8},{6,14},{8,12},{10,18},{12,16},{14,22},{16,20},{... | collective-permute-start | bytes 442376 | tf_op jit(solution)/shard_map/ppermute | solution.py:34
  6.0 7.7 %collective-permute-start.2 = (bf16[256,256]{1,0:T(8,128)(2,1)S(1)}, bf16[256,256]{1,0:T(8,128)(2,1)S(1)}, u32[]{:S(2)}, u32[]{:S(2)}) collective-permute-start(bf16[256,256]{1,0:T(8,128)(2,1)S(1)} %get-tuple-element.27), channel_id=1, source_target_pairs={{0,12},{2,18},{4,16},{6,22},{8,20},{10,26},{12,24},{14,30},{16,28}... | collective-permute-start | bytes 393224 | tf_op jit(solution)/shard_map/ppermute | solution.py:34
  13.8 3.1 %collective-permute-done.1.y_hbm = bf16[288,256]{1,0:T(8,128)(2,1)S(1)} collective-permute-done((bf16[288,256]{1,0:T(8,128)(2,1)S(1)}, bf16[288,256]{1,0:T(8,128)(2,1)S(1)}, u32[]{:S(2)}, u32[]{:S(2)}) %collective-permute-start.1) | collective-permute-done | bytes 147488 | tf_op jit(solution)/shard_map/ppermute | solution.py:34
  16.8 0.0 collective-permute-start.4
  16.9 7.6 %collective-permute-done.2.z_hbm = bf16[256,256]{1,0:T(8,128)(2,1)S(1)} collective-permute-done((bf16[256,256]{1,0:T(8,128)(2,1)S(1)}, bf16[256,256]{1,0:T(8,128)(2,1)S(1)}, u32[]{:S(2)}, u32[]{:S(2)}) %collective-permute-start.2) | collective-permute-done | bytes 131104 | tf_op jit(solution)/shard_map/ppermute | solution.py:34
  24.5 0.0 collective-permute-start.3
  24.5 0.1 pad_add_fusion.where_ref
  24.6 2.1 %prep.1 = (f32[8,4,128,128]{3,2,1,0:T(8,128)S(1)}, bf16[128,1024]{1,0:T(8,128)(2,1)S(1)}, bf16[128,1024]{1,0:T(8,128)(2,1)S(1)}, bf16[128,1024]{1,0:T(8,128)(2,1...) custom-call(s32[3]{0:T(128)S(1)} %pad_add_fusion.where_ref, bf16[64,1024]{1,0:T(8,128)(2,1)} %q_hbm.1), custom_call_target="tpu_custom_call" | custom-call | tf_op jit(solution)/shard_map/prep/pallas_call | solution.py:133
  26.6 0.0 collective-permute-done.4.yp_hbm
  26.6 6.3 %near.1 = (f32[8,4,128,128]{3,2,1,0:T(8,128)S(1)}, f32[4,8,128]{2,1,0:T(8,128)S(1)}, f32[4,8,128]{2,1,0:T(8,128)S(1)}, f32[2,128,1024]{2,1,0:T(8,128)S(1)}, f32[2,128,1024]{2,1,0:T(8,128)S(1)}) custom-call(s32[3]{0:T(128)S(1)} %pad_add_fusion.where_ref, bf16[160,256]{1,0:T(8,128)(2,1)S(1)} %pack.1.own_ref.x0_hbm, bf16[64,256]{1,0:T(8,128)(2,1)} %ks_hbm.1, ...), custom_call_target="tpu_custom_call" | custom-call | tf_op jit(solution)/shard_map/near/pallas_call | solution.py:378
  33.0 0.0 collective-permute-done.3.zp_hbm
  33.0 5.8 %far.1 = (bf16[48,2048]{1,0:T(8,128)(2,1)S(1)}, bf16[48,1024]{1,0:T(8,128)(2,1)S(1)}, bf16[2,320,256]{2,1,0:T(8,128)(2,1)S(1)}, bf16[2,128,256]{2,1,0:T(8,128)(2...) custom-call(s32[3]{0:T(128)S(1)} %pad_add_fusion.where_ref, ...), custom_call_target="tpu_custom_call" | custom-call | tf_op jit(solution)/shard_map/far/pallas_call | solution.py:400
  38.8 2.9 %collective-permute-start.5 = (bf16[48,2048]{1,0:T(8,128)(2,1)S(1)}, bf16[48,2048]{1,0:T(8,128)(2,1)S(1)}, u32[]{:S(2)}, u32[]{:S(2)}) collective-permute-start(bf16[48,2048]{1,0:T(8,128)(2,1)S(1)} %get-tuple-element.45), channel_id=1, source_target_pairs={{0,1},{1,0},{2,3},{3,2},{4,5},{5,4},{6,7},{7,6},{8,9},{9,8},{10,11... | collective-permute-start | bytes 589832 | tf_op jit(solution)/shard_map/ppermute | solution.py:38
  41.8 2.8 %rest.1 = (bf16[16,2048]{1,0:T(8,128)(2,1)S(1)}, bf16[16,1024]{1,0:T(8,128)(2,1)S(1)}) custom-call(s32[3]{0:T(128)S(1)} %pad_add_fusion.where_ref, bf16[2,320,256]{2,1,0:T(8,128)(2,1)S(1)} %get-tuple-element.40.kcat, bf16[2,128,256]{2,1,0:T(8,128)(2,1)S(1)} %get-tuple-element.41.vt, f32[8,4,128,128]{3,2,1,0:T(8,128)S(1)} %get-tuple-element.32.acc1_ref, ...), custom_call_target="tpu_custom_call" | custom-call | tf_op jit(solution)/shard_map/rest/pallas_call | solution.py:423
  44.5 0.7 %collective-permute-start.6 = (bf16[16,2048]{1,0:T(8,128)(2,1)S(1)}, bf16[16,2048]{1,0:T(8,128)(2,1)S(1)}, u32[]{:S(2)}, u32[]{:S(2)}) collective-permute-start(bf16[16,2048]{1,0:T(8,128)(2,1)S(1)} %get-tuple-element.46), channel_id=1, source_target_pairs={{0,1},{1,0},{2,3},{3,2},{4,5},{5,4},{6,7},{7,6},{8,9},{9,8},{10,11... | collective-permute-start | bytes 196616 | tf_op jit(solution)/shard_map/ppermute | solution.py:38
  45.2 0.8 %shard_map.64.mine_ref = f32[64,2048]{1,0:T(8,128)S(1)} custom-call(bf16[48,1024]{1,0:T(8,128)(2,1)S(1)} %get-tuple-element.39.att, bf16[16,1024]{1,0:T(8,128)(2,1)S(1)} %get-tuple-element.43.rest, bf16[1024,2048]{1,0:T(8,128)(2,1)S(1)} %get-tuple-element.44.weight), custom_call_target="tpu_custom_call" | custom-call | tf_op jit(solution)/shard_map/pallas_call | solution.py:438
  46.1 4.2 %collective-permute-done.6.rest_ref = bf16[16,2048]{1,0:T(8,128)(2,1)S(1)} collective-permute-done((bf16[16,2048]{1,0:T(8,128)(2,1)S(1)}, bf16[16,2048]{1,0:T(8,128)(2,1)S(1)}, u32[]{:S(2)}, u32[]{:S(2)}) %collective-permute-start.6) | collective-permute-done | bytes 65568 | tf_op jit(solution)/shard_map/ppermute | solution.py:38
  50.3 0.0 collective-permute-done.5.far_ref
  50.3 0.8 %shard_map.65 = bf16[64,2048]{1,0:T(8,128)(2,1)} custom-call(f32[64,2048]{1,0:T(8,128)S(1)} %shard_map.64.mine_ref, bf16[48,2048]{1,0:T(8,128)(2,1)S(1)} %collective-permute-done.5.far_ref, bf16[16,2048]{1,0:T(8,128)(2,1)S(1)} %collective-permute-done.6.rest_ref), custom_call_target="tpu_custom_call" | custom-call | tf_op jit(solution)/shard_map/pallas_call | solution.py:438
  (1 shorter events, 0.0 us)
Async XLA Ops:
  0.8 1.4 %collective-permute-start = (bf16[160,256]{1,0:T(8,128)(2,1)S(1)}, bf16[160,256]{1,0:T(8,128)(2,1)S(1)}, u32[]{:S(2)}, u32[]{:S(2)}) collective-permute-start(bf16[160,256]{1,0:T(8,128)(2,1)S(1)} %pack.1.own_ref.x0_hbm), channel_id=1, source_target_pairs={{0,2},{2,0},{4,6},{6,4},{8,10},{10,8},{12,14},{14,12},{16,18},{18,... | collective-permute-start | bytes 245768 | tf_op jit(solution)/shard_map/ppermute | solution.py:29
  2.2 14.6 %collective-permute-start.1 = (bf16[288,256]{1,0:T(8,128)(2,1)S(1)}, bf16[288,256]{1,0:T(8,128)(2,1)S(1)}, u32[]{:S(2)}, u32[]{:S(2)}) collective-permute-start(bf16[288,256]{1,0:T(8,128)(2,1)S(1)} %get-tuple-element.26), channel_id=1, source_target_pairs={{0,4},{2,10},{4,8},{6,14},{8,12},{10,18},{12,16},{14,22},{16,20},{... | collective-permute-start | bytes 442376 | tf_op jit(solution)/shard_map/ppermute | solution.py:34
  6.0 18.4 %collective-permute-start.2 = (bf16[256,256]{1,0:T(8,128)(2,1)S(1)}, bf16[256,256]{1,0:T(8,128)(2,1)S(1)}, u32[]{:S(2)}, u32[]{:S(2)}) collective-permute-start(bf16[256,256]{1,0:T(8,128)(2,1)S(1)} %get-tuple-element.27), channel_id=1, source_target_pairs={{0,12},{2,18},{4,16},{6,22},{8,20},{10,26},{12,24},{14,30},{16,28}... | collective-permute-start | bytes 393224 | tf_op jit(solution)/shard_map/ppermute | solution.py:34
  16.8 9.8 %collective-permute-start.4 = (bf16[288,256]{1,0:T(8,128)(2,1)S(1)}, bf16[288,256]{1,0:T(8,128)(2,1)S(1)}, u32[]{:S(2)}, u32[]{:S(2)}) collective-permute-start(bf16[288,256]{1,0:T(8,128)(2,1)S(1)} %collective-permute-done.1.y_hbm), channel_id=1, source_target_pairs={{0,2},{2,0},{4,6},{6,4},{8,10},{10,8},{12,14},{14,12},{16,18},{18,... | collective-permute-start | bytes 442376 | tf_op jit(solution)/shard_map/ppermute | solution.py:29
  24.5 8.5 %collective-permute-start.3 = (bf16[256,256]{1,0:T(8,128)(2,1)S(1)}, bf16[256,256]{1,0:T(8,128)(2,1)S(1)}, u32[]{:S(2)}, u32[]{:S(2)}) collective-permute-start(bf16[256,256]{1,0:T(8,128)(2,1)S(1)} %collective-permute-done.2.z_hbm), channel_id=1, source_target_pairs={{0,2},{2,0},{4,6},{6,4},{8,10},{10,8},{12,14},{14,12},{16,18},{18,... | collective-permute-start | bytes 393224 | tf_op jit(solution)/shard_map/ppermute | solution.py:29
  38.8 11.5 %collective-permute-start.5 = (bf16[48,2048]{1,0:T(8,128)(2,1)S(1)}, bf16[48,2048]{1,0:T(8,128)(2,1)S(1)}, u32[]{:S(2)}, u32[]{:S(2)}) collective-permute-start(bf16[48,2048]{1,0:T(8,128)(2,1)S(1)} %get-tuple-element.45), channel_id=1, source_target_pairs={{0,1},{1,0},{2,3},{3,2},{4,5},{5,4},{6,7},{7,6},{8,9},{9,8},{10,11... | collective-permute-start | bytes 589832 | tf_op jit(solution)/shard_map/ppermute | solution.py:38
  44.5 5.8 %collective-permute-start.6 = (bf16[16,2048]{1,0:T(8,128)(2,1)S(1)}, bf16[16,2048]{1,0:T(8,128)(2,1)S(1)}, u32[]{:S(2)}, u32[]{:S(2)}) collective-permute-start(bf16[16,2048]{1,0:T(8,128)(2,1)S(1)} %get-tuple-element.46), channel_id=1, source_target_pairs={{0,1},{1,0},{2,3},{3,2},{4,5},{5,4},{6,7},{7,6},{8,9},{9,8},{10,11... | collective-permute-start | bytes 196616 | tf_op jit(solution)/shard_map/ppermute | solution.py:38

commit v5 on v3

--- a/solution.py
+++ b/solution.py
@@ -282,8 +282,8 @@
     rows = att.shape[0]
     half = w_hbm.shape[1] // 2
     blocks = vbuf.shape[0] // rows
-    pairs = chip_blocks(z_hbm, rows, 1 - core, core, kcat, vbuf)
-    pairs += chip_blocks(zp_hbm, rows, core, 1 - core, kcat, vbuf)
+    pairs = chip_blocks(z_hbm, rows, core, core, kcat, vbuf)
+    pairs += chip_blocks(zp_hbm, rows, 1 - core, 1 - core, kcat, vbuf)
     pairs += block_copies(y_hbm, 2 * rows, rows, blocks - 1, kcat, vbuf)
     copies = start_all(pairs, sem)
     cols = pl.ds(pl.multiple_of((1 - side) * half, 128), half)
@@ -414,7 +414,7 @@
     twin = core_swap(packed, count)
     near_load, far_load = join(packed, twin)
     near = chip_shift(near_load, count, 1, 2)
-    far = chip_shift(far_load, count, 3, 4)
+    far = chip_shift(far_load, count, 4, 3)
     qt, pick, near_bias, far_bias, near_extra, far_extra = prep(where, queries)
     near_twin = core_swap(near, count)
     sums = attend_near(

time: 51.2 us -> 50.4 us (0.984); the launches traced: 50.9 us -> 49.4 us
  waiting for transfers between devices: 15.7 us -> 13.3 us
  starting transfers between devices: 14.6 us -> 15.6 us
    ppermute x2, waiting for transfers between devices: 10.7 us -> 8.72 us  [chip_shift(): return lax.ppermute(value, 'ctx', [(a, b) for a, b in pairs if b < count])]
  transfers between devices with their start and end apart: 6 -> 6, of which waited for: 4 -> 4; matrix products, arithmetic and copies ran while one was open for 0% -> 0% of each run, Pallas kernels for 23% -> 24%
where the time goes in v5:
time: 50.4 us; the launch traced here: 49.4 us
  Pallas kernels  19.7 us (39%)
  starting transfers between devices  15.6 us (31%)
  waiting for transfers between devices  13.3 us (26%)
  other arithmetic  0.84 us (2%)
    ppermute x2, starting transfers between devices, chip_shift(): return lax.ppermute(value, 'ctx', [(a, b) for a, b in pairs if b < count])  12 us
    ppermute x2, waiting for transfers between devices, chip_shift(): return lax.ppermute(value, 'ctx', [(a, b) for a, b in pairs if b < count])  8.72 us
    pallas_call x1, Pallas kernels, attend_far(): pl.pallas_call(far_kernel, out_shape=(jax.ShapeDtypeStruct((rows, feature...  6.87 us
    pallas_call x1, Pallas kernels, attend_near(): pl.pallas_call(near_kernel, out_shape=(*sums_like(qt), *[jax.ShapeDtypeSt...  6.32 us
    pallas_call x1, Pallas kernels, project_own(): pl.pallas_call(own_kernel, out_shape=jax.ShapeDtypeStruct((rows, features...  3.58 us
    ppermute x1, waiting for transfers between devices, head_swap(): return lax.ppermute(value, 'head', [(0, 1), (1, 0)])  3.27 us
    ppermute x1, starting transfers between devices, head_swap(): return lax.ppermute(value, 'head', [(0, 1), (1, 0)])  3.1 us
    pallas_call x1, Pallas kernels, prep(): pl.pallas_call(prep_kernel, out_shape=(jax.ShapeDtypeStruct((heads, chunk...  2.06 us
  transfers between devices with their start and end apart: 6, of which 4 were waited for; matrix products, arithmetic and copies ran while one was open for 0% of the time, Pallas kernels for 24%

profile of v5, /device:TPU:24, one launch (start us, length us, event | category | flops | bytes accessed | tf_op | source)
XLA Modules:
  0.0 49.4 jit_solution(984321062510778370)
XLA Ops:
  0.0 0.8 %pack.1.own_ref.x0_hbm = bf16[160,256]{1,0:T(8,128)(2,1)S(1)} custom-call(bf16[64,256]{1,0:T(8,128)(2,1)} %k_ref.1, bf16[64,256]{1,0:T(8,128)(2,1)} %v_ref.1, bf16[64,256]{1,0:T(8,128)(2,1)} %ks_hbm.1, bf16[64,256]{1,0:T(8,128)(2,1)} %vs_hbm.1), custom_call_target="tpu_custom_call" | custom-call | tf_op jit(solution)/shard_map/pack/pallas_call | solution.py:58
  0.8 0.1 collective-permute-start
  0.9 1.3 %collective-permute-done.twin_ref.x1_hbm = bf16[160,256]{1,0:T(8,128)(2,1)S(1)} collective-permute-done((bf16[160,256]{1,0:T(8,128)(2,1)S(1)}, bf16[160,256]{1,0:T(8,128)(2,1)S(1)}, u32[]{:S(2)}, u32[]{:S(2)}) %collective-permute-start) | collective-permute-done | bytes 81952 | tf_op jit(solution)/shard_map/ppermute | solution.py:28
  2.2 3.8 %collective-permute-start.1 = (bf16[288,256]{1,0:T(8,128)(2,1)S(1)}, bf16[288,256]{1,0:T(8,128)(2,1)S(1)}, u32[]{:S(2)}, u32[]{:S(2)}) collective-permute-start(bf16[288,256]{1,0:T(8,128)(2,1)S(1)} %get-tuple-element.20), channel_id=1, source_target_pairs={{0,4},{2,10},{4,8},{6,14},{8,12},{10,18},{12,16},{14,22},{16,20},{... | collective-permute-start | bytes 442376 | tf_op jit(solution)/shard_map/ppermute | solution.py:33
  6.0 8.2 %collective-permute-start.2 = (bf16[256,256]{1,0:T(8,128)(2,1)S(1)}, bf16[256,256]{1,0:T(8,128)(2,1)S(1)}, u32[]{:S(2)}, u32[]{:S(2)}) collective-permute-start(bf16[256,256]{1,0:T(8,128)(2,1)S(1)} %get-tuple-element.21), channel_id=1, source_target_pairs={{0,16},{2,14},{4,20},{6,18},{8,24},{10,22},{12,28},{14,26},{16,32}... | collective-permute-start | bytes 393224 | tf_op jit(solution)/shard_map/ppermute | solution.py:33
  14.2 2.6 %collective-permute-done.1.y_hbm = bf16[288,256]{1,0:T(8,128)(2,1)S(1)} collective-permute-done((bf16[288,256]{1,0:T(8,128)(2,1)S(1)}, bf16[288,256]{1,0:T(8,128)(2,1)S(1)}, u32[]{:S(2)}, u32[]{:S(2)}) %collective-permute-start.1) | collective-permute-done | bytes 147488 | tf_op jit(solution)/shard_map/ppermute | solution.py:33
  16.8 0.0 collective-permute-start.4
  16.8 6.2 %collective-permute-done.2.z_hbm = bf16[256,256]{1,0:T(8,128)(2,1)S(1)} collective-permute-done((bf16[256,256]{1,0:T(8,128)(2,1)S(1)}, bf16[256,256]{1,0:T(8,128)(2,1)S(1)}, u32[]{:S(2)}, u32[]{:S(2)}) %collective-permute-start.2) | collective-permute-done | bytes 131104 | tf_op jit(solution)/shard_map/ppermute | solution.py:33
  23.0 0.3 collective-permute-start.3
  23.3 0.1 pad_add_fusion.where_ref
  23.4 2.1 %prep.1 = (f32[8,4,128,128]{3,2,1,0:T(8,128)S(1)}, bf16[128,1024]{1,0:T(8,128)(2,1)S(1)}, bf16[128,1024]{1,0:T(8,128)(2,1)S(1)}, bf16[128,1024]{1,0:T(8,128)(2,1...) custom-call(s32[3]{0:T(128)S(1)} %pad_add_fusion.where_ref, bf16[64,1024]{1,0:T(8,128)(2,1)} %q_hbm.1), custom_call_target="tpu_custom_call" | custom-call | tf_op jit(solution)/shard_map/prep/pallas_call | solution.py:132
  25.5 0.0 collective-permute-done.4.yp_hbm
  25.5 6.3 %near.1 = (f32[8,4,128,128]{3,2,1,0:T(8,128)S(1)}, f32[4,8,128]{2,1,0:T(8,128)S(1)}, f32[4,8,128]{2,1,0:T(8,128)S(1)}, f32[2,128,1024]{2,1,0:T(8,128)S(1)}, f32[2,128,1024]{2,1,0:T(8,128)S(1)}) custom-call(s32[3]{0:T(128)S(1)} %pad_add_fusion.where_ref, bf16[160,256]{1,0:T(8,128)(2,1)S(1)} %pack.1.own_ref.x0_hbm, bf16[64,256]{1,0:T(8,128)(2,1)} %ks_hbm.1, ...), custom_call_target="tpu_custom_call" | custom-call | tf_op jit(solution)/shard_map/near/pallas_call | solution.py:354
  31.8 0.0 collective-permute-done.3.zp_hbm
  31.8 6.9 %far.1 = (bf16[64,2048]{1,0:T(8,128)(2,1)S(1)}, bf16[64,1024]{1,0:T(8,128)(2,1)S(1)}) custom-call(s32[3]{0:T(128)S(1)} %pad_add_fusion.where_ref, bf16[288,256]{1,0:T(8,128)(2,1)S(1)} %collective-permute-done.1.y_hbm, bf16[256,256]{1,0:T(8,128)(2,1)S(1)} %collective-permute-done.2.z_hbm, bf16[256,256]{1,0:T(8,128)(2,1)S(1)} %collective-permute-done.3.zp_hbm, ...), custom_call_target="tpu_custom_call" | custom-call | tf_op jit(solution)/shard_map/far/pallas_call | solution.py:372
  38.7 3.1 %collective-permute-start.5 = (bf16[64,2048]{1,0:T(8,128)(2,1)S(1)}, bf16[64,2048]{1,0:T(8,128)(2,1)S(1)}, u32[]{:S(2)}, u32[]{:S(2)}) collective-permute-start(bf16[64,2048]{1,0:T(8,128)(2,1)S(1)} %get-tuple-element.34), channel_id=1, source_target_pairs={{0,1},{1,0},{2,3},{3,2},{4,5},{5,4},{6,7},{7,6},{8,9},{9,8},{10,11... | collective-permute-start | bytes 786440 | tf_op jit(solution)/shard_map/ppermute | solution.py:37
  41.8 3.6 %own.1 = f32[64,2048]{1,0:T(8,128)S(1)} custom-call(s32[3]{0:T(128)S(1)} %pad_add_fusion.where_ref, bf16[64,1024]{1,0:T(8,128)(2,1)S(1)} %get-tuple-element.33.att, bf16[1024,4096]{1,0:T(8,128)(2,1)} %w_hbm.3), custom_call_target="tpu_custom_call" | custom-call | tf_op jit(solution)/shard_map/own/pallas_call | solution.py:394
  45.4 3.3 %collective-permute-done.5 = bf16[64,2048]{1,0:T(8,128)(2,1)S(1)} collective-permute-done((bf16[64,2048]{1,0:T(8,128)(2,1)S(1)}, bf16[64,2048]{1,0:T(8,128)(2,1)S(1)}, u32[]{:S(2)}, u32[]{:S(2)}) %collective-permute-start.5) | collective-permute-done | bytes 262176 | tf_op jit(solution)/shard_map/ppermute | solution.py:37
  48.7 0.8 %add_convert_fusion = bf16[64,2048]{1,0:T(8,128)(2,1)} fusion(f32[64,2048]{1,0:T(8,128)S(1)} %own.1, bf16[64,2048]{1,0:T(8,128)(2,1)S(1)} %collective-permute-done.5), kind=kLoop, calls=%fused_computation | loop fusion | flops 393216 | bytes 1048576 | tf_op jit(solution)/shard_map/convert_element_type | solution.py:427
  (1 shorter events, 0.0 us)
Async XLA Ops:
  0.8 1.4 %collective-permute-start = (bf16[160,256]{1,0:T(8,128)(2,1)S(1)}, bf16[160,256]{1,0:T(8,128)(2,1)S(1)}, u32[]{:S(2)}, u32[]{:S(2)}) collective-permute-start(bf16[160,256]{1,0:T(8,128)(2,1)S(1)} %pack.1.own_ref.x0_hbm), channel_id=1, source_target_pairs={{0,2},{2,0},{4,6},{6,4},{8,10},{10,8},{12,14},{14,12},{16,18},{18,... | collective-permute-start | bytes 245768 | tf_op jit(solution)/shard_map/ppermute | solution.py:28
  2.2 14.6 %collective-permute-start.1 = (bf16[288,256]{1,0:T(8,128)(2,1)S(1)}, bf16[288,256]{1,0:T(8,128)(2,1)S(1)}, u32[]{:S(2)}, u32[]{:S(2)}) collective-permute-start(bf16[288,256]{1,0:T(8,128)(2,1)S(1)} %get-tuple-element.20), channel_id=1, source_target_pairs={{0,4},{2,10},{4,8},{6,14},{8,12},{10,18},{12,16},{14,22},{16,20},{... | collective-permute-start | bytes 442376 | tf_op jit(solution)/shard_map/ppermute | solution.py:33
  6.0 16.9 %collective-permute-start.2 = (bf16[256,256]{1,0:T(8,128)(2,1)S(1)}, bf16[256,256]{1,0:T(8,128)(2,1)S(1)}, u32[]{:S(2)}, u32[]{:S(2)}) collective-permute-start(bf16[256,256]{1,0:T(8,128)(2,1)S(1)} %get-tuple-element.21), channel_id=1, source_target_pairs={{0,16},{2,14},{4,20},{6,18},{8,24},{10,22},{12,28},{14,26},{16,32}... | collective-permute-start | bytes 393224 | tf_op jit(solution)/shard_map/ppermute | solution.py:33
  16.8 8.7 %collective-permute-start.4 = (bf16[288,256]{1,0:T(8,128)(2,1)S(1)}, bf16[288,256]{1,0:T(8,128)(2,1)S(1)}, u32[]{:S(2)}, u32[]{:S(2)}) collective-permute-start(bf16[288,256]{1,0:T(8,128)(2,1)S(1)} %collective-permute-done.1.y_hbm), channel_id=1, source_target_pairs={{0,2},{2,0},{4,6},{6,4},{8,10},{10,8},{12,14},{14,12},{16,18},{18,... | collective-permute-start | bytes 442376 | tf_op jit(solution)/shard_map/ppermute | solution.py:28
  23.0 8.8 %collective-permute-start.3 = (bf16[256,256]{1,0:T(8,128)(2,1)S(1)}, bf16[256,256]{1,0:T(8,128)(2,1)S(1)}, u32[]{:S(2)}, u32[]{:S(2)}) collective-permute-start(bf16[256,256]{1,0:T(8,128)(2,1)S(1)} %collective-permute-done.2.z_hbm), channel_id=1, source_target_pairs={{0,2},{2,0},{4,6},{6,4},{8,10},{10,8},{12,14},{14,12},{16,18},{18,... | collective-permute-start | bytes 393224 | tf_op jit(solution)/shard_map/ppermute | solution.py:28
  38.7 10.0 %collective-permute-start.5 = (bf16[64,2048]{1,0:T(8,128)(2,1)S(1)}, bf16[64,2048]{1,0:T(8,128)(2,1)S(1)}, u32[]{:S(2)}, u32[]{:S(2)}) collective-permute-start(bf16[64,2048]{1,0:T(8,128)(2,1)S(1)} %get-tuple-element.34), channel_id=1, source_target_pairs={{0,1},{1,0},{2,3},{3,2},{4,5},{5,4},{6,7},{7,6},{8,9},{9,8},{10,11... | collective-permute-start | bytes 786440 | tf_op jit(solution)/shard_map/ppermute | solution.py:37

commit v6 on v5

--- a/solution.py
+++ b/solution.py
@@ -15,7 +15,8 @@
 LOG2E = 1.4426950408889634
 NEG = -1e30
 WIDTH = 256
-UNROLL = 4
+UNROLL = 8
+PAIR = 2
 NEAR = 5
 ANY = pl.BlockSpec(memory_space=pl.ANY)
 VMEM = pl.BlockSpec(memory_space=pltpu.VMEM)
@@ -276,7 +277,7 @@
 def far_kernel(
     where_ref, y_hbm, z_hbm, zp_hbm, acc1_ref, peak1_ref, norm1_ref, ksw, svw, qt, bias, extra, w_hbm,
     other_ref, att,
-    kcat, vbuf, vt, sbuf, wbuf, tops, grows, out, peak, norm, weight, sem, wsem,
+    kcat, vbuf, vt, sbuf, wbuf, tops, grows, out, peak, norm, weight, partial, sem, wsem,
 ):
     core, side = where_ref[1], where_ref[2]
     rows = att.shape[0]
@@ -298,6 +299,7 @@
     heads, chunks = qt.shape[:2]
     few = WIDTH // SECOND
     shifts = [few << i for i in range((128 // few).bit_length() - 1)]
+    factors = []
     for c in range(chunks):
         top = peak[c]
         most = top
@@ -307,13 +309,22 @@
         total = norm[c] * grow
         for shift in shifts:
             total = total + pltpu.roll(total, shift, 1)
-        grow = grow / total
-        for h in range(heads):
-            part = (out[h, c] * grow[h : h + 1]).T
-            part = functools.reduce(jnp.add, [part[i : i + few] for i in range(0, 128, few)])
-            att[c * few : (c + 1) * few, h * HEAD : (h + 1) * HEAD] = part.astype(jnp.bfloat16)
+        factors.append(grow / total)
     fetch.wait()
-    other_ref[...] = jnp.dot(att[...], weight[...], preferred_element_type=jnp.float32).astype(jnp.bfloat16)
+    for k in range(heads // PAIR):
+        for h in range(k * PAIR, (k + 1) * PAIR):
+            for c in range(chunks):
+                part = (out[h, c] * factors[c][h : h + 1]).T
+                part = functools.reduce(jnp.add, [part[i : i + few] for i in range(0, 128, few)])
+                att[c * few : (c + 1) * few, h * HEAD : (h + 1) * HEAD] = part.astype(jnp.bfloat16)
+        at = slice(k * PAIR * HEAD, (k + 1) * PAIR * HEAD)
+        more = jnp.dot(att[:, at], weight[at, :], preferred_element_type=jnp.float32)
+        if k == 0:
+            partial[...] = more
+        elif k < heads // PAIR - 1:
+            partial[...] += more
+        else:
+            other_ref[...] = (partial[...] + more).astype(jnp.bfloat16)
 
 
 def own_kernel(where_ref, att, w_hbm, mine_ref, weight, sem):
@@ -381,6 +392,7 @@
         + [
             *(pltpu.VMEM(a.shape, a.dtype) for a in (acc1, peak1, norm1)),
             pltpu.VMEM((depth, features // 2), jnp.bfloat16),
+            pltpu.VMEM((rows, features // 2), jnp.float32),
             pltpu.SemaphoreType.DMA((15,)),
             pltpu.SemaphoreType.DMA(()),
         ],

time: 50.4 us -> 49.6 us (0.984)
  the two profiles are of different devices: /device:TPU:24 before, /device:TPU:88 now
where the time goes in v6:
time: 49.6 us; the launch traced here: 49.3 us
  Pallas kernels  18.8 us (38%)
  waiting for transfers between devices  16 us (32%)
  starting transfers between devices  13.5 us (27%)
  other arithmetic  0.84 us (2%)
    ppermute x2, waiting for transfers between devices, chip_shift(): return lax.ppermute(value, 'ctx', [(a, b) for a, b in pairs if b < count])  11.1 us
    ppermute x2, starting transfers between devices, chip_shift(): return lax.ppermute(value, 'ctx', [(a, b) for a, b in pairs if b < count])  10.2 us
    pallas_call x1, Pallas kernels, attend_far(): pl.pallas_call(far_kernel, out_shape=(jax.ShapeDtypeStruct((rows, feature...  6.36 us
    pallas_call x1, Pallas kernels, attend_near(): pl.pallas_call(near_kernel, out_shape=(*sums_like(qt), *[jax.ShapeDtypeSt...  6.01 us
    ppermute x1, waiting for transfers between devices, head_swap(): return lax.ppermute(value, 'head', [(0, 1), (1, 0)])  3.59 us
    pallas_call x1, Pallas kernels, project_own(): pl.pallas_call(own_kernel, out_shape=jax.ShapeDtypeStruct((rows, features...  3.58 us
    ppermute x1, starting transfers between devices, head_swap(): return lax.ppermute(value, 'head', [(0, 1), (1, 0)])  3.02 us
    pallas_call x1, Pallas kernels, prep(): pl.pallas_call(prep_kernel, out_shape=(jax.ShapeDtypeStruct((heads, chunk...  2.06 us
  transfers between devices with their start and end apart: 6, of which 3 were waited for; matrix products, arithmetic and copies ran while one was open for 0% of the time, Pallas kernels for 24%

profile of v6, /device:TPU:88, one launch (start us, length us, event | category | flops | bytes accessed | tf_op | source)
XLA Modules:
  0.0 49.3 jit_solution(1166159208972736478)
XLA Ops:
  0.0 0.8 %pack.1.own_ref.x0_hbm = bf16[160,256]{1,0:T(8,128)(2,1)S(1)} custom-call(bf16[64,256]{1,0:T(8,128)(2,1)} %k_ref.1, bf16[64,256]{1,0:T(8,128)(2,1)} %v_ref.1, bf16[64,256]{1,0:T(8,128)(2,1)} %ks_hbm.1, bf16[64,256]{1,0:T(8,128)(2,1)} %vs_hbm.1), custom_call_target="tpu_custom_call" | custom-call | tf_op jit(solution)/shard_map/pack/pallas_call | solution.py:59
  0.8 0.1 collective-permute-start
  0.9 1.3 %collective-permute-done.twin_ref.x1_hbm = bf16[160,256]{1,0:T(8,128)(2,1)S(1)} collective-permute-done((bf16[160,256]{1,0:T(8,128)(2,1)S(1)}, bf16[160,256]{1,0:T(8,128)(2,1)S(1)}, u32[]{:S(2)}, u32[]{:S(2)}) %collective-permute-start) | collective-permute-done | bytes 81952 | tf_op jit(solution)/shard_map/ppermute | solution.py:29
  2.2 3.8 %collective-permute-start.1 = (bf16[288,256]{1,0:T(8,128)(2,1)S(1)}, bf16[288,256]{1,0:T(8,128)(2,1)S(1)}, u32[]{:S(2)}, u32[]{:S(2)}) collective-permute-start(bf16[288,256]{1,0:T(8,128)(2,1)S(1)} %get-tuple-element.20), channel_id=1, source_target_pairs={{0,4},{2,10},{4,8},{6,14},{8,12},{10,18},{12,16},{14,22},{16,20},{... | collective-permute-start | bytes 442376 | tf_op jit(solution)/shard_map/ppermute | solution.py:34
  6.0 6.4 %collective-permute-start.2 = (bf16[256,256]{1,0:T(8,128)(2,1)S(1)}, bf16[256,256]{1,0:T(8,128)(2,1)S(1)}, u32[]{:S(2)}, u32[]{:S(2)}) collective-permute-start(bf16[256,256]{1,0:T(8,128)(2,1)S(1)} %get-tuple-element.21), channel_id=1, source_target_pairs={{0,16},{2,14},{4,20},{6,18},{8,24},{10,22},{12,28},{14,26},{16,32}... | collective-permute-start | bytes 393224 | tf_op jit(solution)/shard_map/ppermute | solution.py:34
  12.4 0.0 collective-permute-done.1.y_hbm
  12.5 0.1 collective-permute-start.4
  12.6 11.1 %collective-permute-done.2.z_hbm = bf16[256,256]{1,0:T(8,128)(2,1)S(1)} collective-permute-done((bf16[256,256]{1,0:T(8,128)(2,1)S(1)}, bf16[256,256]{1,0:T(8,128)(2,1)S(1)}, u32[]{:S(2)}, u32[]{:S(2)}) %collective-permute-start.2) | collective-permute-done | bytes 131104 | tf_op jit(solution)/shard_map/ppermute | solution.py:34
  23.7 0.1 collective-permute-start.3
  23.8 0.1 pad_add_fusion.where_ref
  23.9 2.1 %prep.1 = (f32[8,4,128,128]{3,2,1,0:T(8,128)S(1)}, bf16[128,1024]{1,0:T(8,128)(2,1)S(1)}, bf16[128,1024]{1,0:T(8,128)(2,1)S(1)}, bf16[128,1024]{1,0:T(8,128)(2,1...) custom-call(s32[3]{0:T(128)S(1)} %pad_add_fusion.where_ref, bf16[64,1024]{1,0:T(8,128)(2,1)} %q_hbm.1), custom_call_target="tpu_custom_call" | custom-call | tf_op jit(solution)/shard_map/prep/pallas_call | solution.py:133
  25.9 0.0 collective-permute-done.4.yp_hbm
  25.9 6.0 %near.1 = (f32[8,4,128,128]{3,2,1,0:T(8,128)S(1)}, f32[4,8,128]{2,1,0:T(8,128)S(1)}, f32[4,8,128]{2,1,0:T(8,128)S(1)}, f32[2,128,1024]{2,1,0:T(8,128)S(1)}, f32[2,128,1024]{2,1,0:T(8,128)S(1)}) custom-call(s32[3]{0:T(128)S(1)} %pad_add_fusion.where_ref, bf16[160,256]{1,0:T(8,128)(2,1)S(1)} %pack.1.own_ref.x0_hbm, bf16[64,256]{1,0:T(8,128)(2,1)} %ks_hbm.1, ...), custom_call_target="tpu_custom_call" | custom-call | tf_op jit(solution)/shard_map/near/pallas_call | solution.py:365
  32.0 0.0 collective-permute-done.3.zp_hbm
  32.0 6.4 %far.1 = (bf16[64,2048]{1,0:T(8,128)(2,1)S(1)}, bf16[64,1024]{1,0:T(8,128)(2,1)S(1)}) custom-call(s32[3]{0:T(128)S(1)} %pad_add_fusion.where_ref, bf16[288,256]{1,0:T(8,128)(2,1)S(1)} %collective-permute-done.1.y_hbm, bf16[256,256]{1,0:T(8,128)(2,1)S(1)} %collective-permute-done.2.z_hbm, bf16[256,256]{1,0:T(8,128)(2,1)S(1)} %collective-permute-done.3.zp_hbm, ...), custom_call_target="tpu_custom_call" | custom-call | tf_op jit(solution)/shard_map/far/pallas_call | solution.py:383
  38.3 3.0 %collective-permute-start.5 = (bf16[64,2048]{1,0:T(8,128)(2,1)S(1)}, bf16[64,2048]{1,0:T(8,128)(2,1)S(1)}, u32[]{:S(2)}, u32[]{:S(2)}) collective-permute-start(bf16[64,2048]{1,0:T(8,128)(2,1)S(1)} %get-tuple-element.34), channel_id=1, source_target_pairs={{0,1},{1,0},{2,3},{3,2},{4,5},{5,4},{6,7},{7,6},{8,9},{9,8},{10,11... | collective-permute-start | bytes 786440 | tf_op jit(solution)/shard_map/ppermute | solution.py:38
  41.4 3.6 %own.1 = f32[64,2048]{1,0:T(8,128)S(1)} custom-call(s32[3]{0:T(128)S(1)} %pad_add_fusion.where_ref, bf16[64,1024]{1,0:T(8,128)(2,1)S(1)} %get-tuple-element.33.att, bf16[1024,4096]{1,0:T(8,128)(2,1)} %w_hbm.3), custom_call_target="tpu_custom_call" | custom-call | tf_op jit(solution)/shard_map/own/pallas_call | solution.py:406
  44.9 3.6 %collective-permute-done.5 = bf16[64,2048]{1,0:T(8,128)(2,1)S(1)} collective-permute-done((bf16[64,2048]{1,0:T(8,128)(2,1)S(1)}, bf16[64,2048]{1,0:T(8,128)(2,1)S(1)}, u32[]{:S(2)}, u32[]{:S(2)}) %collective-permute-start.5) | collective-permute-done | bytes 262176 | tf_op jit(solution)/shard_map/ppermute | solution.py:38
  48.5 0.8 %add_convert_fusion = bf16[64,2048]{1,0:T(8,128)(2,1)} fusion(f32[64,2048]{1,0:T(8,128)S(1)} %own.1, bf16[64,2048]{1,0:T(8,128)(2,1)S(1)} %collective-permute-done.5), kind=kLoop, calls=%fused_computation | loop fusion | flops 393216 | bytes 1048576 | tf_op jit(solution)/shard_map/convert_element_type | solution.py:439
  (1 shorter events, 0.0 us)
Async XLA Ops:
  0.8 1.4 %collective-permute-start = (bf16[160,256]{1,0:T(8,128)(2,1)S(1)}, bf16[160,256]{1,0:T(8,128)(2,1)S(1)}, u32[]{:S(2)}, u32[]{:S(2)}) collective-permute-start(bf16[160,256]{1,0:T(8,128)(2,1)S(1)} %pack.1.own_ref.x0_hbm), channel_id=1, source_target_pairs={{0,2},{2,0},{4,6},{6,4},{8,10},{10,8},{12,14},{14,12},{16,18},{18,... | collective-permute-start | bytes 245768 | tf_op jit(solution)/shard_map/ppermute | solution.py:29
  2.2 10.2 %collective-permute-start.1 = (bf16[288,256]{1,0:T(8,128)(2,1)S(1)}, bf16[288,256]{1,0:T(8,128)(2,1)S(1)}, u32[]{:S(2)}, u32[]{:S(2)}) collective-permute-start(bf16[288,256]{1,0:T(8,128)(2,1)S(1)} %get-tuple-element.20), channel_id=1, source_target_pairs={{0,4},{2,10},{4,8},{6,14},{8,12},{10,18},{12,16},{14,22},{16,20},{... | collective-permute-start | bytes 442376 | tf_op jit(solution)/shard_map/ppermute | solution.py:34
  6.0 17.6 %collective-permute-start.2 = (bf16[256,256]{1,0:T(8,128)(2,1)S(1)}, bf16[256,256]{1,0:T(8,128)(2,1)S(1)}, u32[]{:S(2)}, u32[]{:S(2)}) collective-permute-start(bf16[256,256]{1,0:T(8,128)(2,1)S(1)} %get-tuple-element.21), channel_id=1, source_target_pairs={{0,16},{2,14},{4,20},{6,18},{8,24},{10,22},{12,28},{14,26},{16,32}... | collective-permute-start | bytes 393224 | tf_op jit(solution)/shard_map/ppermute | solution.py:34
  12.5 13.5 %collective-permute-start.4 = (bf16[288,256]{1,0:T(8,128)(2,1)S(1)}, bf16[288,256]{1,0:T(8,128)(2,1)S(1)}, u32[]{:S(2)}, u32[]{:S(2)}) collective-permute-start(bf16[288,256]{1,0:T(8,128)(2,1)S(1)} %collective-permute-done.1.y_hbm), channel_id=1, source_target_pairs={{0,2},{2,0},{4,6},{6,4},{8,10},{10,8},{12,14},{14,12},{16,18},{18,... | collective-permute-start | bytes 442376 | tf_op jit(solution)/shard_map/ppermute | solution.py:29
  23.7 8.3 %collective-permute-start.3 = (bf16[256,256]{1,0:T(8,128)(2,1)S(1)}, bf16[256,256]{1,0:T(8,128)(2,1)S(1)}, u32[]{:S(2)}, u32[]{:S(2)}) collective-permute-start(bf16[256,256]{1,0:T(8,128)(2,1)S(1)} %collective-permute-done.2.z_hbm), channel_id=1, source_target_pairs={{0,2},{2,0},{4,6},{6,4},{8,10},{10,8},{12,14},{14,12},{16,18},{18,... | collective-permute-start | bytes 393224 | tf_op jit(solution)/shard_map/ppermute | solution.py:29
  38.3 10.2 %collective-permute-start.5 = (bf16[64,2048]{1,0:T(8,128)(2,1)S(1)}, bf16[64,2048]{1,0:T(8,128)(2,1)S(1)}, u32[]{:S(2)}, u32[]{:S(2)}) collective-permute-start(bf16[64,2048]{1,0:T(8,128)(2,1)S(1)} %get-tuple-element.34), channel_id=1, source_target_pairs={{0,1},{1,0},{2,3},{3,2},{4,5},{5,4},{6,7},{7,6},{8,9},{9,8},{10,11... | collective-permute-start | bytes 786440 | tf_op jit(solution)/shard_map/ppermute | solution.py:38

commit v7 on v6

--- a/solution.py
+++ b/solution.py
@@ -96,11 +96,9 @@
     return few * (lane // WIDTH) + lane % few, (lane % WIDTH) // few
 
 
-def prep_kernel(where_ref, q_hbm, qt_ref, pick_ref, near_bias_ref, far_bias_ref, near_extra_ref, far_extra_ref, q, sem):
+def masks_kernel(where_ref, pick_ref, near_bias_ref, far_bias_ref, near_extra_ref, far_extra_ref):
     shard = where_ref[0]
-    copy = pltpu.make_async_copy(q_hbm, q, sem)
-    copy.start()
-    rows = q.shape[0]
+    rows = pick_ref.shape[1] // SECOND
     shape = pick_ref.shape
     feature = lax.broadcasted_iota(jnp.int32, shape, 0)
     token, offset = lane_token(lax.broadcasted_iota(jnp.int32, shape, 1))
@@ -118,6 +116,27 @@
         gone = jnp.where(first + row // rows < 0, NEG, 0.0)
         extra = jnp.where(col == rows, gone, jnp.where(col == rows + 1, 1.0, 0.0))
         ref[...] = jnp.where((col < rows) & (row - cut == col), 1.0, extra).astype(jnp.bfloat16)
+
+
+def masks(where, rows):
+    lanes = SECOND * rows
+    return pl.pallas_call(
+        masks_kernel,
+        out_shape=(
+            *[jax.ShapeDtypeStruct((HEAD, lanes), jnp.bfloat16)] * 3,
+            jax.ShapeDtypeStruct((NEAR * rows, HEAD), jnp.bfloat16),
+            jax.ShapeDtypeStruct((FIRST + rows - NEAR * rows, HEAD), jnp.bfloat16),
+        ),
+        in_specs=[SMEM],
+        out_specs=(VMEM,) * 5,
+        compiler_params=GRANT,
+        name="masks",
+    )(where)
+
+
+def turn_kernel(q_hbm, qt_ref, q, sem):
+    copy = pltpu.make_async_copy(q_hbm, q, sem)
+    copy.start()
     copy.wait()
     scale = LOG2E / math.sqrt(HEAD)
     few = WIDTH // SECOND
@@ -127,23 +146,18 @@
             qt_ref[h, c] = jnp.concatenate([part[c * few : (c + 1) * few]] * (128 // few), axis=0).T
 
 
-def prep(where, q):
+def turn(q):
     rows, wide = q.shape
-    heads, lanes, chunks = wide // HEAD, SECOND * rows, SECOND * rows // WIDTH
-    return pl.pallas_call(
-        prep_kernel,
-        out_shape=(
-            jax.ShapeDtypeStruct((heads, chunks, HEAD, 128), jnp.float32),
-            *[jax.ShapeDtypeStruct((HEAD, lanes), jnp.bfloat16)] * 3,
-            jax.ShapeDtypeStruct((NEAR * rows, HEAD), jnp.bfloat16),
-            jax.ShapeDtypeStruct((FIRST + rows - NEAR * rows, HEAD), jnp.bfloat16),
-        ),
-        in_specs=[SMEM, ANY],
-        out_specs=(VMEM,) * 6,
+    heads, chunks = wide // HEAD, SECOND * rows // WIDTH
+    return pl.pallas_call(
+        turn_kernel,
+        out_shape=jax.ShapeDtypeStruct((heads, chunks, HEAD, 128), jnp.float32),
+        in_specs=[ANY],
+        out_specs=VMEM,
         scratch_shapes=[pltpu.VMEM(q.shape, q.dtype), pltpu.SemaphoreType.DMA(())],
         compiler_params=GRANT,
-        name="prep",
-    )(where, q)
+        name="turn",
+    )(q)
 
 
 def windows(where_ref, ks, vs, x1, y, pick, ksw, svw, rows):
@@ -427,7 +441,8 @@
     near_load, far_load = join(packed, twin)
     near = chip_shift(near_load, count, 1, 2)
     far = chip_shift(far_load, count, 4, 3)
-    qt, pick, near_bias, far_bias, near_extra, far_extra = prep(where, queries)
+    pick, near_bias, far_bias, near_extra, far_extra = masks(where, queries.shape[0])
+    qt = turn(queries)
     near_twin = core_swap(near, count)
     sums = attend_near(
         where, packed, keys_second, secondary_value_array, twin, near, near_twin, qt, pick, near_bias, near_extra

time: 49.6 us -> 49.8 us (level)
    pallas_call x1 -> x2, Pallas kernels: 2.06 us -> 2.24 us  [the longest x1 1.52 us: turn(): pl.pallas_call(turn_kernel, out_shape=jax.ShapeDtypeStruct((heads, chunks...]
where the time goes in v7:
time: 49.8 us; the launch traced here: 49.5 us
  Pallas kernels  19 us (38%)
  waiting for transfers between devices  16 us (32%)
  starting transfers between devices  13.5 us (27%)
  other arithmetic  0.83 us (2%)
    ppermute x2, waiting for transfers between devices, chip_shift(): return lax.ppermute(value, 'ctx', [(a, b) for a, b in pairs if b < count])  11.1 us
    ppermute x2, starting transfers between devices, chip_shift(): return lax.ppermute(value, 'ctx', [(a, b) for a, b in pairs if b < count])  10.2 us
    pallas_call x1, Pallas kernels, attend_far(): pl.pallas_call(far_kernel, out_shape=(jax.ShapeDtypeStruct((rows, feature...  6.36 us
    pallas_call x1, Pallas kernels, attend_near(): pl.pallas_call(near_kernel, out_shape=(*sums_like(qt), *[jax.ShapeDtypeSt...  6.01 us
    ppermute x1, waiting for transfers between devices, head_swap(): return lax.ppermute(value, 'head', [(0, 1), (1, 0)])  3.59 us
    pallas_call x1, Pallas kernels, project_own(): pl.pallas_call(own_kernel, out_shape=jax.ShapeDtypeStruct((rows, features...  3.58 us
    ppermute x1, starting transfers between devices, head_swap(): return lax.ppermute(value, 'head', [(0, 1), (1, 0)])  3.02 us
    pallas_call x1, Pallas kernels, turn(): pl.pallas_call(turn_kernel, out_shape=jax.ShapeDtypeStruct((heads, chunks...  1.52 us
  transfers between devices with their start and end apart: 6, of which 3 were waited for; matrix products, arithmetic and copies ran while one was open for 0% of the time, Pallas kernels for 24%

profile of v7, /device:TPU:88, one launch (start us, length us, event | category | flops | bytes accessed | tf_op | source)
XLA Modules:
  0.0 49.5 jit_solution(7591628533923586900)
XLA Ops:
  0.0 0.8 %pack.1.own_ref.x0_hbm = bf16[160,256]{1,0:T(8,128)(2,1)S(1)} custom-call(bf16[64,256]{1,0:T(8,128)(2,1)} %k_ref.1, bf16[64,256]{1,0:T(8,128)(2,1)} %v_ref.1, bf16[64,256]{1,0:T(8,128)(2,1)} %ks_hbm.1, bf16[64,256]{1,0:T(8,128)(2,1)} %vs_hbm.1), custom_call_target="tpu_custom_call" | custom-call | tf_op jit(solution)/shard_map/pack/pallas_call | solution.py:59
  0.8 0.1 collective-permute-start
  0.9 1.3 %collective-permute-done.twin_ref.x1_hbm = bf16[160,256]{1,0:T(8,128)(2,1)S(1)} collective-permute-done((bf16[160,256]{1,0:T(8,128)(2,1)S(1)}, bf16[160,256]{1,0:T(8,128)(2,1)S(1)}, u32[]{:S(2)}, u32[]{:S(2)}) %collective-permute-start) | collective-permute-done | bytes 81952 | tf_op jit(solution)/shard_map/ppermute | solution.py:29
  2.2 3.8 %collective-permute-start.1 = (bf16[288,256]{1,0:T(8,128)(2,1)S(1)}, bf16[288,256]{1,0:T(8,128)(2,1)S(1)}, u32[]{:S(2)}, u32[]{:S(2)}) collective-permute-start(bf16[288,256]{1,0:T(8,128)(2,1)S(1)} %get-tuple-element.19), channel_id=1, source_target_pairs={{0,4},{2,10},{4,8},{6,14},{8,12},{10,18},{12,16},{14,22},{16,20},{... | collective-permute-start | bytes 442376 | tf_op jit(solution)/shard_map/ppermute | solution.py:34
  6.0 6.4 %collective-permute-start.2 = (bf16[256,256]{1,0:T(8,128)(2,1)S(1)}, bf16[256,256]{1,0:T(8,128)(2,1)S(1)}, u32[]{:S(2)}, u32[]{:S(2)}) collective-permute-start(bf16[256,256]{1,0:T(8,128)(2,1)S(1)} %get-tuple-element.20), channel_id=1, source_target_pairs={{0,16},{2,14},{4,20},{6,18},{8,24},{10,22},{12,28},{14,26},{16,32}... | collective-permute-start | bytes 393224 | tf_op jit(solution)/shard_map/ppermute | solution.py:34
  12.4 0.0 collective-permute-done.1.y_hbm
  12.5 0.1 collective-permute-start.4
  12.6 11.1 %collective-permute-done.2.z_hbm = bf16[256,256]{1,0:T(8,128)(2,1)S(1)} collective-permute-done((bf16[256,256]{1,0:T(8,128)(2,1)S(1)}, bf16[256,256]{1,0:T(8,128)(2,1)S(1)}, u32[]{:S(2)}, u32[]{:S(2)}) %collective-permute-start.2) | collective-permute-done | bytes 131104 | tf_op jit(solution)/shard_map/ppermute | solution.py:34
  23.7 0.1 collective-permute-start.3
  23.8 0.1 pad_add_fusion.where_ref
  23.9 0.7 %masks.1 = (bf16[128,1024]{1,0:T(8,128)(2,1)S(1)}, bf16[128,1024]{1,0:T(8,128)(2,1)S(1)}, bf16[128,1024]{1,0:T(8,128)(2,1)S(1)}, bf16[320,128]{1,0:T(8,128)(2,1)S(1)}, bf16[256,128]{1,0:T(8,128)(2,1)S(1)}) custom-call(s32[3]{0:T(128)S(1)} %pad_add_fusion.where_ref), custom_call_target="tpu_custom_call" | custom-call | tf_op jit(solution)/shard_map/masks/pallas_call | solution.py:123
  24.6 1.5 %turn.1.qt = f32[8,4,128,128]{3,2,1,0:T(8,128)S(1)} custom-call(bf16[64,1024]{1,0:T(8,128)(2,1)} %q_hbm.1), custom_call_target="tpu_custom_call" | custom-call | tf_op jit(solution)/shard_map/turn/pallas_call | solution.py:152
  26.1 0.0 collective-permute-done.4.yp_hbm
  26.1 6.0 %near.1 = (f32[8,4,128,128]{3,2,1,0:T(8,128)S(1)}, f32[4,8,128]{2,1,0:T(8,128)S(1)}, f32[4,8,128]{2,1,0:T(8,128)S(1)}, f32[2,128,1024]{2,1,0:T(8,128)S(1)}, f32[2,128,1024]{2,1,0:T(8,128)S(1)}) custom-call(s32[3]{0:T(128)S(1)} %pad_add_fusion.where_ref, bf16[160,256]{1,0:T(8,128)(2,1)S(1)} %pack.1.own_ref.x0_hbm, bf16[64,256]{1,0:T(8,128)(2,1)} %ks_hbm.1, ...), custom_call_target="tpu_custom_call" | custom-call | tf_op jit(solution)/shard_map/near/pallas_call | solution.py:379
  32.1 0.0 collective-permute-done.3.zp_hbm
  32.2 6.4 %far.1 = (bf16[64,2048]{1,0:T(8,128)(2,1)S(1)}, bf16[64,1024]{1,0:T(8,128)(2,1)S(1)}) custom-call(s32[3]{0:T(128)S(1)} %pad_add_fusion.where_ref, bf16[288,256]{1,0:T(8,128)(2,1)S(1)} %collective-permute-done.1.y_hbm, bf16[256,256]{1,0:T(8,128)(2,1)S(1)} %collective-permute-done.2.z_hbm, bf16[256,256]{1,0:T(8,128)(2,1)S(1)} %collective-permute-done.3.zp_hbm, ...), custom_call_target="tpu_custom_call" | custom-call | tf_op jit(solution)/shard_map/far/pallas_call | solution.py:397
  38.5 3.0 %collective-permute-start.5 = (bf16[64,2048]{1,0:T(8,128)(2,1)S(1)}, bf16[64,2048]{1,0:T(8,128)(2,1)S(1)}, u32[]{:S(2)}, u32[]{:S(2)}) collective-permute-start(bf16[64,2048]{1,0:T(8,128)(2,1)S(1)} %get-tuple-element.32), channel_id=1, source_target_pairs={{0,1},{1,0},{2,3},{3,2},{4,5},{5,4},{6,7},{7,6},{8,9},{9,8},{10,11... | collective-permute-start | bytes 786440 | tf_op jit(solution)/shard_map/ppermute | solution.py:38
  41.5 3.6 %own.1 = f32[64,2048]{1,0:T(8,128)S(1)} custom-call(s32[3]{0:T(128)S(1)} %pad_add_fusion.where_ref, bf16[64,1024]{1,0:T(8,128)(2,1)S(1)} %get-tuple-element.31.att, bf16[1024,4096]{1,0:T(8,128)(2,1)} %w_hbm.3), custom_call_target="tpu_custom_call" | custom-call | tf_op jit(solution)/shard_map/own/pallas_call | solution.py:420
  45.1 3.6 %collective-permute-done.5 = bf16[64,2048]{1,0:T(8,128)(2,1)S(1)} collective-permute-done((bf16[64,2048]{1,0:T(8,128)(2,1)S(1)}, bf16[64,2048]{1,0:T(8,128)(2,1)S(1)}, u32[]{:S(2)}, u32[]{:S(2)}) %collective-permute-start.5) | collective-permute-done | bytes 262176 | tf_op jit(solution)/shard_map/ppermute | solution.py:38
  48.7 0.8 %add_convert_fusion = bf16[64,2048]{1,0:T(8,128)(2,1)} fusion(f32[64,2048]{1,0:T(8,128)S(1)} %own.1, bf16[64,2048]{1,0:T(8,128)(2,1)S(1)} %collective-permute-done.5), kind=kLoop, calls=%fused_computation | loop fusion | flops 393216 | bytes 1048576 | tf_op jit(solution)/shard_map/convert_element_type | solution.py:454
  (1 shorter events, 0.0 us)
Async XLA Ops:
  0.8 1.4 %collective-permute-start = (bf16[160,256]{1,0:T(8,128)(2,1)S(1)}, bf16[160,256]{1,0:T(8,128)(2,1)S(1)}, u32[]{:S(2)}, u32[]{:S(2)}) collective-permute-start(bf16[160,256]{1,0:T(8,128)(2,1)S(1)} %pack.1.own_ref.x0_hbm), channel_id=1, source_target_pairs={{0,2},{2,0},{4,6},{6,4},{8,10},{10,8},{12,14},{14,12},{16,18},{18,... | collective-permute-start | bytes 245768 | tf_op jit(solution)/shard_map/ppermute | solution.py:29
  2.2 10.2 %collective-permute-start.1 = (bf16[288,256]{1,0:T(8,128)(2,1)S(1)}, bf16[288,256]{1,0:T(8,128)(2,1)S(1)}, u32[]{:S(2)}, u32[]{:S(2)}) collective-permute-start(bf16[288,256]{1,0:T(8,128)(2,1)S(1)} %get-tuple-element.19), channel_id=1, source_target_pairs={{0,4},{2,10},{4,8},{6,14},{8,12},{10,18},{12,16},{14,22},{16,20},{... | collective-permute-start | bytes 442376 | tf_op jit(solution)/shard_map/ppermute | solution.py:34
  6.0 17.6 %collective-permute-start.2 = (bf16[256,256]{1,0:T(8,128)(2,1)S(1)}, bf16[256,256]{1,0:T(8,128)(2,1)S(1)}, u32[]{:S(2)}, u32[]{:S(2)}) collective-permute-start(bf16[256,256]{1,0:T(8,128)(2,1)S(1)} %get-tuple-element.20), channel_id=1, source_target_pairs={{0,16},{2,14},{4,20},{6,18},{8,24},{10,22},{12,28},{14,26},{16,32}... | collective-permute-start | bytes 393224 | tf_op jit(solution)/shard_map/ppermute | solution.py:34
  12.5 13.7 %collective-permute-start.4 = (bf16[288,256]{1,0:T(8,128)(2,1)S(1)}, bf16[288,256]{1,0:T(8,128)(2,1)S(1)}, u32[]{:S(2)}, u32[]{:S(2)}) collective-permute-start(bf16[288,256]{1,0:T(8,128)(2,1)S(1)} %collective-permute-done.1.y_hbm), channel_id=1, source_target_pairs={{0,2},{2,0},{4,6},{6,4},{8,10},{10,8},{12,14},{14,12},{16,18},{18,... | collective-permute-start | bytes 442376 | tf_op jit(solution)/shard_map/ppermute | solution.py:29
  23.7 8.5 %collective-permute-start.3 = (bf16[256,256]{1,0:T(8,128)(2,1)S(1)}, bf16[256,256]{1,0:T(8,128)(2,1)S(1)}, u32[]{:S(2)}, u32[]{:S(2)}) collective-permute-start(bf16[256,256]{1,0:T(8,128)(2,1)S(1)} %collective-permute-done.2.z_hbm), channel_id=1, source_target_pairs={{0,2},{2,0},{4,6},{6,4},{8,10},{10,8},{12,14},{14,12},{16,18},{18,... | collective-permute-start | bytes 393224 | tf_op jit(solution)/shard_map/ppermute | solution.py:29
  38.5 10.2 %collective-permute-start.5 = (bf16[64,2048]{1,0:T(8,128)(2,1)S(1)}, bf16[64,2048]{1,0:T(8,128)(2,1)S(1)}, u32[]{:S(2)}, u32[]{:S(2)}) collective-permute-start(bf16[64,2048]{1,0:T(8,128)(2,1)S(1)} %get-tuple-element.32), channel_id=1, source_target_pairs={{0,1},{1,0},{2,3},{3,2},{4,5},{5,4},{6,7},{7,6},{8,9},{9,8},{10,11... | collective-permute-start | bytes 786440 | tf_op jit(solution)/shard_map/ppermute | solution.py:38
